TPU v7x, 32 devices: a whole 2x2x4 slice. The times are simulated.
32 devices in a mesh: seq: 16 (over z, x, core), fsdp: 2 (over y).
Axes of the slice: x: 2, y: 2, z: 4, core: 2. Of those that a mesh axis runs over, the one named last changes fastest.
Arguments:
- hidden_in: bfloat16 [16, 1024, 1024], P('fsdp', 'seq'), may hold values from -10 to 10
- out_grad: bfloat16 [16, 1024, 1024], P('fsdp', 'seq'), may hold values from -6 to 6
- qkv_weight: bfloat16 [1024, 3072], P(('seq', 'fsdp')), may hold values from -0.25 to 0.25
- attn_out_weight: bfloat16 [1024, 1024], P(('seq', 'fsdp')), may hold values from -1 to 1
- in_weight: bfloat16 [1024, 5248], P(('seq', 'fsdp')), may hold values from -0.1875 to 0.1875
- down_weight: bfloat16 [2624, 1024], P(None, ('seq', 'fsdp')), may hold values from -0.25 to 0.25
- attn_gain: bfloat16 [1024], P(('seq', 'fsdp')), may hold values from 0.25 to 1.75
- mlp_gain: bfloat16 [1024], P(('seq', 'fsdp')), may hold values from 0.25 to 1.75
- seq_lengths: int32 [16], replicated, may hold values from 256 to 1024, as said below
- slot_order: int32 [16], replicated, may hold values from 0 to 15, each once
Outputs:
- output: bfloat16 [16, 1024, 1024], P('fsdp', 'seq')
- input_grad: bfloat16 [16, 1024, 1024], P('fsdp', 'seq')
- qkv_grad: float32 [1024, 3072], P(('seq', 'fsdp'))
- attn_out_grad: float32 [1024, 1024], P(('seq', 'fsdp'))
- in_grad: float32 [1024, 5248], P(('seq', 'fsdp'))
- down_grad: float32 [2624, 1024], P(None, ('seq', 'fsdp'))
- attn_gain_grad: float32 [1024], P(('seq', 'fsdp'))
- mlp_gain_grad: float32 [1024], P(('seq', 'fsdp'))
- root_squares: float32 [5], replicated
Inputs may be any that keep to these rules, and one draw needn't show every extreme that they name: `seq_lengths`: one sequence has exactly 1024 valid positions.
All inputs are finite; a program needn't handle non-finite values.
Results may differ from a plain program's by a relative error of at most 0.025.
Values may be sent and summed in bfloat16 or wider, within the bound.
A program may use at most 320 MiB of HBM per device.

v0:
```python
import functools

import jax
import jax.numpy as jnp
from jax import lax
from jax.experimental import pallas as pl
from jax.experimental.pallas import tpu as pltpu
from jax.sharding import PartitionSpec as P

HEADS = 16
LINE = 4
LANES = 128
EPS = 1e-05
THETA = 160000.0
F32 = jnp.float32
BF16 = jnp.bfloat16
MESH = pl.DeviceIdType.MESH


def up_to(size, unit):
    return -(-size // unit) * unit


class Place:
    def __init__(self, seq_size, fsdp_size):
        self.seq_size, self.fsdp_size = seq_size, fsdp_size
        self.rest = seq_size // (2 * LINE)
        self.swap = self.rest == fsdp_size
        self.nf, self.ng = self.rest, fsdp_size
        self.blocks = LINE * self.nf * self.ng
        self.seq = lax.axis_index("seq")
        self.y = lax.axis_index("fsdp")
        self.core = self.seq % 2
        self.r = (self.seq // 2) % self.rest
        self.z = self.seq // (2 * self.rest)
        self.f, self.g = self.split(self.r, self.y, self.core)

    def split(self, r, y, core):
        if not self.swap:
            return r, y
        return (1 - core) * r + core * y, (1 - core) * y + core * r

    def device(self, z, f, g, core=None):
        core = self.core if core is None else core
        r, y = self.split(f, g, core)
        return (z * self.rest + r) * 2 + core, y

    def row_block(self, z, f, g, core=None):
        seq, y = self.device(z, f, g, core)
        return seq * self.fsdp_size + y

    def index(self, z, f, g):
        return (z * self.nf + f) * self.ng + g

    def partner(self):
        return self.seq + 1 - 2 * self.core, self.y


def both(first, second):
    if first is True:
        return second
    if second is True:
        return first
    return jnp.logical_and(first, second)


def when(condition, body):
    if condition is True:
        body()
    else:
        pl.when(condition)(body)


def meet(peers, awaited):
    barrier = pltpu.get_barrier_semaphore()
    for condition, device in peers:
        when(
            condition,
            functools.partial(
                pl.semaphore_signal, barrier, inc=1, device_id=device, device_id_type=MESH
            ),
        )
    pl.semaphore_wait(barrier, awaited)


def plane_peers(at):
    below, above = at.z > 0, at.z < LINE - 1
    peers = [
        (below, at.device(at.z - 1, at.f, at.g)),
        (above, at.device(at.z + 1, at.f, at.g)),
        (True, at.partner()),
    ]
    for step in range(1, at.nf):
        peers.append((True, at.device(at.z, (at.f + step) % at.nf, at.g)))
    for step in range(1, at.ng):
        peers.append((True, at.device(at.z, at.f, (at.g + step) % at.ng)))
    count = 1 + (at.nf - 1) + (at.ng - 1)
    count = count + jnp.where(below, 1, 0) + jnp.where(above, 1, 0)
    return peers, count


def slot_peers(at, slots):
    group = at.seq_size // slots
    own_slot, own_part = at.seq // group, at.seq % group
    same = at.seq // slots == own_part
    peers = []
    for step in range(slots):
        wide = ((own_slot + step) % slots) * group + at.seq // slots
        narrow = own_part * slots + (at.seq + step) % slots
        condition = True if step else jnp.logical_not(same)
        peers.append((condition, (wide, at.y)))
        peers.append((condition, (narrow, at.y)))
    return peers, 2 * slots - 2 * jnp.where(same, 1, 0)


def steps_of(at):
    out = []
    for dz in (0, -1, 1, -2, 2, -3, 3):
        for df in range(at.nf):
            for dg in range(at.ng):
                out.append((abs(dz) + (df > 0) + (dg > 0), dz, df, dg))
    out.sort(key=lambda item: item[0])
    return [item[1:] for item in out]


def present(at, dz):
    if dz == 0:
        return True
    return at.z + dz >= 0 if dz < 0 else at.z + dz < LINE


class Gather:
    def __init__(self, at, sections, sems, phase):
        self.at, self.sections, self.phase = at, sections, phase
        self.send_sems, self.plane_sems, self.pair_sems = sems

    @staticmethod
    def scratch(count, nf, ng):
        dma = pltpu.SemaphoreType.DMA
        blocks, kinds = LINE * nf * ng, 3 + (nf - 1) + (ng - 1)
        return [dma((count, blocks, kinds)), dma((count, blocks)), dma((count, blocks + 1))]

    def own(self, number):
        source, _, columns, _ = self.sections[number]
        return source.at[:, columns]

    def block(self, number, z, f, g):
        source, whole, columns, _ = self.sections[number]
        rows = source.shape[0]
        start = pl.multiple_of(self.at.row_block(z, f, g) * rows, rows)
        return whole.at[pl.ds(start, rows), columns]

    def forward(self, number, condition, source, dz, df, dg):
        at, order = self.at, self.sections[number][3]
        z, f, g = at.z + dz, (at.f + df) % at.nf, (at.g + dg) % at.ng
        place, target = at.index(z, f, g), self.block(number, z, f, g)
        moved = {"z": dz, "f": df, "g": dg}
        last = max([i for i, axis in enumerate(order) if moved[axis]], default=-1)

        def send(allowed, kind, device, pair=False):
            sem = (self.pair_sems if pair else self.plane_sems).at[number, place]
            start_copy(
                self.phase,
                both(condition, allowed),
                source,
                target,
                self.send_sems.at[number, place, kind],
                sem,
                device,
            )

        for i, axis in enumerate(order):
            if axis == "z" and i >= last:
                rising, sinking = dz <= 0, dz >= 0
                if rising:
                    send(at.z < LINE - 1, 0, at.device(at.z + 1, at.f, at.g))
                if sinking:
                    send(at.z > 0, 1, at.device(at.z - 1, at.f, at.g))
            if axis == "f" and i > last:
                for step in range(1, at.nf):
                    send(True, 1 + step, at.device(at.z, (at.f + step) % at.nf, at.g))
            if axis == "g" and i > last:
                for step in range(1, at.ng):
                    send(True, at.nf + step, at.device(at.z, at.f, (at.g + step) % at.ng))
        send(True, at.nf + at.ng, at.partner(), pair=True)

    def begin(self):
        at = self.at
        for number in range(len(self.sections)):
            self.forward(number, True, self.own(number), 0, 0, 0)
            own = pltpu.make_async_copy(
                self.own(number),
                self.block(number, at.z, at.f, at.g),
                self.pair_sems.at[number, at.blocks],
            )
            if self.phase.ending:
                own.wait()
            else:
                own.start()

    def arrival(self, number, dz, df, dg):
        at = self.at
        z, f, g = at.z + dz, (at.f + df) % at.nf, (at.g + dg) % at.ng
        condition = present(at, dz)
        block = self.block(number, z, f, g)
        sem = self.plane_sems.at[number, at.index(z, f, g)]
        if not self.phase.ending:
            when(condition, functools.partial(await_block, block, sem))
        self.forward(number, condition, block, dz, df, dg)

    def events(self):
        return [
            functools.partial(self.arrival, number, *item)
            for item in steps_of(self.at)[1:]
            for number in range(len(self.sections))
        ]

    def finish(self):
        for number in range(len(self.sections)):
            for place in range(self.at.blocks):
                await_block(self.block(number, 0, 0, 0), self.pair_sems.at[number, place])


def trade_in(at, source_ref, target_ref, send_sems, recv_sems, phase):
    slots, positions = source_ref.shape[0], source_ref.shape[1]
    group = at.seq_size // slots
    own_slot, own_part = at.seq // group, at.seq % group
    same = at.seq // slots == own_part
    lane = at.seq % slots
    target = target_ref.at[pl.ds(pl.multiple_of(lane * positions, positions), positions), :]
    for step in range(slots):
        slot = (own_slot + step) % slots
        if step == 0 and not phase.ending:
            local = pltpu.make_async_copy(source_ref.at[slot], target, recv_sems.at[lane])
            when(same, local.start)
        start_copy(
            phase,
            True if step else jnp.logical_not(same),
            source_ref.at[slot],
            target,
            send_sems.at[step],
            recv_sems.at[lane],
            (slot * group + at.seq // slots, at.y),
        )
        if phase.ending:
            await_block(target_ref.at[pl.ds(step * positions, positions), :], recv_sems.at[step])


def trade_out(at, source_ref, target_ref, send_sems, recv_sems, phase):
    slots, positions = target_ref.shape[0], target_ref.shape[1]
    group = at.seq_size // slots
    own_slot, own_part = at.seq // group, at.seq % group
    same = at.seq // slots == own_part
    target = target_ref.at[own_slot]
    for step in range(slots):
        lane = (at.seq + step) % slots
        source = source_ref.at[pl.ds(pl.multiple_of(lane * positions, positions), positions), :]
        if step == 0 and not phase.ending:
            local = pltpu.make_async_copy(source, target, recv_sems.at[own_slot])
            when(same, local.start)
        start_copy(
            phase,
            True if step else jnp.logical_not(same),
            source,
            target,
            send_sems.at[step],
            recv_sems.at[own_slot],
            (own_part * slots + lane, at.y),
        )
        if phase.ending:
            await_block(target_ref.at[step], recv_sems.at[step])


def first_kernel(sizes, *refs):
    at = Place(*sizes)
    weight_ref, gains_ref, hidden_ref, whole_ref, all_gains_ref, rows_ref = refs[:6]
    sems, (trade_send, trade_recv) = refs[6:9], refs[9:]
    peers, count = plane_peers(at)
    more, extra = slot_peers(at, hidden_ref.shape[0])
    meet(peers + more, count + extra)
    phase = Phase()
    sections = [
        (weight_ref, whole_ref, pl.ds(0, weight_ref.shape[1]), "zfg"),
        (gains_ref, all_gains_ref, pl.ds(0, gains_ref.shape[1]), "zfg"),
    ]
    gather = Gather(at, sections, sems, phase)
    events = gather.events()
    for phase.ending in (False, True):
        gather.begin()
        trade_in(at, hidden_ref, rows_ref, trade_send, trade_recv, phase)
        run_all(events)
    gather.finish()


def gather_first(weight, gains, hidden, seq_size, fsdp_size):
    slots, positions, model = hidden.shape
    nf, ng = seq_size // (2 * LINE), fsdp_size
    devices = seq_size * fsdp_size
    dma = pltpu.SemaphoreType.DMA
    return pl.pallas_call(
        functools.partial(first_kernel, (seq_size, fsdp_size)),
        out_shape=(
            jax.ShapeDtypeStruct((weight.shape[0] * devices, weight.shape[1]), BF16),
            jax.ShapeDtypeStruct((gains.shape[0] * devices, gains.shape[1]), BF16),
            jax.ShapeDtypeStruct((slots * positions, model), BF16),
        ),
        in_specs=[pl.BlockSpec(memory_space=pltpu.VMEM)] * 3,
        out_specs=[pl.BlockSpec(memory_space=pl.ANY)] * 3,
        scratch_shapes=Gather.scratch(2, nf, ng) + [dma((slots,)), dma((slots,))],
        compiler_params=pltpu.CompilerParams(collective_id=0, has_side_effects=True),
        name="gather_first",
    )(weight, gains, hidden)


def add_blocks(target, others, width):
    pieces = 5 if width % (5 * LANES) == 0 else 1
    piece = width // pieces

    def body(number, carry):
        columns = pl.ds(pl.multiple_of(number * piece, LANES), piece)
        total = target[:, columns].astype(F32)
        for other in others:
            total = total + other[:, columns].astype(F32)
        target[:, columns] = total.astype(target.dtype)
        return carry

    lax.fori_loop(0, pieces, body, 0)


def line_targets(at):
    order = []
    for dz in (-3, 3, -2, 2, -1, 1, 0):
        for df in list(range(1, at.nf)) + [0]:
            for dg in list(range(1, at.ng)) + [0]:
                order.append((dg == 0, df == 0, -abs(dz), dz, df, dg))
    order.sort(key=lambda item: item[:3])
    return [item[3:] for item in order]


class Phase:
    def __init__(self):
        self.ending = False


def start_copy(phase, condition, source, target, send_sem, recv_sem, device):
    copy = pltpu.make_async_remote_copy(
        src_ref=source,
        dst_ref=target,
        send_sem=send_sem,
        recv_sem=recv_sem,
        device_id=device,
        device_id_type=MESH,
    )
    when(condition, copy.wait_send if phase.ending else copy.start)


def run_all(events):
    for event in events:
        event()


def await_block(buffer, sem):
    pltpu.make_async_copy(buffer, buffer, sem).wait()


def scatter_scratch(nf, ng, rows, width):
    dma = pltpu.SemaphoreType.DMA
    blocks, beyond_g, beyond_f = LINE * nf * ng, (ng - 1) * LINE * nf, (nf - 1) * LINE
    counts = (blocks, blocks, beyond_g, beyond_f, LINE, LINE)
    buffers = [pltpu.VMEM((count, rows, width), BF16) for count in counts]
    sems = (blocks, blocks, blocks, beyond_g, beyond_g, beyond_f, beyond_f, LINE, LINE, LINE, LINE)
    return buffers + [dma((count,)) for count in sems]


SCATTER_SCRATCH = 17


def scatter_events(at, sources, owned, scratch, phase):
    acc, from_pair, from_g, from_f, from_below, from_above = scratch[:6]
    load_sems, pair_send, pair_recv, g_send, g_recv, f_send, f_recv = scratch[6:13]
    up_send, up_recv, down_send, down_recv = scratch[13:]
    rows, width = acc.shape[1], acc.shape[2]
    order = line_targets(at)
    other = 1 - at.core
    send = functools.partial(start_copy, phase)

    def where_is(dz, df, dg):
        return at.z + dz, (at.f + df) % at.nf, (at.g + dg) % at.ng

    def spans():
        start = 0
        for source in sources:
            yield source, pl.ds(start, source.shape[1])
            start += source.shape[1]

    def rows_of(source, z, f, g, core=None):
        start = pl.multiple_of(at.row_block(z, f, g, core) * rows, rows)
        return source.at[pl.ds(start, rows), :]

    def begin(dz, df, dg):
        z, f, g = where_is(dz, df, dg)
        condition = present(at, dz)
        place = at.index(z, f, g)
        pf, pg = at.split(*at.split(f, g, at.core), other)
        there = at.index(z, pf, pg)

        def body():
            if phase.ending:
                await_block(from_pair.at[there], pair_send.at[there])
                return
            for source, columns in spans():
                pltpu.make_async_copy(
                    rows_of(source, z, f, g), acc.at[place, :, columns], load_sems.at[place]
                ).start()
                pltpu.make_async_remote_copy(
                    src_ref=rows_of(source, z, pf, pg, other),
                    dst_ref=from_pair.at[there, :, columns],
                    send_sem=pair_send.at[there],
                    recv_sem=pair_recv.at[there],
                    device_id=at.partner(),
                    device_id_type=MESH,
                ).start()

        when(condition, body)

    def over_pair(dz, df, dg):
        z, f, g = where_is(dz, df, dg)
        condition = present(at, dz)
        place = at.index(z, f, g)

        def join():
            await_block(acc.at[place], load_sems.at[place])
            await_block(from_pair.at[place], pair_recv.at[place])
            add_blocks(acc.at[place], [from_pair.at[place]], width)

        if not phase.ending:
            when(condition, join)
        if dg:
            slot = (dg - 1) * LINE * at.nf + z * at.nf + f
            device = at.device(at.z, at.f, g)
            send(condition, acc.at[place], from_g.at[slot], g_send.at[slot], g_recv.at[slot], device)

    def over_g(dz, df):
        z, f, g = where_is(dz, df, 0)
        condition = present(at, dz)
        place = at.index(z, f, g)

        def join():
            parts = []
            for step in range(1, at.ng):
                slot = (step - 1) * LINE * at.nf + z * at.nf + f
                await_block(from_g.at[slot], g_recv.at[slot])
                parts.append(from_g.at[slot])
            add_blocks(acc.at[place], parts, width)

        if not phase.ending:
            when(condition, join)
        if df:
            slot = (df - 1) * LINE + z
            device = at.device(at.z, f, at.g)
            send(condition, acc.at[place], from_f.at[slot], f_send.at[slot], f_recv.at[slot], device)

    def over_f(dz):
        z = at.z + dz
        condition = present(at, dz)
        place = at.index(z, at.f, at.g)

        def join():
            parts = []
            for step in range(1, at.nf):
                slot = (step - 1) * LINE + z
                await_block(from_f.at[slot], f_recv.at[slot])
                parts.append(from_f.at[slot])
            add_blocks(acc.at[place], parts, width)

            def rise():
                await_block(from_below.at[z], up_recv.at[z])
                add_blocks(acc.at[place], [from_below.at[z]], width)

            def sink():
                await_block(from_above.at[z], down_recv.at[z])
                add_blocks(acc.at[place], [from_above.at[z]], width)

            if 0 <= dz < LINE - 1:
                pl.when(at.z > 0)(rise)
            if 1 - LINE < dz <= 0:
                pl.when(at.z < LINE - 1)(sink)

        if not phase.ending:
            when(condition, join)
        if dz > 0:
            device = at.device(at.z + 1, at.f, at.g)
            send(condition, acc.at[place], from_below.at[z], up_send.at[z], up_recv.at[z], device)
        elif dz < 0:
            device = at.device(at.z - 1, at.f, at.g)
            send(condition, acc.at[place], from_above.at[z], down_send.at[z], down_recv.at[z], device)

    def finish():
        place = at.index(at.z, at.f, at.g)
        start = 0
        for source, target in zip(sources, owned):
            size = source.shape[1]
            if target.shape[1] <= size:
                target[...] = acc[place, :, start : start + target.shape[1]].astype(F32)
            start += size

    part = functools.partial
    return (
        [part(begin, *item) for item in order],
        [part(over_pair, *item) for item in order],
        [part(over_g, *item[:2]) for item in order if item[2] == 0],
        [part(over_f, dz) for dz in (-3, 3, -2, 2, -1, 1, 0)],
        finish,
    )


def scatter_kernel(sizes, count, *refs):
    at = Place(*sizes)
    sources, refs = refs[:count], refs[count:]
    result_ref, input_ref, vector_ref = refs[:3]
    owned, refs = refs[3 : 3 + count], refs[3 + count :]
    out_ref, grad_ref, total_ref = refs[:3]
    scratch, refs = refs[3 : 3 + SCATTER_SCRATCH], refs[3 + SCATTER_SCRATCH :]
    sq_g, sq_f, sq_z, sq_c, trade_send, trade_recv, sq_send, sq_recv = refs
    slots, positions = out_ref.shape[0], out_ref.shape[1]
    group = at.seq_size // slots
    peers, number = plane_peers(at)
    more, extra = slot_peers(at, slots)
    meet(peers + more, number + extra)
    phase = Phase()
    send = functools.partial(start_copy, phase)
    begins, pairs, gs, fs, finish = scatter_events(at, sources, owned, scratch, phase)
    other = 1 - at.core

    def vectors_g():
        for step in range(1, at.ng):
            device = at.device(at.z, at.f, (at.g + step) % at.ng)
            send(True, sq_g.at[at.g], sq_g.at[at.g], sq_send.at[0, step], sq_recv.at[0, at.g], device)

    def vectors_f():
        for step in range(1, at.nf):
            device = at.device(at.z, (at.f + step) % at.nf, at.g)
            send(True, sq_f.at[at.f], sq_f.at[at.f], sq_send.at[1, step], sq_recv.at[1, at.f], device)

    def line_send(condition, held, kind):
        device = at.device(at.z - 1 if kind else at.z + 1, at.f, at.g)
        send(condition, sq_z.at[held], sq_z.at[held], sq_send.at[2 + kind, held], sq_recv.at[2, held], device)

    def vectors_line(distance):
        for kind, held in enumerate((at.z - distance, at.z + distance)):
            there = held < LINE if kind else held >= 0
            onward = at.z > 0 if kind else at.z < LINE - 1
            if distance and not phase.ending:
                when(
                    there,
                    functools.partial(await_block, sq_z.at[held], sq_recv.at[2, held]),
                )
            line_send(both(there, onward), held, kind)

    def vectors_pair():
        send(
            True,
            sq_c.at[at.core],
            sq_c.at[at.core],
            sq_send.at[4, 0],
            sq_recv.at[3, at.core],
            at.partner(),
        )

    run_all(begins)
    trade_out(at, result_ref, out_ref, trade_send.at[0], trade_recv.at[0], phase)
    trade_out(at, input_ref, grad_ref, trade_send.at[1], trade_recv.at[1], phase)
    sq_g[at.g] = vector_ref[...]
    vectors_g()
    run_all(pairs)
    for step in range(1, at.ng):
        peer = (at.g + step) % at.ng
        await_block(sq_g.at[peer], sq_recv.at[0, peer])
    total = sq_g[0]
    for number in range(1, at.ng):
        total = total + sq_g[number]
    sq_f[at.f] = total
    vectors_f()
    run_all(gs)
    for step in range(1, at.nf):
        peer = (at.f + step) % at.nf
        await_block(sq_f.at[peer], sq_recv.at[1, peer])
    total = sq_f[0]
    for number in range(1, at.nf):
        total = total + sq_f[number]
    sq_z[at.z] = total
    vectors_line(0)
    run_all(fs[:-1])
    for distance in range(1, LINE):
        vectors_line(distance)
    total = sq_z[0]
    for number in range(1, LINE):
        total = total + sq_z[number]
    sq_c[at.core] = total
    vectors_pair()
    fs[-1]()
    finish()
    await_block(sq_c.at[other], sq_recv.at[3, other])
    total_ref[...] = sq_c[0] + sq_c[1]

    phase.ending = True
    run_all(begins + pairs + gs + fs)
    trade_out(at, result_ref, out_ref, trade_send.at[0], trade_recv.at[0], phase)
    trade_out(at, input_ref, grad_ref, trade_send.at[1], trade_recv.at[1], phase)
    vectors_g()
    vectors_f()
    for distance in range(LINE):
        vectors_line(distance)
    vectors_pair()


def scatter_all(sources, result, input_grad, vectors, slots, seq_size, fsdp_size):
    rows = sources[0].shape[0] // (seq_size * fsdp_size)
    width = sum(source.shape[1] for source in sources)
    own_rows, model = result.shape
    positions = own_rows // slots
    nf, ng = seq_size // (2 * LINE), fsdp_size
    dma = pltpu.SemaphoreType.DMA
    widest = max(nf, ng, LINE)
    vmem = pl.BlockSpec(memory_space=pltpu.VMEM)
    count = len(sources)
    return pl.pallas_call(
        functools.partial(scatter_kernel, (seq_size, fsdp_size), count),
        out_shape=tuple(
            [jax.ShapeDtypeStruct((rows, source.shape[1]), F32) for source in sources]
            + [jax.ShapeDtypeStruct((slots, positions, model), BF16)] * 2
            + [jax.ShapeDtypeStruct(vectors.shape, F32)]
        ),
        in_specs=[pl.BlockSpec(memory_space=pl.ANY)] * count + [vmem] * 3,
        out_specs=[vmem] * (count + 3),
        scratch_shapes=scatter_scratch(nf, ng, rows, width)
        + [pltpu.VMEM((size, *vectors.shape), F32) for size in (ng, nf, LINE, 2)]
        + [dma((2, slots)), dma((2, slots)), dma((5, widest)), dma((4, widest))],
        compiler_params=pltpu.CompilerParams(
            collective_id=3, has_side_effects=True, vmem_limit_bytes=63_000_000
        ),
        name="scatter_all",
    )(*sources, result, input_grad, vectors)


def meet_group(at, group):
    base, part = (at.seq // group) * group, at.seq % group
    members = [base + (part + step) % group for step in range(1, group)]
    meet([(True, (member, at.y)) for member in members], group - 1)
    return part, members


def first_half(shape):
    lane = lax.broadcasted_iota(jnp.int32, shape, 1)
    return lane % 64 < 32


def turn(values, cosine, sine):
    half = first_half(values.shape)
    away = jnp.where(half, -pltpu.roll(values, 96, 1), pltpu.roll(values, 32, 1))
    return values * cosine + away * sine


def turn_back(grads, cosine, sine):
    half = first_half(grads.shape)
    moved = grads * sine
    away = jnp.where(half, pltpu.roll(moved, 96, 1), -pltpu.roll(moved, 32, 1))
    return grads * cosine + away


def sum_kernel(
    sizes, group, keys_ref, values_ref, cos_ref, sin_ref, out_ref, arrived, send_sems, recv_sems
):
    at = Place(*sizes)
    rows, width = out_ref.shape
    half = width // 2
    part, members = meet_group(at, group)
    waits = []
    for kind, parts_ref in enumerate((keys_ref, values_ref)):
        for step, member in enumerate(members):
            owner = (part + step + 1) % group
            copy = pltpu.make_async_remote_copy(
                src_ref=parts_ref.at[pl.ds(pl.multiple_of(owner * rows, rows), rows), :],
                dst_ref=arrived.at[kind, step],
                send_sem=send_sems.at[kind, step],
                recv_sem=recv_sems.at[kind, step],
                device_id=(member, at.y),
                device_id_type=MESH,
            )
            copy.start()
            waits.append(copy.wait_send)
    own = pl.ds(pl.multiple_of(part * rows, rows), rows)
    cosine, sine = cos_ref[...], sin_ref[...]
    for kind, parts_ref in enumerate((keys_ref, values_ref)):
        for step in range(group - 1):
            await_block(arrived.at[kind, step], recv_sems.at[kind, step])

        def body(number, carry, kind=kind, parts_ref=parts_ref):
            start = pl.multiple_of(number * LANES, LANES)
            total = parts_ref[own, pl.ds(start, LANES)].astype(F32)
            for step in range(group - 1):
                total = total + arrived[kind, step, :, pl.ds(start, LANES)].astype(F32)
            if kind == 0:
                total = turn_back(total, cosine, sine)
            target = pl.ds(pl.multiple_of(kind * half + number * LANES, LANES), LANES)
            out_ref[:, target] = total.astype(BF16)
            return carry

        lax.fori_loop(0, half // LANES, body, 0)
    for wait in waits:
        wait()


def sum_rows(keys, values, cosine, sine, group, seq_size, fsdp_size):
    rows, width = keys.shape[0] // group, keys.shape[1]
    dma = pltpu.SemaphoreType.DMA
    vmem = pl.BlockSpec(memory_space=pltpu.VMEM)
    return pl.pallas_call(
        functools.partial(sum_kernel, (seq_size, fsdp_size), group),
        out_shape=jax.ShapeDtypeStruct((rows, 2 * width), BF16),
        in_specs=[vmem] * 4,
        out_specs=vmem,
        scratch_shapes=[
            pltpu.VMEM((2, group - 1, rows, width), BF16),
            dma((2, group)),
            dma((2, group)),
        ],
        compiler_params=pltpu.CompilerParams(
            collective_id=2, has_side_effects=True, vmem_limit_bytes=63_000_000
        ),
        name="sum_rows",
    )(keys, values, cosine, sine)


def normalize(values):
    average = jnp.mean(values, axis=-1, keepdims=True)
    centered = values - average
    variance = jnp.mean(centered * centered, axis=-1, keepdims=True)
    inverse = lax.rsqrt(variance + EPS)
    return centered * inverse, inverse


def norm_back(grad_normed, normed, inverse, gain_values):
    scaled = grad_normed * gain_values
    first_mean = jnp.mean(scaled, axis=-1, keepdims=True)
    second_mean = jnp.mean(scaled * normed, axis=-1, keepdims=True)
    return inverse * (scaled - first_mean - normed * second_mean)


def head_lanes(shape, head):
    return lax.broadcasted_iota(jnp.int32, shape, 1) // 64 == head


def scores_of(keys, queries, bias):
    scores = lax.dot_general(keys, queries, (((1,), (1,)), ((), ())), preferred_element_type=F32)
    return scores + bias


def key_bias(length, shape):
    return jnp.where(lax.broadcasted_iota(jnp.int32, shape, 0) < length, 0.0, -jnp.inf)


def attend(length, queries, keys, values):
    queries = queries * 0.125
    bias = key_bias(length, (keys.shape[0], 1))
    zero = jnp.zeros((), BF16)
    total, logs = None, []
    for head in range(2):
        only = head_lanes(queries.shape, head)
        scores = scores_of(keys, jnp.where(only, queries, zero), bias)
        largest = jnp.max(scores, axis=0, keepdims=True)
        weights = jnp.exp(scores - largest)
        summed = jnp.sum(weights, axis=0, keepdims=True)
        logs.append(largest + jnp.log(summed))
        held = jnp.where(head_lanes(values.shape, head), values, zero)
        part = lax.dot_general(
            held, weights.astype(BF16), (((0,), (0,)), ((), ())), preferred_element_type=F32
        )
        part = part / summed
        total = part if total is None else total + part
    return total.T.astype(BF16), logs


FRONT_TILE = 512


def front_kernel(sizes, group, spans, *refs):
    at = Place(*sizes)
    count = len(spans)
    length_ref, x_ref, gains_ref, cos_ref, sin_ref, w_ref, dy_ref = refs[:7]
    sources, refs = refs[7 : 7 + count], refs[7 + count :]
    act_ref, gain_ref, q_ref, shared_out, o_ref, log_ref, dy_rows_ref = refs[:7]
    wholes, refs = refs[7 : 7 + count], refs[7 + count :]
    sems, (trade_send, trade_recv, share_send, share_recv, shared_ref, out_sem) = refs[:3], refs[3:]
    step = pl.program_id(0)
    rows, model = q_ref.shape
    slots = dy_ref.shape[0]
    tile = o_ref.shape[0]
    tiles = rows // tile
    projecting = 3 * model // FRONT_TILE
    steps = projecting + model // LANES * tiles
    kept = 2 * model // FRONT_TILE
    phase = Phase()
    sections = []
    for number, parts in enumerate(spans):
        start = 0
        for size, order in parts:
            sections.append((sources[number], wholes[number], pl.ds(start, size), order))
            start += size
    gather = Gather(at, sections, sems, phase)
    base, part = (at.seq // group) * group, at.seq % group
    members = [base + (part + other) % group for other in range(1, group)]
    own_rows = pl.ds(pl.multiple_of(part * rows, rows), rows)

    @pl.when(step == 0)
    def _():
        peers, number = plane_peers(at)
        more, extra = slot_peers(at, slots)
        others = [(True, (member, at.y)) for member in members]
        meet(peers + more + others, number + extra + group - 1)

    @pl.when(step == 0)
    def _():
        gather.begin()
        trade_in(at, dy_ref, dy_rows_ref, trade_send, trade_recv, phase)

    @pl.when(step == 0)
    def _():
        normed, _ = normalize(x_ref[...].astype(F32))
        turned = gains_ref[...].astype(F32).T
        gain_ref[...] = turned[:8]
        act_ref[...] = (normed * turned[:1]).astype(BF16)

    def share(number):
        place = shared_ref.at[own_rows, pl.ds(number * FRONT_TILE, FRONT_TILE)]
        for other, member in enumerate(members):
            start_copy(
                phase,
                True,
                place,
                place,
                share_send.at[number, other],
                share_recv.at[number, part],
                (member, at.y),
            )

    def receive():
        for number in range(kept):
            for other in range(1, group):
                source = (part + other) % group
                place = shared_ref.at[
                    pl.ds(pl.multiple_of(source * rows, rows), rows),
                    pl.ds(number * FRONT_TILE, FRONT_TILE),
                ]
                await_block(place, share_recv.at[number, source])
        pltpu.make_async_copy(shared_ref, shared_out, out_sem).start()

    for number in range(kept):
        pl.when(step == number + 1)(functools.partial(share, number))
    pl.when(step == projecting)(receive)

    @pl.when(step < projecting)
    def _():
        mixed = jnp.dot(act_ref[...], w_ref[...], preferred_element_type=F32)

        def turned():
            cosine, sine = cos_ref[...], sin_ref[...]
            pieces = [
                turn(mixed[:, start : start + LANES], cosine, sine).astype(BF16)
                for start in range(0, FRONT_TILE, LANES)
            ]
            return jnp.concatenate(pieces, axis=1)

        @pl.when(step < kept // 2)
        def _():
            columns = pl.ds(pl.multiple_of(step * FRONT_TILE, FRONT_TILE), FRONT_TILE)
            shared_ref[own_rows, columns] = turned()

        @pl.when(both(step >= kept // 2, step < kept))
        def _():
            columns = pl.ds(pl.multiple_of(step * FRONT_TILE, FRONT_TILE), FRONT_TILE)
            shared_ref[own_rows, columns] = mixed.astype(BF16)

        @pl.when(step >= kept)
        def _():
            columns = pl.ds(pl.multiple_of((step - kept) * FRONT_TILE, FRONT_TILE), FRONT_TILE)
            q_ref[:, columns] = turned()

    @pl.when(step >= projecting)
    def _():
        pair, piece = (step - projecting) // tiles, (step - projecting) % tiles
        start = pl.multiple_of(pair * LANES, LANES)
        out, logs = attend(
            length_ref[0],
            q_ref[pl.ds(pl.multiple_of(piece * tile, tile), tile), pl.ds(start, LANES)],
            shared_ref[:, pl.ds(start, LANES)],
            shared_ref[:, pl.ds(pl.multiple_of(model + start, LANES), LANES)],
        )
        o_ref[...] = out
        for head in range(2):
            log_ref[0, head : head + 1, :] = logs[head]

    events = gather.events()
    pace = FRONT_PACE
    for number in range(steps - 1):
        group_events = events[number * pace : (number + 1) * pace]
        if group_events:
            pl.when(step == number)(functools.partial(run_all, group_events))

    @pl.when(step == steps - 1)
    def _():
        run_all(events[(steps - 1) * pace :])
        phase.ending = True
        gather.begin()
        trade_in(at, dy_ref, dy_rows_ref, trade_send, trade_recv, phase)
        run_all(events)
        for number in range(kept):
            share(number)
        gather.finish()
        pltpu.make_async_copy(shared_ref, shared_out, out_sem).wait()
        phase.ending = False


FRONT_PACE = 2


def front(length, x_rows, gains, cosine, sine, weight, dy, sources, spans, group, tile, seq_size, fsdp_size):
    rows, model = x_rows.shape
    slots, positions, _ = dy.shape
    pairs, tiles = model // LANES, rows // tile
    projecting, kept = 3 * model // FRONT_TILE, 2 * model // FRONT_TILE
    nf, ng = seq_size // (2 * LINE), fsdp_size
    devices = seq_size * fsdp_size
    count = sum(len(parts) for parts in spans)
    dma = pltpu.SemaphoreType.DMA
    vmem, anywhere = pl.BlockSpec(memory_space=pltpu.VMEM), pl.BlockSpec(memory_space=pl.ANY)

    def pair_of(i):
        return jnp.maximum(i - projecting, 0) // tiles

    def tile_of(i):
        return jnp.maximum(i - projecting, 0) % tiles

    return pl.pallas_call(
        functools.partial(front_kernel, (seq_size, fsdp_size), group, spans),
        grid=(projecting + pairs * tiles,),
        out_shape=tuple(
            [
                jax.ShapeDtypeStruct((rows, model), BF16),
                jax.ShapeDtypeStruct((8, model), F32),
                jax.ShapeDtypeStruct((rows, model), BF16),
                jax.ShapeDtypeStruct((rows * group, 2 * model), BF16),
                jax.ShapeDtypeStruct((rows, model), BF16),
                jax.ShapeDtypeStruct((pairs, 8, rows), F32),
                jax.ShapeDtypeStruct((slots * positions, model), BF16),
            ]
            + [
                jax.ShapeDtypeStruct((source.shape[0] * devices, source.shape[1]), BF16)
                for source in sources
            ]
        ),
        in_specs=[pl.BlockSpec(memory_space=pltpu.SMEM), vmem, vmem, vmem, vmem]
        + [
            pl.BlockSpec(
                (model, FRONT_TILE),
                lambda i: (0, (jnp.minimum(i, projecting - 1) + projecting - kept) % projecting),
            )
        ]
        + [vmem] * (1 + len(sources)),
        out_specs=[
            vmem,
            vmem,
            vmem,
            anywhere,
            pl.BlockSpec((tile, LANES), lambda i: (tile_of(i), pair_of(i))),
            pl.BlockSpec((1, 8, tile), lambda i: (pair_of(i), 0, tile_of(i))),
        ]
        + [anywhere] * (1 + len(sources)),
        scratch_shapes=Gather.scratch(count, nf, ng)
        + [dma((slots,)), dma((slots,)), dma((kept, group)), dma((kept, group))]
        + [pltpu.VMEM((rows * group, 2 * model), BF16), dma],
        compiler_params=pltpu.CompilerParams(
            collective_id=1, has_side_effects=True, vmem_limit_bytes=63_000_000
        ),
        name="front",
    )(length, x_rows, gains, cosine, sine, weight, dy, *sources)


def attend_back_kernel(
    length_ref,
    q_ref,
    k_ref,
    v_ref,
    g_ref,
    o_ref,
    log_ref,
    cos_ref,
    sin_ref,
    dq_ref,
    dk_ref,
    dv_ref,
    dk_acc,
    dv_acc,
):
    step = pl.program_id(1)
    keys, values, queries = k_ref[...], v_ref[...], q_ref[...] * 0.125
    grads = g_ref[...]
    bias = key_bias(length_ref[0], (keys.shape[0], 1))
    zero = jnp.zeros((), BF16)
    product = (grads.astype(F32) * o_ref[...].astype(F32)).T
    dq = dk = dv = None
    for head in range(2):
        only = head_lanes(queries.shape, head)
        query = jnp.where(only, queries, zero)
        grad = jnp.where(only, grads, zero)
        key = jnp.where(head_lanes(keys.shape, head), keys, zero)
        delta = jnp.sum(product[64 * head : 64 * head + 64], axis=0, keepdims=True)
        scores = scores_of(keys, query, bias)
        probs = jnp.exp(scores - log_ref[0, head : head + 1, :])
        grad_probs = lax.dot_general(
            values, grad, (((1,), (1,)), ((), ())), preferred_element_type=F32
        )
        grad_scores = (probs * (grad_probs - delta)).astype(BF16)
        value_part = jnp.dot(probs.astype(BF16), grad, preferred_element_type=F32)
        key_part = jnp.dot(grad_scores, query, preferred_element_type=F32)
        query_part = lax.dot_general(
            key, grad_scores, (((0,), (0,)), ((), ())), preferred_element_type=F32
        )
        dq = query_part if dq is None else dq + query_part
        dk = key_part if dk is None else dk + key_part
        dv = value_part if dv is None else dv + value_part
    dq_ref[...] = turn_back(dq.T * 0.125, cos_ref[...], sin_ref[...]).astype(BF16)

    @pl.when(step == 0)
    def _():
        dk_acc[...] = dk
        dv_acc[...] = dv

    @pl.when(step > 0)
    def _():
        dk_acc[...] += dk
        dv_acc[...] += dv

    @pl.when(step == pl.num_programs(1) - 1)
    def _():
        dk_ref[...] = dk_acc[...].astype(BF16)
        dv_ref[...] = dv_acc[...].astype(BF16)


def attend_back(lengths, queries, shared, grads, heads_out, logs, cosine, sine, model, tile):
    rows, keys = queries.shape[0], shared.shape[0]
    pairs = model // LANES
    by_row = pl.BlockSpec((tile, LANES), lambda p, i: (i, p))
    by_key = pl.BlockSpec((keys, LANES), lambda p, i: (0, p))
    table = pl.BlockSpec((tile, LANES), lambda p, i: (i, 0))
    return pl.pallas_call(
        attend_back_kernel,
        grid=(pairs, rows // tile),
        out_shape=(
            jax.ShapeDtypeStruct((rows, model), BF16),
            jax.ShapeDtypeStruct((keys, model), BF16),
            jax.ShapeDtypeStruct((keys, model), BF16),
        ),
        in_specs=[
            pl.BlockSpec(memory_space=pltpu.SMEM),
            by_row,
            by_key,
            pl.BlockSpec((keys, LANES), lambda p, i: (0, pairs + p)),
            by_row,
            by_row,
            pl.BlockSpec((1, 8, tile), lambda p, i: (p, 0, i)),
            table,
            table,
        ],
        out_specs=(by_row, by_key, by_key),
        scratch_shapes=[pltpu.VMEM((keys, LANES), F32), pltpu.VMEM((keys, LANES), F32)],
        name="attend_back",
    )(lengths, queries, shared, shared, grads, heads_out, logs, cosine, sine)


def rotary_tables(places, head_size):
    halfway = head_size // 2
    ladder = jnp.arange(halfway, dtype=F32) * (2.0 / head_size)
    inverse = 1.0 / THETA**ladder
    angles = places.astype(F32)[:, None] * inverse[None, :]
    angles = jnp.concatenate([angles] * 4, axis=-1)
    return jnp.cos(angles), jnp.sin(angles)


def gelu_exact(values):
    return jax.nn.gelu(values, approximate=False)


def mm(left, right):
    return jnp.dot(left, right, preferred_element_type=F32)


def mm_right_t(left, right):
    return lax.dot_general(left, right, (((1,), (1,)), ((), ())), preferred_element_type=F32)


def mm_left_t(left, right):
    return lax.dot_general(left, right, (((0,), (0,)), ((), ())), preferred_element_type=F32)


def shards(
    hidden_in,
    out_grad,
    qkv_weight,
    attn_out_weight,
    in_weight,
    down_weight,
    attn_gain,
    mlp_gain,
    seq_lengths,
    slot_order,
):
    seq_size, fsdp_size = lax.axis_size("seq"), lax.axis_size("fsdp")
    seq_place, fsdp_place = lax.axis_index("seq"), lax.axis_index("fsdp")
    slots, positions, model = hidden_in.shape
    shard = qkv_weight.shape[0]
    ff = down_weight.shape[0]
    wide = up_to(ff, LANES)
    spare = wide - ff
    group = seq_size // slots
    rows = slots * positions
    head_size = model // HEADS

    lead = jnp.zeros((shard, spare), BF16)
    gains = jnp.concatenate(
        [attn_gain[:, None], mlp_gain[:, None], jnp.zeros((shard, LANES - 2), BF16)], axis=1
    )
    in_pack = jnp.concatenate([in_weight[:, :ff], lead, in_weight[:, ff:], lead], axis=1)
    down_pack = jnp.concatenate([down_weight.T, lead], axis=1)
    w_qkv, all_gains, x_rows = gather_first(qkv_weight, gains, hidden_in, seq_size, fsdp_size)

    slot = fsdp_place * slots + seq_place // group
    order = jnp.sum(jnp.where(jnp.arange(slot_order.shape[0]) == slot, slot_order, 0))
    length = jnp.sum(jnp.where(jnp.arange(seq_lengths.shape[0]) == order, seq_lengths, 0))
    lengths = length.astype(jnp.int32)[None]
    places = (seq_place % group) * rows + jnp.arange(rows, dtype=jnp.int32)
    valid = (places < length).astype(F32)[:, None]
    cosine, sine = rotary_tables(places, head_size)

    tile = 512 if rows % 512 == 0 and rows * group <= 1024 else 128
    act_one, gain_rows, queries, shared, heads_out, logs, dy_rows, w_attn, w_input, w_down = front(
        lengths,
        x_rows,
        all_gains,
        cosine,
        sine,
        w_qkv,
        out_grad,
        (attn_out_weight, in_pack, down_pack),
        (((model, "fzg"),), ((wide, "zfg"), (wide, "zfg")), ((wide, "fzg"),)),
        group,
        tile,
        seq_size,
        fsdp_size,
    )
    gain_attn, gain_mlp = gain_rows[0:1], gain_rows[1:2]

    x_wide = x_rows.astype(F32)
    attn = mm(heads_out, w_attn)
    middle = x_wide + attn
    normed_two, inverse_two = normalize(middle)
    act_two = (normed_two * gain_mlp).astype(BF16)
    joined = mm(act_two, w_input)
    input_half = joined[:, :wide]
    gate_half = joined[:, wide:]
    active, active_pull = jax.vjp(gelu_exact, input_half)
    product = (active * gate_half).astype(BF16)
    branch = mm_right_t(product, w_down)
    result = (middle + branch) * valid
    squares = [
        jnp.sum(valid * tensor * tensor, axis=0) for tensor in (x_wide, middle, result, attn, branch)
    ]

    grad_y = dy_rows.astype(F32) * valid
    grad_branch = grad_y.astype(BF16)
    down_part = mm_left_t(grad_branch, product).astype(BF16)
    grad_product = mm(grad_branch, w_down)
    grad_joined = jnp.concatenate(
        [active_pull(grad_product * gate_half)[0], grad_product * active], axis=1
    ).astype(BF16)
    input_part = mm_left_t(act_two, grad_joined).astype(BF16)
    grad_act_two = mm_right_t(grad_joined, w_input)
    mlp_gain_part = jnp.sum(grad_act_two * normed_two, axis=0)
    grad_middle = grad_y + norm_back(grad_act_two, normed_two, inverse_two, gain_mlp)
    grad_attn = grad_middle.astype(BF16)
    attn_part = mm_left_t(heads_out, grad_attn).astype(BF16)
    grad_heads = mm_right_t(grad_attn, w_attn).astype(BF16)

    grad_q, grad_k, grad_v = attend_back(
        lengths, queries, shared, grad_heads, heads_out, logs, cosine, sine, model, tile
    )
    grad_kv = sum_rows(grad_k, grad_v, cosine, sine, group, seq_size, fsdp_size)
    grad_mixed = jnp.concatenate([grad_q, grad_kv], axis=1)
    qkv_part = mm_left_t(act_one, grad_mixed).astype(BF16)
    grad_act_one = mm_right_t(grad_mixed, w_qkv)
    normed_one, inverse_one = normalize(x_wide)
    attn_gain_part = jnp.sum(grad_act_one * normed_one, axis=0)
    grad_x = grad_middle + norm_back(grad_act_one, normed_one, inverse_one, gain_attn)

    vectors = jnp.stack(squares + [attn_gain_part, mlp_gain_part, jnp.zeros((model,), F32)])
    own_qkv, own_attn, own_in, own_down, out_rows, grad_rows, totals = scatter_all(
        [qkv_part, attn_part, input_part, down_part],
        result.astype(BF16),
        grad_x.astype(BF16),
        vectors,
        slots,
        seq_size,
        fsdp_size,
    )
    tokens_valid = jnp.sum(seq_lengths).astype(F32)
    root_squares = jnp.sqrt(jnp.sum(totals[:5], axis=1) / (tokens_valid * model))
    own_gains = lax.dynamic_slice_in_dim(totals, (seq_place * fsdp_size + fsdp_place) * shard, shard, 1)
    return (
        out_rows,
        grad_rows,
        own_qkv,
        own_attn,
        jnp.concatenate([own_in[:, :ff], own_in[:, wide : wide + ff]], axis=1),
        own_down[:, :ff].T,
        own_gains[5],
        own_gains[6],
        root_squares,
    )


def solution(mesh):
    placed = (
        P("fsdp", "seq", None),
        P("fsdp", "seq", None),
        P(("seq", "fsdp"), None),
        P(("seq", "fsdp"), None),
        P(("seq", "fsdp"), None),
        P(None, ("seq", "fsdp")),
        P(("seq", "fsdp")),
        P(("seq", "fsdp")),
        P(),
        P(),
    )
    return jax.shard_map(
        shards,
        mesh=mesh,
        in_specs=placed,
        out_specs=(
            P("fsdp", "seq", None),
            P("fsdp", "seq", None),
            P(("seq", "fsdp"), None),
            P(("seq", "fsdp"), None),
            P(("seq", "fsdp"), None),
            P(None, ("seq", "fsdp")),
            P(("seq", "fsdp")),
            P(("seq", "fsdp")),
            P(),
        ),
        check_vma=False,
    )
```

profile of v0, /device:TPU:27, one launch (start us, length us, event | category | flops | bytes accessed | tf_op | source)
XLA Modules:
  0.0 490.3 jit_solution(7090413858876415032)
XLA Ops:
  0.7 0.1 broadcast_multiply_fusion
  0.8 1.9 fusion.33
  2.7 1.3 fusion.38
  4.0 2.0 fusion.45
  6.0 0.7 copy.19
  6.7 0.8 copy.20
  7.5 0.1 pad.13.clone
  7.5 0.7 maximum_maximum_fusion.refs_1_
  8.2 57.5 %gather_first.1 = (bf16[1024,3072]{1,0:T(8,128)(2,1)}, bf16[1024,128]{1,0:T(8,128)(2,1)}, bf16[512,1024]{1,0:T(8,128)(2,1)}) custom-call(bf16[32,3072]{1,0:T(8,128)(2,1)} %refs_0_.1, bf16[32,128]{1,0:T(8,128)(2,1)} %maximum_maximum_fusion.refs_1_, bf16[8,64,1024]{2,1,0:T(8,128)(2,1)} %refs_2_.1), custom_call_target="tpu_custom_call" | custom-call | tf_op jit(solution)/shard_map/gather_first/pallas_call | solution.py:300
  65.7 1.1 fusion.49
  66.8 0.0 copy-start
  66.9 0.8 concatenate.24.refs_8_
  67.7 1.6 concatenate.25.refs_9_
  69.3 98.2 %front.1 = (bf16[512,1024]{1,0:T(8,128)(2,1)}, f32[8,1024]{1,0:T(8,128)}, bf16[512,1024]{1,0:T(8,128)(2,1)}, bf16[1024,2048]{1,0:T(8,128)(2,1)}, bf16[512,1024]{...) custom-call(s32[1]{0:T(128)} %bitcast.refs_0_.length_ref, ...), custom_call_target="tpu_custom_call" | custom-call | tf_op jit(solution)/shard_map/front/pallas_call | solution.py:944
  167.5 0.2 convert_reduce_fusion
  167.7 4.7 fusion.47
  172.4 0.3 multiply_reduce_fusion.2
  172.7 0.8 fusion.50
  173.6 8.6 %fusion.44 = f32[512,5376]{1,0:T(8,128)S(1)} fusion(bf16[1024,5376]{1,0:T(8,128)(2,1)} %get-tuple-element.42, f32[512,1024]{1,0:T(8,128)S(1)} %get-tuple-element.74, f32[1024]{0:T(1024)S(1)} %bitcast.32, f32[512]{0:T(512)S(1)} %add_rsqrt_fusion.1, f32[512]{0:T(512)S(1)} %get-tuple-element.92), kind=kOutput, calls=%fused_computation.103 | convolution fusion | flops 5639241728 | bytes 24125440 | tf_op jit(solution)/shard_map/dot_general | solution.py:1095
  182.2 13.0 %multiply_convert_fusion = (bf16[512,2688]{1,0:T(8,128)(2,1)}, f32[512,2688]{1,0:T(8,128)S(1)}) fusion(f32[512,5376]{1,0:T(8,128)S(1)} %fusion.44), kind=kLoop, calls=%fused_computation.6 | loop fusion | flops 90832896 | bytes 19267584 | tf_op jit(solution)/shard_map/convert_element_type | solution.py:1172
  195.2 0.6 fusion.37
  195.9 9.5 %add_convert_fusion = (bf16[512,2688]{1,0:T(8,128)(2,1)}, bf16[512,2688]{1,0:T(8,128)(2,1)}) fusion(f32[512,2688]{1,0:T(8,128)S(1)} %get-tuple-element.72, f32[512,5376]{1,0:T(8,128)S(1)} %fusion.44, bf16[1024,2688]{1,0:T(8,128)(2,1)} %get-tuple-element.43, bf16[512,1024]{1,0:T(8,128)(2,1)S(1)} %copy-done.8, f32[512]{0:T(512)S(1)} %fusion.37), kind=kOutput, calls=%fused_computation.8 | convolution fusion | flops 2844917760 | bytes 28575744 | tf_op jit(solution)/shard_map/dot_general | solution.py:1095
  205.3 10.4 %fusion.7 = f32[512,1024]{1,0:T(8,128)S(1)} fusion(bf16[1024,5376]{1,0:T(8,128)(2,1)} %get-tuple-element.42, bf16[512,2688]{1,0:T(8,128)(2,1)} %get-tuple-element.76, bf16[512,2688]{1,0:T(8,128)(2,1)} %get-tuple-element.75), kind=kOutput, calls=%fused_computation.29 | convolution fusion | flops 5648154624 | bytes 18612224 | tf_op jit(solution)/shard_map/dot_general | solution.py:1099
  215.8 7.6 %fusion.23 = (f32[1024]{0:T(1024)S(1)}, f32[1024]{0:T(1024)S(1)}, f32[1024]{0:T(1024)S(1)}, f32[512]{0:T(512)S(1)}, f32[512]{0:T(512)S(1)}, /*index=5*/f32[1024]{0:T(1024)S(1)}, bf16[512,1024]{1,0:T(8,128)(2,1)}) fusion(f32[512]{0:T(512)S(1)} %fusion.37, f32[512,1024]{1,0:T(8,128)S(1)} %get-tuple-element.74, f32[512,1024]{1,0:T(8,128)S(1)} %fusion.7, ...), kind=kOutput, calls=%fused_computation.50 | convolution fusion | flops 2829052928 | bytes 13531136 | tf_op jit(solution)/shard_map/dot_general | solution.py:1099
  223.4 0.8 multiply_add_fusion
  224.3 1.3 copy-done.1
  225.6 2.3 convolution_convert_fusion.4.g_ref
  227.8 26.6 %attend_back.1 = (bf16[512,1024]{1,0:T(8,128)(2,1)}, bf16[1024,1024]{1,0:T(8,128)(2,1)}, bf16[1024,1024]{1,0:T(8,128)(2,1)}) custom-call(s32[1]{0:T(128)} %bitcast.refs_0_.length_ref, bf16[512,1024]{1,0:T(8,128)(2,1)} %get-tuple-element.36.q_ref, bf16[1024,2048]{1,0:T(8,128)(2,1)} %get-tuple-element.37.k_ref.v_ref, ...), custom_call_target="tpu_custom_call" | custom-call | tf_op jit(solution)/shard_map/attend_back/pallas_call | solution.py:1056
  254.4 8.9 %sum_rows.1 = bf16[512,2048]{1,0:T(8,128)(2,1)} custom-call(bf16[1024,1024]{1,0:T(8,128)(2,1)} %get-tuple-element.46.keys_ref, bf16[1024,1024]{1,0:T(8,128)(2,1)} %get-tuple-element.47.values_ref, f32[512,128]{1,0:T(8,128)} %get-tuple-element.84.refs_3_.cos_ref, f32[512,128]{1,0:T(8,128)} %get-tuple-element.83.refs_4_.sin_ref), custom_call_target="tpu_custom_call" | custom-call | tf_op jit(solution)/shard_map/sum_rows/pallas_call | solution.py:718
  263.3 9.7 %fusion.18 = (f32[1024]{0:T(1024)S(1)}, f32[512]{0:T(512)S(1)}, f32[512]{0:T(512)S(1)}, f32[1024]{0:T(1024)S(1)}, f32[1024]{0:T(1024)S(1)}, /*index=5*/f32[512,1024]{1,0:T(8,128)}) fusion(bf16[512,1024]{1,0:T(8,128)(2,1)S(1)} %copy-done, f32[512]{0:T(512)S(1)} %get-tuple-element.91, f32[512]{0:T(512)S(1)} %broadcast_multiply_fusion.3, ...), kind=kOutput, calls=%fused_computation.45 | convolution fusion | flops 3235377152 | bytes 14706688 | tf_op jit(solution)/shard_map/dot_general | solution.py:1099
  273.0 0.7 stack.31.refs_6_
  273.7 4.1 fusion.17.refs_5_
  277.7 5.2 %convolution_convert_fusion.1.refs_3_ = bf16[1024,2688]{1,0:T(8,128)(2,1)} fusion(bf16[512,2688]{1,0:T(8,128)(2,1)S(1)} %copy-done.4, bf16[512,1024]{1,0:T(8,128)(2,1)S(1)} %copy-done.9, f32[512]{0:T(512)S(1)} %fusion.37), kind=kOutput, calls=%fused_computation.2 | convolution fusion | flops 2822897664 | bytes 9308160 | tf_op jit(solution)/shard_map/dot_general | solution.py:1103
  282.9 11.8 %convolution_convert_fusion.refs_2_ = bf16[1024,5376]{1,0:T(8,128)(2,1)} fusion(bf16[512,2688]{1,0:T(8,128)(2,1)} %get-tuple-element.76, bf16[512,2688]{1,0:T(8,128)(2,1)} %get-tuple-element.75, f32[512,1024]{1,0:T(8,128)S(1)} %get-tuple-element.74, f32[1024]{0:T(1024)S(1)} %bitcast.35, f32[512]{0:T(512)S(1)} %add_rsqrt_fusion.1, f32[512]{0:T(512)S(1)} %get-tuple-element.92), kind=kOutput, calls=%fused_computation | convolution fusion | flops 5655756800 | bytes 18620416 | tf_op jit(solution)/shard_map/dot_general | solution.py:1103
  294.7 2.7 convolution_convert_fusion.3.refs_1_
  297.4 5.5 %convolution_convert_fusion.2.refs_0_ = bf16[1024,3072]{1,0:T(8,128)(2,1)} fusion(bf16[512,1024]{1,0:T(8,128)(2,1)S(1)} %copy-done.13, bf16[512,2048]{1,0:T(8,128)(2,1)S(1)} %copy-done.5, bf16[512,1024]{1,0:T(8,128)(2,1)S(1)} %copy-done.14), kind=kOutput, calls=%fused_computation.3 | convolution fusion | flops 3230662656 | bytes 10485760 | tf_op jit(solution)/shard_map/dot_general | solution.py:1103
  303.0 175.2 %scatter_all.1 = (f32[32,3072]{1,0:T(8,128)}, f32[32,1024]{1,0:T(8,128)}, f32[32,5376]{1,0:T(8,128)}, f32[32,2688]{1,0:T(8,128)}, bf16[8,64,1024]{2,1,0:T(8,128)...) custom-call(bf16[1024,3072]{1,0:T(8,128)(2,1)} %convolution_convert_fusion.2.refs_0_, ...), custom_call_target="tpu_custom_call" | custom-call | tf_op jit(solution)/shard_map/scatter_all/pallas_call | solution.py:627
  478.2 1.2 fusion.48
  479.5 1.0 pad_maximum_fusion.6
  480.5 1.7 slice_bitcast_fusion
  482.2 0.7 constant_dynamic-slice_fusion
  483.0 0.5 slice_bitcast_fusion.1
  483.5 0.9 slice_reduce_fusion
  485.0 0.5 divide_sqrt_fusion
  485.5 2.3 copy.25
  487.8 1.0 copy.26
  488.7 0.7 copy.27
  489.5 0.7 copy.28
  (40 shorter events, 0.1 us)
Async XLA Ops:
  66.8 100.7 %copy-start = (bf16[512,1024]{1,0:T(8,128)(2,1)S(1)}, bf16[512,1024]{1,0:T(8,128)(2,1)}, u32[]{:S(2)}) copy-start(bf16[512,1024]{1,0:T(8,128)(2,1)} %get-tuple-element.32.refs_1_) | copy-start | bytes 3145732
  182.2 13.6 %copy-start.8 = (bf16[512,1024]{1,0:T(8,128)(2,1)S(1)}, bf16[512,1024]{1,0:T(8,128)(2,1)}, u32[]{:S(2)}) copy-start(bf16[512,1024]{1,0:T(8,128)(2,1)} %get-tuple-element.38) | copy-start | bytes 3145732
  205.3 10.4 %copy-start.3 = (bf16[512,2688]{1,0:T(8,128)(2,1)S(1)}, bf16[512,2688]{1,0:T(8,128)(2,1)}, u32[]{:S(2)}) copy-start(bf16[512,2688]{1,0:T(8,128)(2,1)} %get-tuple-element.71) | copy-start | bytes 8257540
  223.4 2.2 copy-start.12
  224.3 1.3 copy-start.1
  273.7 4.1 copy-start.4
  273.7 4.1 copy-start.9
  282.9 11.8 %copy-start.2 = (f32[512,1024]{1,0:T(8,128)S(1)}, f32[512,1024]{1,0:T(8,128)}, u32[]{:S(2)}) copy-start(f32[512,1024]{1,0:T(8,128)} %copy-done.1) | copy-start | bytes 6291460
  282.9 11.8 %copy-start.6 = (bf16[512,1024]{1,0:T(8,128)(2,1)S(1)}, bf16[512,1024]{1,0:T(8,128)(2,1)}, u32[]{:S(2)}) copy-start(bf16[512,1024]{1,0:T(8,128)(2,1)} %get-tuple-element.39.o_ref) | copy-start | bytes 3145732
  294.7 2.7 copy-start.5
  294.7 2.7 copy-start.13
  294.7 2.7 copy-start.14
  478.2 9.6 %copy-start.7 = (bf16[8,64,1024]{2,1,0:T(8,128)(2,1)S(1)}, bf16[8,64,1024]{2,1,0:T(8,128)(2,1)}, u32[]{:S(2)}) copy-start(bf16[8,64,1024]{2,1,0:T(8,128)(2,1)} %get-tuple-element.103) | copy-start | bytes 3145732
  478.2 10.5 %copy-start.10 = (f32[32,3072]{1,0:T(8,128)S(1)}, f32[32,3072]{1,0:T(8,128)}, u32[]{:S(2)}) copy-start(f32[32,3072]{1,0:T(8,128)} %get-tuple-element.104) | copy-start | bytes 1179652
  478.2 11.3 %copy-start.11 = (f32[32,1024]{1,0:T(8,128)S(1)}, f32[32,1024]{1,0:T(8,128)}, u32[]{:S(2)}) copy-start(f32[32,1024]{1,0:T(8,128)} %get-tuple-element.105) | copy-start | bytes 393220
where the time goes:
time: 494 us; the launch traced here: 490 us
  Pallas kernels  366 us (74%)
  matrix products  77.9 us (16%)
  other arithmetic  27.5 us (6%)
  local copies, waits for them, and re-layouts  16.9 us (3%)
    pallas_call x1, Pallas kernels, scatter_all(): pl.pallas_call(functools.partial(scatter_kernel, (seq_size, fsdp_size), c...  175 us
    pallas_call x1, Pallas kernels, front(): pl.pallas_call(functools.partial(front_kernel, (seq_size, fsdp_size), gro...  98.2 us
    pallas_call x1, Pallas kernels, gather_first(): pl.pallas_call(functools.partial(first_kernel, (seq_size, fsdp_size)), ou...  57.5 us
    dot_general x4, matrix products, mm_right_t(): lax.dot_general(left, right, (((1,), (1,)), ((), ())), preferred_element_...  30 us
    pallas_call x1, Pallas kernels, attend_back(): pl.pallas_call(attend_back_kernel, grid=(pairs, rows // tile), out_shape=...  26.6 us
    dot_general x4, matrix products, mm_left_t(): lax.dot_general(left, right, (((0,), (0,)), ((), ())), preferred_element_...  25.2 us
    dot_general x3, matrix products, mm(): return jnp.dot(left, right, preferred_element_type=F32)  22.8 us
    convert_element_type x1, other arithmetic, shards(): product = (active * gate_half).astype(BF16)  13 us

commit v1 on v0

--- a/solution.py
+++ b/solution.py
@@ -312,9 +312,9 @@
     )(weight, gains, hidden)
 
 
-def add_blocks(target, others, width):
-    pieces = 5 if width % (5 * LANES) == 0 else 1
-    piece = width // pieces
+def add_blocks(target, others):
+    width = target.shape[1]
+    piece = next(size for size in (512, 384, 256, LANES) if width % size == 0)
 
     def body(number, carry):
         columns = pl.ds(pl.multiple_of(number * piece, LANES), piece)
@@ -324,7 +324,7 @@
         target[:, columns] = total.astype(target.dtype)
         return carry
 
-    lax.fori_loop(0, pieces, body, 0)
+    lax.fori_loop(0, width // piece, body, 0)
 
 
 def line_targets(at):
@@ -363,173 +363,249 @@
     pltpu.make_async_copy(buffer, buffer, sem).wait()
 
 
-def scatter_scratch(nf, ng, rows, width):
-    dma = pltpu.SemaphoreType.DMA
-    blocks, beyond_g, beyond_f = LINE * nf * ng, (ng - 1) * LINE * nf, (nf - 1) * LINE
-    counts = (blocks, blocks, beyond_g, beyond_f, LINE, LINE)
-    buffers = [pltpu.VMEM((count, rows, width), BF16) for count in counts]
-    sems = (blocks, blocks, blocks, beyond_g, beyond_g, beyond_f, beyond_f, LINE, LINE, LINE, LINE)
-    return buffers + [dma((count,)) for count in sems]
-
-
-SCATTER_SCRATCH = 17
-
-
-def scatter_events(at, sources, owned, scratch, phase):
-    acc, from_pair, from_g, from_f, from_below, from_above = scratch[:6]
-    load_sems, pair_send, pair_recv, g_send, g_recv, f_send, f_recv = scratch[6:13]
-    up_send, up_recv, down_send, down_recv = scratch[13:]
-    rows, width = acc.shape[1], acc.shape[2]
-    order = line_targets(at)
-    other = 1 - at.core
-    send = functools.partial(start_copy, phase)
-
-    def where_is(dz, df, dg):
+class Scatter:
+    PARTS = 17
+
+    @staticmethod
+    def scratch(order, rows, width, nf, ng):
+        dma = pltpu.SemaphoreType.DMA
+        plane, beyond_g = LINE * nf * ng, (ng - 1) * LINE * nf
+        beyond_f = (nf - 1) * (LINE if order == "fz" else 1)
+        line = LINE * (1 if order == "fz" else nf)
+        counts = (plane, plane, beyond_g, beyond_f, line, line)
+        buffers = [pltpu.VMEM((count, rows, width), BF16) for count in counts]
+        sems = (plane, plane, plane, beyond_g, beyond_g, beyond_f, beyond_f, line, line, line, line)
+        return buffers + [dma((count,)) for count in sems]
+
+    def __init__(self, at, source, columns, order, scratch, phase):
+        self.at, self.source, self.columns, self.order = at, source, columns, order
+        self.phase = phase
+        self.acc, self.from_pair, self.from_g, self.from_f = scratch[:4]
+        self.from_below, self.from_above = scratch[4:6]
+        self.load_sems, self.pair_send, self.pair_recv = scratch[6:9]
+        self.g_send, self.g_recv, self.f_send, self.f_recv = scratch[9:13]
+        self.up_send, self.up_recv, self.down_send, self.down_recv = scratch[13:]
+        self.rows = self.acc.shape[1]
+
+    def where_is(self, dz, df, dg):
+        at = self.at
         return at.z + dz, (at.f + df) % at.nf, (at.g + dg) % at.ng
 
-    def spans():
-        start = 0
-        for source in sources:
-            yield source, pl.ds(start, source.shape[1])
-            start += source.shape[1]
-
-    def rows_of(source, z, f, g, core=None):
-        start = pl.multiple_of(at.row_block(z, f, g, core) * rows, rows)
-        return source.at[pl.ds(start, rows), :]
-
-    def begin(dz, df, dg):
-        z, f, g = where_is(dz, df, dg)
+    def rows_of(self, z, f, g, core=None):
+        start = pl.multiple_of(self.at.row_block(z, f, g, core) * self.rows, self.rows)
+        return self.source.at[pl.ds(start, self.rows), self.columns]
+
+    def begin(self, dz, df, dg):
+        at = self.at
+        z, f, g = self.where_is(dz, df, dg)
+        place, other = at.index(z, f, g), 1 - at.core
+        pf, pg = at.split(*at.split(f, g, at.core), other)
+        there = at.index(z, pf, pg)
+
+        def body():
+            if self.phase.ending:
+                await_block(self.from_pair.at[there], self.pair_send.at[there])
+                return
+            pltpu.make_async_copy(
+                self.rows_of(z, f, g), self.acc.at[place], self.load_sems.at[place]
+            ).start()
+            pltpu.make_async_remote_copy(
+                src_ref=self.rows_of(z, pf, pg, other),
+                dst_ref=self.from_pair.at[there],
+                send_sem=self.pair_send.at[there],
+                recv_sem=self.pair_recv.at[there],
+                device_id=at.partner(),
+                device_id_type=MESH,
+            ).start()
+
+        when(present(at, dz), body)
+
+    def join(self, condition, place, parts):
+        if self.phase.ending:
+            return
+
+        def body():
+            ready = [(buffer, sem) for allowed, buffer, sem in parts if allowed is True]
+            for buffer, sem in ready:
+                await_block(buffer, sem)
+            if ready:
+                add_blocks(self.acc.at[place], [buffer for buffer, _ in ready])
+            for allowed, buffer, sem in parts:
+                if allowed is not True:
+
+                    def more(buffer=buffer, sem=sem):
+                        await_block(buffer, sem)
+                        add_blocks(self.acc.at[place], [buffer])
+
+                    pl.when(allowed)(more)
+
+        when(condition, body)
+
+    def over_pair(self, dz, df, dg):
+        at = self.at
+        z, f, g = self.where_is(dz, df, dg)
         condition = present(at, dz)
         place = at.index(z, f, g)
-        pf, pg = at.split(*at.split(f, g, at.core), other)
-        there = at.index(z, pf, pg)
-
-        def body():
-            if phase.ending:
-                await_block(from_pair.at[there], pair_send.at[there])
-                return
-            for source, columns in spans():
-                pltpu.make_async_copy(
-                    rows_of(source, z, f, g), acc.at[place, :, columns], load_sems.at[place]
-                ).start()
-                pltpu.make_async_remote_copy(
-                    src_ref=rows_of(source, z, pf, pg, other),
-                    dst_ref=from_pair.at[there, :, columns],
-                    send_sem=pair_send.at[there],
-                    recv_sem=pair_recv.at[there],
-                    device_id=at.partner(),
-                    device_id_type=MESH,
-                ).start()
-
-        when(condition, body)
-
-    def over_pair(dz, df, dg):
-        z, f, g = where_is(dz, df, dg)
-        condition = present(at, dz)
-        place = at.index(z, f, g)
-
-        def join():
-            await_block(acc.at[place], load_sems.at[place])
-            await_block(from_pair.at[place], pair_recv.at[place])
-            add_blocks(acc.at[place], [from_pair.at[place]], width)
-
-        if not phase.ending:
-            when(condition, join)
+        if not self.phase.ending:
+            when(
+                condition,
+                functools.partial(await_block, self.acc.at[place], self.load_sems.at[place]),
+            )
+        self.join(condition, place, [(True, self.from_pair.at[place], self.pair_recv.at[place])])
         if dg:
             slot = (dg - 1) * LINE * at.nf + z * at.nf + f
-            device = at.device(at.z, at.f, g)
-            send(condition, acc.at[place], from_g.at[slot], g_send.at[slot], g_recv.at[slot], device)
-
-    def over_g(dz, df):
-        z, f, g = where_is(dz, df, 0)
-        condition = present(at, dz)
-        place = at.index(z, f, g)
-
-        def join():
-            parts = []
-            for step in range(1, at.ng):
-                slot = (step - 1) * LINE * at.nf + z * at.nf + f
-                await_block(from_g.at[slot], g_recv.at[slot])
-                parts.append(from_g.at[slot])
-            add_blocks(acc.at[place], parts, width)
-
-        if not phase.ending:
-            when(condition, join)
-        if df:
-            slot = (df - 1) * LINE + z
-            device = at.device(at.z, f, at.g)
-            send(condition, acc.at[place], from_f.at[slot], f_send.at[slot], f_recv.at[slot], device)
-
-    def over_f(dz):
-        z = at.z + dz
-        condition = present(at, dz)
-        place = at.index(z, at.f, at.g)
-
-        def join():
-            parts = []
-            for step in range(1, at.nf):
-                slot = (step - 1) * LINE + z
-                await_block(from_f.at[slot], f_recv.at[slot])
-                parts.append(from_f.at[slot])
-            add_blocks(acc.at[place], parts, width)
-
-            def rise():
-                await_block(from_below.at[z], up_recv.at[z])
-                add_blocks(acc.at[place], [from_below.at[z]], width)
-
-            def sink():
-                await_block(from_above.at[z], down_recv.at[z])
-                add_blocks(acc.at[place], [from_above.at[z]], width)
-
-            if 0 <= dz < LINE - 1:
-                pl.when(at.z > 0)(rise)
-            if 1 - LINE < dz <= 0:
-                pl.when(at.z < LINE - 1)(sink)
-
-        if not phase.ending:
-            when(condition, join)
-        if dz > 0:
-            device = at.device(at.z + 1, at.f, at.g)
-            send(condition, acc.at[place], from_below.at[z], up_send.at[z], up_recv.at[z], device)
-        elif dz < 0:
-            device = at.device(at.z - 1, at.f, at.g)
-            send(condition, acc.at[place], from_above.at[z], down_send.at[z], down_recv.at[z], device)
-
-    def finish():
-        place = at.index(at.z, at.f, at.g)
+            start_copy(
+                self.phase,
+                condition,
+                self.acc.at[place],
+                self.from_g.at[slot],
+                self.g_send.at[slot],
+                self.g_recv.at[slot],
+                at.device(at.z, at.f, g),
+            )
+
+    def g_parts(self, z, f):
+        slots = [(step - 1) * LINE * self.at.nf + z * self.at.nf + f for step in range(1, self.at.ng)]
+        return [(True, self.from_g.at[slot], self.g_recv.at[slot]) for slot in slots]
+
+    def f_slot(self, z, step):
+        return (step - 1) * LINE + z if self.order == "fz" else step - 1
+
+    def f_parts(self, z):
+        slots = [self.f_slot(z, step) for step in range(1, self.at.nf)]
+        return [(True, self.from_f.at[slot], self.f_recv.at[slot]) for slot in slots]
+
+    def line_slot(self, z, f):
+        return z if self.order == "fz" else z * self.at.nf + f
+
+    def line_parts(self, dz, z, f):
+        slot, parts = self.line_slot(z, f), []
+        if 0 <= dz < LINE - 1:
+            parts.append((self.at.z > 0, self.from_below.at[slot], self.up_recv.at[slot]))
+        if 1 - LINE < dz <= 0:
+            parts.append((self.at.z < LINE - 1, self.from_above.at[slot], self.down_recv.at[slot]))
+        return parts
+
+    def send_f(self, condition, df, z, f, place):
+        slot = self.f_slot(z, df)
+        start_copy(
+            self.phase,
+            condition,
+            self.acc.at[place],
+            self.from_f.at[slot],
+            self.f_send.at[slot],
+            self.f_recv.at[slot],
+            self.at.device(self.at.z, f, self.at.g),
+        )
+
+    def send_line(self, condition, dz, z, f, place):
+        slot = self.line_slot(z, f)
+        rising = dz > 0
+        start_copy(
+            self.phase,
+            condition,
+            self.acc.at[place],
+            (self.from_below if rising else self.from_above).at[slot],
+            (self.up_send if rising else self.down_send).at[slot],
+            (self.up_recv if rising else self.down_recv).at[slot],
+            self.at.device(self.at.z + (1 if rising else -1), self.at.f, self.at.g),
+        )
+
+    def second(self, dz, df):
+        z, f, _ = self.where_is(dz, df, 0)
+        condition = present(self.at, dz)
+        place = self.at.index(z, f, self.at.g)
+        parts = self.g_parts(z, f)
+        if self.order == "zf":
+            parts = parts + self.line_parts(dz, z, f)
+        self.join(condition, place, parts)
+        if self.order == "zf" and dz:
+            self.send_line(condition, dz, z, f, place)
+        elif df:
+            self.send_f(condition, df, z, f, place)
+
+    def third(self, dz):
+        z, f = self.at.z + dz, self.at.f
+        condition = present(self.at, dz)
+        place = self.at.index(z, f, self.at.g)
+        parts = self.f_parts(z)
+        if self.order == "fz":
+            parts = parts + self.line_parts(dz, z, f)
+        self.join(condition, place, parts)
+        if dz:
+            self.send_line(condition, dz, z, f, place)
+
+    def stages(self):
+        order = line_targets(self.at)
+        part = functools.partial
+        begins = [part(self.begin, *item) for item in order]
+        pairs = [part(self.over_pair, *item) for item in order]
+        if self.order == "fz":
+            seconds = [part(self.second, *item[:2]) for item in order if item[2] == 0]
+            thirds = [part(self.third, dz) for dz in (-3, 3, -2, 2, -1, 1, 0)]
+        else:
+            dfs = list(range(1, self.at.nf)) + [0]
+            seconds = [part(self.second, dz, df) for dz in (-3, 3, -2, 2, -1, 1, 0) for df in dfs]
+            thirds = [part(self.third, 0)]
+        return begins, pairs, seconds, thirds
+
+    def store(self, target, start):
+        place = self.at.index(self.at.z, self.at.f, self.at.g)
+        target[:, pl.ds(start, self.acc.shape[2])] = self.acc[place].astype(F32)
+
+
+def mixed(first, second):
+    marked = [((i + 0.5) / len(steps), kind, step) for kind, steps in enumerate((first, second)) for i, step in enumerate(steps)]
+    return [step for _, _, step in sorted(marked, key=lambda item: item[:2])]
+
+
+def pipelined(scatters):
+    stages = [scatter.stages() for scatter in scatters]
+    begins = [step for stage in stages for step in stage[0]]
+    events = []
+    for slot in range(len(scatters) + 2):
+        turn_steps = []
+        for kind in (3, 2, 1):
+            number = slot - (kind - 1)
+            if 0 <= number < len(scatters):
+                turn_steps = mixed(turn_steps, stages[number][kind]) if turn_steps else stages[number][kind]
+        events += turn_steps
+    return begins, events
+
+
+def split_scratch(refs, count):
+    size = Scatter.PARTS
+    return [refs[i * size : (i + 1) * size] for i in range(count)], refs[count * size :]
+
+
+def scatter_sections(at, sources, spans, scratches, phase):
+    scatters, places = [], []
+    for number, parts in enumerate(spans):
         start = 0
-        for source, target in zip(sources, owned):
-            size = source.shape[1]
-            if target.shape[1] <= size:
-                target[...] = acc[place, :, start : start + target.shape[1]].astype(F32)
+        for size, order in parts:
+            scratch = scratches[len(scatters)]
+            scatters.append(Scatter(at, sources[number], pl.ds(start, size), order, scratch, phase))
+            places.append((number, start))
             start += size
-
-    part = functools.partial
-    return (
-        [part(begin, *item) for item in order],
-        [part(over_pair, *item) for item in order],
-        [part(over_g, *item[:2]) for item in order if item[2] == 0],
-        [part(over_f, dz) for dz in (-3, 3, -2, 2, -1, 1, 0)],
-        finish,
-    )
-
-
-def scatter_kernel(sizes, count, *refs):
+    return scatters, places
+
+
+def scatter_kernel(sizes, spans, *refs):
     at = Place(*sizes)
+    count, sections = len(spans), sum(len(parts) for parts in spans)
     sources, refs = refs[:count], refs[count:]
-    result_ref, input_ref, vector_ref = refs[:3]
-    owned, refs = refs[3 : 3 + count], refs[3 + count :]
-    out_ref, grad_ref, total_ref = refs[:3]
-    scratch, refs = refs[3 : 3 + SCATTER_SCRATCH], refs[3 + SCATTER_SCRATCH :]
+    input_ref, vector_ref, grad_ref, total_ref = refs[:4]
+    owned, refs = refs[4 : 4 + count], refs[4 + count :]
+    scratches, refs = split_scratch(refs, sections)
     sq_g, sq_f, sq_z, sq_c, trade_send, trade_recv, sq_send, sq_recv = refs
-    slots, positions = out_ref.shape[0], out_ref.shape[1]
-    group = at.seq_size // slots
+    slots = grad_ref.shape[0]
     peers, number = plane_peers(at)
     more, extra = slot_peers(at, slots)
     meet(peers + more, number + extra)
     phase = Phase()
     send = functools.partial(start_copy, phase)
-    begins, pairs, gs, fs, finish = scatter_events(at, sources, owned, scratch, phase)
+    scatters, places = scatter_sections(at, sources, spans, scratches, phase)
+    begins, events = pipelined(scatters)
     other = 1 - at.core
 
     def vectors_g():
@@ -567,46 +643,49 @@
             at.partner(),
         )
 
+    def sums():
+        def g():
+            for step in range(1, at.ng):
+                peer = (at.g + step) % at.ng
+                await_block(sq_g.at[peer], sq_recv.at[0, peer])
+            total = sq_g[0]
+            for number in range(1, at.ng):
+                total = total + sq_g[number]
+            sq_f[at.f] = total
+            vectors_f()
+
+        def f():
+            for step in range(1, at.nf):
+                peer = (at.f + step) % at.nf
+                await_block(sq_f.at[peer], sq_recv.at[1, peer])
+            total = sq_f[0]
+            for number in range(1, at.nf):
+                total = total + sq_f[number]
+            sq_z[at.z] = total
+            vectors_line(0)
+
+        def pair():
+            total = sq_z[0]
+            for number in range(1, LINE):
+                total = total + sq_z[number]
+            sq_c[at.core] = total
+            vectors_pair()
+
+        return [g, f] + [functools.partial(vectors_line, d) for d in range(1, LINE)] + [pair]
+
+    sq_g[at.g] = vector_ref[...]
     run_all(begins)
-    trade_out(at, result_ref, out_ref, trade_send.at[0], trade_recv.at[0], phase)
-    trade_out(at, input_ref, grad_ref, trade_send.at[1], trade_recv.at[1], phase)
-    sq_g[at.g] = vector_ref[...]
     vectors_g()
-    run_all(pairs)
-    for step in range(1, at.ng):
-        peer = (at.g + step) % at.ng
-        await_block(sq_g.at[peer], sq_recv.at[0, peer])
-    total = sq_g[0]
-    for number in range(1, at.ng):
-        total = total + sq_g[number]
-    sq_f[at.f] = total
-    vectors_f()
-    run_all(gs)
-    for step in range(1, at.nf):
-        peer = (at.f + step) % at.nf
-        await_block(sq_f.at[peer], sq_recv.at[1, peer])
-    total = sq_f[0]
-    for number in range(1, at.nf):
-        total = total + sq_f[number]
-    sq_z[at.z] = total
-    vectors_line(0)
-    run_all(fs[:-1])
-    for distance in range(1, LINE):
-        vectors_line(distance)
-    total = sq_z[0]
-    for number in range(1, LINE):
-        total = total + sq_z[number]
-    sq_c[at.core] = total
-    vectors_pair()
-    fs[-1]()
-    finish()
+    trade_out(at, input_ref, grad_ref, trade_send, trade_recv, phase)
+    run_all(mixed(events, sums()))
+    for scatter, (number, start) in zip(scatters, places):
+        scatter.store(owned[number], start)
     await_block(sq_c.at[other], sq_recv.at[3, other])
     total_ref[...] = sq_c[0] + sq_c[1]
 
     phase.ending = True
-    run_all(begins + pairs + gs + fs)
-    trade_out(at, result_ref, out_ref, trade_send.at[0], trade_recv.at[0], phase)
-    trade_out(at, input_ref, grad_ref, trade_send.at[1], trade_recv.at[1], phase)
+    run_all(begins + events)
+    trade_out(at, input_ref, grad_ref, trade_send, trade_recv, phase)
     vectors_g()
     vectors_f()
     for distance in range(LINE):
@@ -614,40 +693,37 @@
     vectors_pair()
 
 
-def scatter_all(sources, result, input_grad, vectors, slots, seq_size, fsdp_size):
+def scatter_last(sources, spans, input_grad, vectors, slots, seq_size, fsdp_size):
     rows = sources[0].shape[0] // (seq_size * fsdp_size)
-    width = sum(source.shape[1] for source in sources)
-    own_rows, model = result.shape
+    own_rows, model = input_grad.shape
     positions = own_rows // slots
     nf, ng = seq_size // (2 * LINE), fsdp_size
     dma = pltpu.SemaphoreType.DMA
     widest = max(nf, ng, LINE)
     vmem = pl.BlockSpec(memory_space=pltpu.VMEM)
-    count = len(sources)
+    scratch = []
+    for parts in spans:
+        for size, order in parts:
+            scratch += Scatter.scratch(order, rows, size, nf, ng)
     return pl.pallas_call(
-        functools.partial(scatter_kernel, (seq_size, fsdp_size), count),
+        functools.partial(scatter_kernel, (seq_size, fsdp_size), spans),
         out_shape=tuple(
-            [jax.ShapeDtypeStruct((rows, source.shape[1]), F32) for source in sources]
-            + [jax.ShapeDtypeStruct((slots, positions, model), BF16)] * 2
-            + [jax.ShapeDtypeStruct(vectors.shape, F32)]
+            [
+                jax.ShapeDtypeStruct((slots, positions, model), BF16),
+                jax.ShapeDtypeStruct(vectors.shape, F32),
+            ]
+            + [jax.ShapeDtypeStruct((rows, source.shape[1]), F32) for source in sources]
         ),
-        in_specs=[pl.BlockSpec(memory_space=pl.ANY)] * count + [vmem] * 3,
-        out_specs=[vmem] * (count + 3),
-        scratch_shapes=scatter_scratch(nf, ng, rows, width)
+        in_specs=[pl.BlockSpec(memory_space=pl.ANY)] * len(sources) + [vmem] * 2,
+        out_specs=[vmem] * (2 + len(sources)),
+        scratch_shapes=scratch
         + [pltpu.VMEM((size, *vectors.shape), F32) for size in (ng, nf, LINE, 2)]
-        + [dma((2, slots)), dma((2, slots)), dma((5, widest)), dma((4, widest))],
+        + [dma((slots,)), dma((slots,)), dma((5, widest)), dma((4, widest))],
         compiler_params=pltpu.CompilerParams(
             collective_id=3, has_side_effects=True, vmem_limit_bytes=63_000_000
         ),
-        name="scatter_all",
-    )(*sources, result, input_grad, vectors)
-
-
-def meet_group(at, group):
-    base, part = (at.seq // group) * group, at.seq % group
-    members = [base + (part + step) % group for step in range(1, group)]
-    meet([(True, (member, at.y)) for member in members], group - 1)
-    return part, members
+        name="scatter_last",
+    )(*sources, input_grad, vectors)
 
 
 def first_half(shape):
@@ -666,70 +742,6 @@
     moved = grads * sine
     away = jnp.where(half, pltpu.roll(moved, 96, 1), -pltpu.roll(moved, 32, 1))
     return grads * cosine + away
-
-
-def sum_kernel(
-    sizes, group, keys_ref, values_ref, cos_ref, sin_ref, out_ref, arrived, send_sems, recv_sems
-):
-    at = Place(*sizes)
-    rows, width = out_ref.shape
-    half = width // 2
-    part, members = meet_group(at, group)
-    waits = []
-    for kind, parts_ref in enumerate((keys_ref, values_ref)):
-        for step, member in enumerate(members):
-            owner = (part + step + 1) % group
-            copy = pltpu.make_async_remote_copy(
-                src_ref=parts_ref.at[pl.ds(pl.multiple_of(owner * rows, rows), rows), :],
-                dst_ref=arrived.at[kind, step],
-                send_sem=send_sems.at[kind, step],
-                recv_sem=recv_sems.at[kind, step],
-                device_id=(member, at.y),
-                device_id_type=MESH,
-            )
-            copy.start()
-            waits.append(copy.wait_send)
-    own = pl.ds(pl.multiple_of(part * rows, rows), rows)
-    cosine, sine = cos_ref[...], sin_ref[...]
-    for kind, parts_ref in enumerate((keys_ref, values_ref)):
-        for step in range(group - 1):
-            await_block(arrived.at[kind, step], recv_sems.at[kind, step])
-
-        def body(number, carry, kind=kind, parts_ref=parts_ref):
-            start = pl.multiple_of(number * LANES, LANES)
-            total = parts_ref[own, pl.ds(start, LANES)].astype(F32)
-            for step in range(group - 1):
-                total = total + arrived[kind, step, :, pl.ds(start, LANES)].astype(F32)
-            if kind == 0:
-                total = turn_back(total, cosine, sine)
-            target = pl.ds(pl.multiple_of(kind * half + number * LANES, LANES), LANES)
-            out_ref[:, target] = total.astype(BF16)
-            return carry
-
-        lax.fori_loop(0, half // LANES, body, 0)
-    for wait in waits:
-        wait()
-
-
-def sum_rows(keys, values, cosine, sine, group, seq_size, fsdp_size):
-    rows, width = keys.shape[0] // group, keys.shape[1]
-    dma = pltpu.SemaphoreType.DMA
-    vmem = pl.BlockSpec(memory_space=pltpu.VMEM)
-    return pl.pallas_call(
-        functools.partial(sum_kernel, (seq_size, fsdp_size), group),
-        out_shape=jax.ShapeDtypeStruct((rows, 2 * width), BF16),
-        in_specs=[vmem] * 4,
-        out_specs=vmem,
-        scratch_shapes=[
-            pltpu.VMEM((2, group - 1, rows, width), BF16),
-            dma((2, group)),
-            dma((2, group)),
-        ],
-        compiler_params=pltpu.CompilerParams(
-            collective_id=2, has_side_effects=True, vmem_limit_bytes=63_000_000
-        ),
-        name="sum_rows",
-    )(keys, values, cosine, sine)
 
 
 def normalize(values):
@@ -986,28 +998,11 @@
     )(length, x_rows, gains, cosine, sine, weight, dy, *sources)
 
 
-def attend_back_kernel(
-    length_ref,
-    q_ref,
-    k_ref,
-    v_ref,
-    g_ref,
-    o_ref,
-    log_ref,
-    cos_ref,
-    sin_ref,
-    dq_ref,
-    dk_ref,
-    dv_ref,
-    dk_acc,
-    dv_acc,
-):
-    step = pl.program_id(1)
-    keys, values, queries = k_ref[...], v_ref[...], q_ref[...] * 0.125
-    grads = g_ref[...]
-    bias = key_bias(length_ref[0], (keys.shape[0], 1))
+def attend_back(length, queries, keys, values, grads, heads_out, logs):
+    queries = queries * 0.125
+    bias = key_bias(length, (keys.shape[0], 1))
     zero = jnp.zeros((), BF16)
-    product = (grads.astype(F32) * o_ref[...].astype(F32)).T
+    product = (grads.astype(F32) * heads_out.astype(F32)).T
     dq = dk = dv = None
     for head in range(2):
         only = head_lanes(queries.shape, head)
@@ -1016,7 +1011,7 @@
         key = jnp.where(head_lanes(keys.shape, head), keys, zero)
         delta = jnp.sum(product[64 * head : 64 * head + 64], axis=0, keepdims=True)
         scores = scores_of(keys, query, bias)
-        probs = jnp.exp(scores - log_ref[0, head : head + 1, :])
+        probs = jnp.exp(scores - logs[head : head + 1])
         grad_probs = lax.dot_general(
             values, grad, (((1,), (1,)), ((), ())), preferred_element_type=F32
         )
@@ -1029,53 +1024,192 @@
         dq = query_part if dq is None else dq + query_part
         dk = key_part if dk is None else dk + key_part
         dv = value_part if dv is None else dv + value_part
-    dq_ref[...] = turn_back(dq.T * 0.125, cos_ref[...], sin_ref[...]).astype(BF16)
+    return dq.T * 0.125, dk, dv
+
+
+def back_kernel(sizes, group, spans, *refs):
+    at = Place(*sizes)
+    sections = sum(len(parts) for parts in spans)
+    count = len(spans)
+    length_ref, q_ref, k_ref, v_ref, g_ref, o_ref, log_ref, cos_ref, sin_ref, result_ref = refs[:10]
+    sources, refs = refs[10 : 10 + count], refs[10 + count :]
+    mixed_ref, out_ref = refs[:2]
+    owned, refs = refs[2 : 2 + count], refs[2 + count :]
+    scratches, refs = split_scratch(refs, sections)
+    dk_acc, dv_acc, parts_ref, arrived, sum_send, sum_recv, trade_send, trade_recv = refs
+    step = pl.program_id(0)
+    tile = q_ref.shape[0]
+    rows, model = result_ref.shape
+    tiles, pairs = rows // tile, model // LANES
+    steps = pairs * tiles + 1
+    slots = out_ref.shape[0]
+    phase = Phase()
+    scatters, places = scatter_sections(at, sources, spans, scratches, phase)
+    begins, events = pipelined(scatters)
+    base, part = (at.seq // group) * group, at.seq % group
+    members = [base + (part + other) % group for other in range(1, group)]
+
+    def columns_of(pair):
+        return pl.ds(pl.multiple_of(pair * LANES, LANES), LANES)
+
+    def share(pair):
+        for kind in range(2):
+            for other, member in enumerate(members):
+                owner = (part + other + 1) % group
+                start_copy(
+                    phase,
+                    True,
+                    parts_ref.at[kind, pl.ds(pl.multiple_of(owner * rows, rows), rows), columns_of(pair)],
+                    arrived.at[kind, other, :, columns_of(pair)],
+                    sum_send.at[kind, other, pair],
+                    sum_recv.at[kind, other, pair],
+                    (member, at.y),
+                )
 
     @pl.when(step == 0)
     def _():
-        dk_acc[...] = dk
-        dv_acc[...] = dv
-
-    @pl.when(step > 0)
+        peers, number = plane_peers(at)
+        more, extra = slot_peers(at, slots)
+        others = [(True, (member, at.y)) for member in members]
+        meet(peers + more + others, number + extra + group - 1)
+        run_all(begins)
+        trade_out(at, result_ref, out_ref, trade_send, trade_recv, phase)
+
+    pl.when(both(step > 0, step % tiles == 0))(lambda: share(step // tiles - 1))
+
+    @pl.when(step < steps - 1)
     def _():
-        dk_acc[...] += dk
-        dv_acc[...] += dv
-
-    @pl.when(step == pl.num_programs(1) - 1)
+        pair, piece = step // tiles, step % tiles
+        own = pl.ds(pl.multiple_of(piece * tile, tile), tile)
+        dq, dk, dv = attend_back(
+            length_ref[0], q_ref[...], k_ref[...], v_ref[...], g_ref[...], o_ref[...], log_ref[0]
+        )
+        mixed_ref[own, columns_of(pair)] = turn_back(dq, cos_ref[own], sin_ref[own]).astype(BF16)
+        if tiles == 1:
+            parts_ref[0, :, columns_of(pair)] = dk.astype(BF16)
+            parts_ref[1, :, columns_of(pair)] = dv.astype(BF16)
+            return
+
+        @pl.when(piece == 0)
+        def _():
+            dk_acc[...] = dk
+            dv_acc[...] = dv
+
+        @pl.when(piece > 0)
+        def _():
+            dk_acc[...] += dk
+            dv_acc[...] += dv
+
+        @pl.when(piece == tiles - 1)
+        def _():
+            parts_ref[0, :, columns_of(pair)] = dk_acc[...].astype(BF16)
+            parts_ref[1, :, columns_of(pair)] = dv_acc[...].astype(BF16)
+
+    def add_parts():
+        own = pl.ds(pl.multiple_of(part * rows, rows), rows)
+
+        def body(pair, carry):
+            for kind in range(2):
+                total = parts_ref[kind, own, columns_of(pair)].astype(F32)
+                for other in range(group - 1):
+                    piece = arrived.at[kind, other, :, columns_of(pair)]
+                    await_block(piece, sum_recv.at[kind, other, pair])
+                    total = total + piece[...].astype(F32)
+                if kind == 0:
+                    total = turn_back(total, cos_ref[...], sin_ref[...])
+                start = pl.multiple_of((kind + 1) * model + pair * LANES, LANES)
+                mixed_ref[:, pl.ds(start, LANES)] = total.astype(BF16)
+            return carry
+
+        lax.fori_loop(0, pairs, body, 0)
+
+    for number in range(steps - 1):
+        some = events[number * BACK_PACE : (number + 1) * BACK_PACE]
+        if some:
+            pl.when(step == number)(functools.partial(run_all, some))
+
+    @pl.when(step == steps - 1)
     def _():
-        dk_ref[...] = dk_acc[...].astype(BF16)
-        dv_ref[...] = dv_acc[...].astype(BF16)
-
-
-def attend_back(lengths, queries, shared, grads, heads_out, logs, cosine, sine, model, tile):
-    rows, keys = queries.shape[0], shared.shape[0]
-    pairs = model // LANES
-    by_row = pl.BlockSpec((tile, LANES), lambda p, i: (i, p))
-    by_key = pl.BlockSpec((keys, LANES), lambda p, i: (0, p))
-    table = pl.BlockSpec((tile, LANES), lambda p, i: (i, 0))
+        add_parts()
+        run_all(events[(steps - 1) * BACK_PACE :])
+        for scatter, (number, start) in zip(scatters, places):
+            scatter.store(owned[number], start)
+        phase.ending = True
+        run_all(begins + events)
+        trade_out(at, result_ref, out_ref, trade_send, trade_recv, phase)
+
+        def body(pair, carry):
+            share(pair)
+            return carry
+
+        lax.fori_loop(0, pairs, body, 0)
+        phase.ending = False
+
+
+BACK_PACE = 5
+
+
+def back(length, queries, shared, grads, heads_out, logs, cosine, sine, result, sources, spans, tile, slots, seq_size, fsdp_size):
+    rows, keys, model = queries.shape[0], shared.shape[0], queries.shape[1]
+    group, positions = keys // rows, rows // slots
+    pairs, tiles = model // LANES, rows // tile
+    nf, ng = seq_size // (2 * LINE), fsdp_size
+    devices = seq_size * fsdp_size
+    shard = sources[0].shape[0] // devices
+    vmem, anywhere = pl.BlockSpec(memory_space=pltpu.VMEM), pl.BlockSpec(memory_space=pl.ANY)
+    dma = pltpu.SemaphoreType.DMA
+
+    def pair_of(i):
+        return jnp.minimum(i, pairs * tiles - 1) // tiles
+
+    def tile_of(i):
+        return jnp.minimum(i, pairs * tiles - 1) % tiles
+
+    by_row = pl.BlockSpec((tile, LANES), lambda i: (tile_of(i), pair_of(i)))
+    scratch = []
+    for parts in spans:
+        for size, order in parts:
+            scratch += Scatter.scratch(order, shard, size, nf, ng)
     return pl.pallas_call(
-        attend_back_kernel,
-        grid=(pairs, rows // tile),
-        out_shape=(
-            jax.ShapeDtypeStruct((rows, model), BF16),
-            jax.ShapeDtypeStruct((keys, model), BF16),
-            jax.ShapeDtypeStruct((keys, model), BF16),
+        functools.partial(back_kernel, (seq_size, fsdp_size), group, spans),
+        grid=(pairs * tiles + 1,),
+        out_shape=tuple(
+            [
+                jax.ShapeDtypeStruct((rows, 3 * model), BF16),
+                jax.ShapeDtypeStruct((slots, positions, model), BF16),
+            ]
+            + [jax.ShapeDtypeStruct((shard, source.shape[1]), F32) for source in sources]
         ),
         in_specs=[
             pl.BlockSpec(memory_space=pltpu.SMEM),
             by_row,
-            by_key,
-            pl.BlockSpec((keys, LANES), lambda p, i: (0, pairs + p)),
+            pl.BlockSpec((keys, LANES), lambda i: (0, pair_of(i))),
+            pl.BlockSpec((keys, LANES), lambda i: (0, pairs + pair_of(i))),
             by_row,
             by_row,
-            pl.BlockSpec((1, 8, tile), lambda p, i: (p, 0, i)),
-            table,
-            table,
+            pl.BlockSpec((1, 8, tile), lambda i: (pair_of(i), 0, tile_of(i))),
+            vmem,
+            vmem,
+            vmem,
+        ]
+        + [anywhere] * len(sources),
+        out_specs=[vmem, anywhere] + [vmem] * len(sources),
+        scratch_shapes=scratch
+        + [
+            pltpu.VMEM((keys, LANES), F32),
+            pltpu.VMEM((keys, LANES), F32),
+            pltpu.VMEM((2, keys, model), BF16),
+            pltpu.VMEM((2, group - 1, rows, model), BF16),
+            dma((2, group - 1, pairs)),
+            dma((2, group - 1, pairs)),
+            dma((slots,)),
+            dma((slots,)),
         ],
-        out_specs=(by_row, by_key, by_key),
-        scratch_shapes=[pltpu.VMEM((keys, LANES), F32), pltpu.VMEM((keys, LANES), F32)],
-        name="attend_back",
-    )(lengths, queries, shared, shared, grads, heads_out, logs, cosine, sine)
+        compiler_params=pltpu.CompilerParams(
+            collective_id=2, has_side_effects=True, vmem_limit_bytes=67_000_000
+        ),
+        name="back",
+    )(length, queries, shared, shared, grads, heads_out, logs, cosine, sine, result, *sources)
 
 
 def rotary_tables(places, head_size):
@@ -1191,11 +1325,30 @@
     attn_part = mm_left_t(heads_out, grad_attn).astype(BF16)
     grad_heads = mm_right_t(grad_attn, w_attn).astype(BF16)
 
-    grad_q, grad_k, grad_v = attend_back(
-        lengths, queries, shared, grad_heads, heads_out, logs, cosine, sine, model, tile
+    second = "zf" if seq_size == 4 * LINE else "fz"
+    early = [(attn_part, ((model, second),)), (down_part, ((wide, second),))]
+    wide_part = (input_part, ((wide, "fz"), (wide, "fz")))
+    if rows * group <= 1024:
+        early, late = [early[0], wide_part, early[1]], []
+    else:
+        late = [wide_part]
+    grad_mixed, out_rows, *owned = back(
+        lengths,
+        queries,
+        shared,
+        grad_heads,
+        heads_out,
+        logs,
+        cosine,
+        sine,
+        result.astype(BF16),
+        [part for part, _ in early],
+        tuple(parts for _, parts in early),
+        tile,
+        slots,
+        seq_size,
+        fsdp_size,
     )
-    grad_kv = sum_rows(grad_k, grad_v, cosine, sine, group, seq_size, fsdp_size)
-    grad_mixed = jnp.concatenate([grad_q, grad_kv], axis=1)
     qkv_part = mm_left_t(act_one, grad_mixed).astype(BF16)
     grad_act_one = mm_right_t(grad_mixed, w_qkv)
     normed_one, inverse_one = normalize(x_wide)
@@ -1203,15 +1356,19 @@
     grad_x = grad_middle + norm_back(grad_act_one, normed_one, inverse_one, gain_attn)
 
     vectors = jnp.stack(squares + [attn_gain_part, mlp_gain_part, jnp.zeros((model,), F32)])
-    own_qkv, own_attn, own_in, own_down, out_rows, grad_rows, totals = scatter_all(
-        [qkv_part, attn_part, input_part, down_part],
-        result.astype(BF16),
+    half = 3 * model // 2
+    late.append((qkv_part, ((half, "fz"), (half, second))))
+    grad_rows, totals, *more = scatter_last(
+        [part for part, _ in late],
+        tuple(parts for _, parts in late),
         grad_x.astype(BF16),
         vectors,
         slots,
         seq_size,
         fsdp_size,
     )
+    own_attn, own_down, own_qkv = owned[0], owned[-1], more[-1]
+    own_in = more[0] if len(more) == 2 else owned[1]
     tokens_valid = jnp.sum(seq_lengths).astype(F32)
     root_squares = jnp.sqrt(jnp.sum(totals[:5], axis=1) / (tokens_valid * model))
     own_gains = lax.dynamic_slice_in_dim(totals, (seq_place * fsdp_size + fsdp_place) * shard, shard, 1)

time: 494 us -> 458 us (0.927)
  Pallas kernels: 366 us -> 338 us
    pallas_call x3 -> x2, Pallas kernels: 211 us -> 182 us  [the longest x1 124 us: back(): pl.pallas_call(functools.partial(back_kernel, (seq_size, fsdp_size), grou...]
    dot_general x4, matrix products: 30 us -> 24.4 us  [mm_right_t(): lax.dot_general(left, right, (((1,), (1,)), ((), ())), preferred_element_...]
where the time goes in v1:
time: 458 us; the launch traced here: 454 us
  Pallas kernels  338 us (74%)
  matrix products  75.8 us (17%)
  other arithmetic  25.3 us (6%)
  local copies, waits for them, and re-layouts  13.7 us (3%)
    pallas_call x1, Pallas kernels, back(): pl.pallas_call(functools.partial(back_kernel, (seq_size, fsdp_size), grou...  124 us
    pallas_call x1, Pallas kernels, front(): pl.pallas_call(functools.partial(front_kernel, (seq_size, fsdp_size), gro...  98 us
    pallas_call x1, Pallas kernels, scatter_last(): pl.pallas_call(functools.partial(scatter_kernel, (seq_size, fsdp_size), s...  57.7 us
    pallas_call x1, Pallas kernels, gather_first(): pl.pallas_call(functools.partial(first_kernel, (seq_size, fsdp_size)), ou...  57.5 us
    dot_general x4, matrix products, mm_left_t(): lax.dot_general(left, right, (((0,), (0,)), ((), ())), preferred_element_...  27.7 us
    dot_general x4, matrix products, mm_right_t(): lax.dot_general(left, right, (((1,), (1,)), ((), ())), preferred_element_...  24.4 us
    dot_general x3, matrix products, mm(): return jnp.dot(left, right, preferred_element_type=F32)  23.7 us
    convert_element_type x1, other arithmetic, shards(): product = (active * gate_half).astype(BF16)  12.9 us

profile of v1, /device:TPU:27, one launch (start us, length us, event | category | flops | bytes accessed | tf_op | source)
XLA Modules:
  0.0 454.3 jit_solution(11231436415047253541)
XLA Ops:
  0.7 1.3 fusion.37
  2.0 1.9 fusion.42
  3.9 0.7 copy.20
  4.6 0.8 copy.19
  5.4 0.1 pad.11.clone
  5.5 0.7 maximum_maximum_fusion.refs_1_
  6.2 57.5 %gather_first.1 = (bf16[1024,3072]{1,0:T(8,128)(2,1)}, bf16[1024,128]{1,0:T(8,128)(2,1)}, bf16[512,1024]{1,0:T(8,128)(2,1)}) custom-call(bf16[32,3072]{1,0:T(8,128)(2,1)} %refs_0_.1, bf16[32,128]{1,0:T(8,128)(2,1)} %maximum_maximum_fusion.refs_1_, bf16[8,64,1024]{2,1,0:T(8,128)(2,1)} %refs_2_.1), custom_call_target="tpu_custom_call" | custom-call | tf_op jit(solution)/shard_map/gather_first/pallas_call | solution.py:300
  63.7 0.1 broadcast_multiply_fusion
  63.8 2.1 fusion.32
  66.0 1.1 fusion.46
  67.1 0.8 concatenate.21.refs_8_
  67.9 1.6 concatenate.22.refs_9_
  69.5 98.0 %front.1 = (bf16[512,1024]{1,0:T(8,128)(2,1)}, f32[8,1024]{1,0:T(8,128)}, bf16[512,1024]{1,0:T(8,128)(2,1)}, bf16[1024,2048]{1,0:T(8,128)(2,1)}, bf16[512,1024]{...) custom-call(s32[1]{0:T(128)} %bitcast.refs_0_, ...), custom_call_target="tpu_custom_call" | custom-call | tf_op jit(solution)/shard_map/front/pallas_call | solution.py:956
  167.6 0.0 copy-done
  167.6 0.2 convert_reduce_fusion
  167.8 4.7 %fusion.44 = (f32[512]{0:T(512)S(1)}, f32[512,1024]{1,0:T(8,128)S(1)}, f32[512]{0:T(512)S(1)}, f32[512,1024]{1,0:T(8,128)}) fusion(bf16[512,1024]{1,0:T(8,128)(2,1)S(1)} %copy-done, f32[512]{0:T(512)S(1)} %broadcast_multiply_fusion.3, bf16[512,1024]{1,0:T(8,128)(2,1)} %get-tuple-element.36.refs_5_, bf16[1024,1024]{1,0:T(8,128)(2,1)} %get-tuple-element.37), kind=kOutput, calls=%fused_computation.101 | convolution fusion | flops 1076886528 | bytes 8394752 | tf_op jit(solution)/shard_map/dot_general | solution.py:1229
  172.5 0.8 fusion.47
  173.3 0.3 multiply_reduce_fusion.2
  173.7 9.2 %fusion.41 = f32[512,5376]{1,0:T(8,128)S(1)} fusion(bf16[1024,5376]{1,0:T(8,128)(2,1)} %get-tuple-element.39, f32[512,1024]{1,0:T(8,128)S(1)} %get-tuple-element.70, f32[1024]{0:T(1024)S(1)} %bitcast.34, f32[512]{0:T(512)S(1)} %add_rsqrt_fusion.1, f32[512]{0:T(512)S(1)} %get-tuple-element.88), kind=kOutput, calls=%fused_computation.99 | convolution fusion | flops 5639241728 | bytes 24125440 | tf_op jit(solution)/shard_map/dot_general | solution.py:1229
  182.9 0.0 copy-start.7
  182.9 12.9 %multiply_convert_fusion = (bf16[512,2688]{1,0:T(8,128)(2,1)S(1)}, f32[512,2688]{1,0:T(8,128)}) fusion(f32[512,5376]{1,0:T(8,128)S(1)} %fusion.41), kind=kLoop, calls=%fused_computation.6 | loop fusion | flops 90832896 | bytes 19267584 | tf_op jit(solution)/shard_map/convert_element_type | solution.py:1306
  195.8 0.6 fusion.36
  196.4 0.0 slice-start
  196.5 9.8 %add_convert_fusion = (bf16[512,2688]{1,0:T(8,128)(2,1)S(1)}, bf16[512,2688]{1,0:T(8,128)(2,1)}) fusion(f32[512,2688]{1,0:T(8,128)} %get-tuple-element.68, f32[512,5376]{1,0:T(8,128)S(1)} %fusion.41, bf16[1024,2688]{1,0:T(8,128)(2,1)} %get-tuple-element.40, bf16[512,1024]{1,0:T(8,128)(2,1)S(1)} %copy-done.7, f32[512]{0:T(512)S(1)} %fusion.36), kind=kOutput, calls=%fused_computation.8 | convolution fusion | flops 2844917760 | bytes 28575744 | tf_op jit(solution)/shard_map/dot_general | solution.py:1229
  206.2 10.7 %fusion.7 = f32[512,1024]{1,0:T(8,128)S(1)} fusion(bf16[1024,5376]{1,0:T(8,128)(2,1)} %get-tuple-element.39, bf16[512,2688]{1,0:T(8,128)(2,1)} %get-tuple-element.72, bf16[512,2688]{1,0:T(8,128)(2,1)S(1)} %get-tuple-element.71), kind=kOutput, calls=%fused_computation.29 | convolution fusion | flops 5648154624 | bytes 18612224 | tf_op jit(solution)/shard_map/dot_general | solution.py:1233
  217.0 5.1 %fusion.23 = (f32[1024]{0:T(1024)S(1)}, f32[1024]{0:T(1024)S(1)}, f32[1024]{0:T(1024)S(1)}, f32[512]{0:T(512)S(1)}, f32[512]{0:T(512)S(1)}, /*index=5*/f32[1024]{0:T(1024)S(1)}, bf16[512,1024]{1,0:T(8,128)(2,1)}) fusion(f32[512]{0:T(512)S(1)} %fusion.36, f32[512,1024]{1,0:T(8,128)S(1)} %get-tuple-element.70, f32[512,1024]{1,0:T(8,128)S(1)} %fusion.7, ...), kind=kOutput, calls=%fused_computation.49 | convolution fusion | flops 2829052928 | bytes 13531136 | tf_op jit(solution)/shard_map/dot_general | solution.py:1233
  222.1 0.8 multiply_add_fusion
  222.9 0.7 copy-done.12
  223.7 2.3 convolution_convert_fusion.4.refs_4_
  225.9 2.6 convolution_convert_fusion.3.refs_10_
  228.5 11.5 %convolution_convert_fusion.refs_11_ = bf16[1024,5376]{1,0:T(8,128)(2,1)} fusion(bf16[512,2688]{1,0:T(8,128)(2,1)} %get-tuple-element.72, bf16[512,2688]{1,0:T(8,128)(2,1)} %copy-done.14, f32[512,1024]{1,0:T(8,128)S(1)} %get-tuple-element.70, f32[1024]{0:T(1024)S(1)} %bitcast.37, f32[512]{0:T(512)S(1)} %add_rsqrt_fusion.1, f32[512]{0:T(512)S(1)} %get-tuple-element.88), kind=kOutput, calls=%fused_computation | convolution fusion | flops 5655756800 | bytes 18620416 | tf_op jit(solution)/shard_map/dot_general | solution.py:1237
  240.0 5.2 %convolution_convert_fusion.2.refs_12_ = bf16[1024,2688]{1,0:T(8,128)(2,1)} fusion(bf16[512,2688]{1,0:T(8,128)(2,1)S(1)} %get-tuple-element.67, bf16[512,1024]{1,0:T(8,128)(2,1)S(1)} %copy-done.7, f32[512]{0:T(512)S(1)} %fusion.36), kind=kOutput, calls=%fused_computation.3 | convolution fusion | flops 2822897664 | bytes 9308160 | tf_op jit(solution)/shard_map/dot_general | solution.py:1237
  245.2 124.4 %back.1 = (bf16[512,3072]{1,0:T(8,128)(2,1)}, bf16[8,64,1024]{2,1,0:T(8,128)(2,1)}, f32[32,1024]{1,0:T(8,128)}, f32[32,5376]{1,0:T(8,128)}, f32[32,2688]{1,0:T(8,128)}) custom-call(s32[1]{0:T(128)} %bitcast.refs_0_, bf16[512,1024]{1,0:T(8,128)(2,1)} %get-tuple-element.33.refs_1_, bf16[1024,2048]{1,0:T(8,128)(2,1)} %get-tuple-element.34.refs_2_.refs_3_, ...), custom_call_target="tpu_custom_call" | custom-call | tf_op jit(solution)/shard_map/back/pallas_call | solution.py:1173
  369.7 8.5 %convolution_convert_fusion.1.refs_0_ = bf16[1024,3072]{1,0:T(8,128)(2,1)} fusion(bf16[512,1024]{1,0:T(8,128)(2,1)} %get-tuple-element.43, bf16[512,3072]{1,0:T(8,128)(2,1)} %get-tuple-element.44), kind=kOutput, calls=%fused_computation.2 | convolution fusion | flops 3224371200 | bytes 10485760 | tf_op jit(solution)/shard_map/dot_general | solution.py:1237
  378.2 6.4 %fusion.18 = (f32[1024]{0:T(1024)S(1)}, f32[512]{0:T(512)S(1)}, f32[512]{0:T(512)S(1)}, f32[1024]{0:T(1024)S(1)}, f32[1024]{0:T(1024)S(1)}, /*index=5*/f32[512,1024]{1,0:T(8,128)S(1)}) fusion(bf16[512,1024]{1,0:T(8,128)(2,1)S(1)} %copy-done.1, f32[512]{0:T(512)S(1)} %get-tuple-element.87, f32[512]{0:T(512)S(1)} %broadcast_multiply_fusion.3, ...), kind=kOutput, calls=%fused_computation.44 | convolution fusion | flops 3229085696 | bytes 14706688 | tf_op jit(solution)/shard_map/dot_general | solution.py:1233
  384.6 1.7 fusion.17.refs_1_
  386.3 0.7 stack.31.refs_2_
  387.0 57.7 %scatter_last.1 = (bf16[8,64,1024]{2,1,0:T(8,128)(2,1)}, f32[8,1024]{1,0:T(8,128)}, f32[32,3072]{1,0:T(8,128)}) custom-call(bf16[1024,3072]{1,0:T(8,128)(2,1)} %convolution_convert_fusion.1.refs_0_, bf16[512,1024]{1,0:T(8,128)(2,1)} %fusion.17.refs_1_, f32[8,1024]{1,0:T(8,128)} %stack.31.refs_2_), custom_call_target="tpu_custom_call" | custom-call | tf_op jit(solution)/shard_map/scatter_last/pallas_call | solution.py:708
  444.8 1.0 pad_maximum_fusion.3
  445.8 0.8 slice_bitcast_fusion
  446.5 0.7 constant_dynamic-slice_fusion
  447.3 0.5 slice_bitcast_fusion.1
  447.8 0.9 slice_reduce_fusion
  449.2 0.5 divide_sqrt_fusion
  449.8 1.0 copy.25
  450.8 1.0 copy.26
  451.7 0.7 copy.27
  452.5 1.6 copy.28
  (44 shorter events, 0.2 us)
Async XLA Ops:
  67.1 100.5 %copy-start = (bf16[512,1024]{1,0:T(8,128)(2,1)S(1)}, bf16[512,1024]{1,0:T(8,128)(2,1)}, u32[]{:S(2)}) copy-start(bf16[512,1024]{1,0:T(8,128)(2,1)} %get-tuple-element.30.refs_1_) | copy-start | bytes 3145732
  182.9 13.5 %copy-start.7 = (bf16[512,1024]{1,0:T(8,128)(2,1)S(1)}, bf16[512,1024]{1,0:T(8,128)(2,1)}, u32[]{:S(2)}) copy-start(bf16[512,1024]{1,0:T(8,128)(2,1)} %get-tuple-element.35) | copy-start | bytes 3145732
  196.4 20.5 %slice-start = ((s8[5505024]{0:T(1024)(128)(4,1)}), s8[1310720]{0:T(1024)(128)(4,1)S(1)}, s32[]{:S(2)}) async-start(s8[5505024]{0:T(1024)(128)(4,1)} %bitcast.49), calls=%async_computation | async-start | bytes 2621440
  206.2 10.7 %copy-start.14 = (bf16[512,2688]{1,0:T(8,128)(2,1)}, bf16[512,2688]{1,0:T(8,128)(2,1)S(1)}, u32[]{:S(2)}) copy-start(bf16[512,2688]{1,0:T(8,128)(2,1)S(1)} %get-tuple-element.71) | copy-start | bytes 8257540
  206.2 10.7 %slice-start.1 = ((s8[5505024]{0:T(1024)(128)(4,1)}), s8[4194304]{0:T(1024)(128)(4,1)S(1)}, s32[]{:S(2)}) async-start(s8[5505024]{0:T(1024)(128)(4,1)} %bitcast.49), calls=%async_computation.1 | async-start | bytes 8388608
  222.1 1.6 copy-start.12
  222.1 3.9 copy-start.4
  223.7 2.3 copy-start.2
  369.6 8.5 %copy-start.1 = (bf16[512,1024]{1,0:T(8,128)(2,1)S(1)}, bf16[512,1024]{1,0:T(8,128)(2,1)}, u32[]{:S(2)}) copy-start(bf16[512,1024]{1,0:T(8,128)(2,1)} %get-tuple-element.30.refs_1_) | copy-start | bytes 3145732
  369.6 8.5 %copy-start.11 = (bf16[512,3072]{1,0:T(8,128)(2,1)S(1)}, bf16[512,3072]{1,0:T(8,128)(2,1)}, u32[]{:S(2)}) copy-start(bf16[512,3072]{1,0:T(8,128)(2,1)} %get-tuple-element.44) | copy-start | bytes 9437188
  369.6 8.5 %copy-start.13 = (f32[512,1024]{1,0:T(8,128)S(1)}, f32[512,1024]{1,0:T(8,128)}, u32[]{:S(2)}) copy-start(f32[512,1024]{1,0:T(8,128)} %get-tuple-element.85) | copy-start | bytes 6291460
  378.2 6.4 %copy-start.3 = (f32[512,1024]{1,0:T(8,128)S(1)}, f32[512,1024]{1,0:T(8,128)}, u32[]{:S(2)}) copy-start(f32[512,1024]{1,0:T(8,128)} %copy-done.2) | copy-start | bytes 6291460
  384.6 60.1 %copy-start.8 = (f32[32,5376]{1,0:T(8,128)S(1)}, f32[32,5376]{1,0:T(8,128)}, u32[]{:S(2)}) copy-start(f32[32,5376]{1,0:T(8,128)} %get-tuple-element.48) | copy-start | bytes 2064388
  386.3 59.5 %copy-start.10 = (f32[32,2688]{1,0:T(8,128)S(1)}, f32[32,2688]{1,0:T(8,128)}, u32[]{:S(2)}) copy-start(f32[32,2688]{1,0:T(8,128)} %get-tuple-element.49) | copy-start | bytes 1032196
  386.3 63.5 %copy-start.5 = (bf16[8,64,1024]{2,1,0:T(8,128)(2,1)S(1)}, bf16[8,64,1024]{2,1,0:T(8,128)(2,1)}, u32[]{:S(2)}) copy-start(bf16[8,64,1024]{2,1,0:T(8,128)(2,1)} %get-tuple-element.98) | copy-start | bytes 3145732
  444.7 6.1 %copy-start.6 = (bf16[8,64,1024]{2,1,0:T(8,128)(2,1)S(1)}, bf16[8,64,1024]{2,1,0:T(8,128)(2,1)}, u32[]{:S(2)}) copy-start(bf16[8,64,1024]{2,1,0:T(8,128)(2,1)} %get-tuple-element.99) | copy-start | bytes 3145732
  444.7 7.0 %copy-start.9 = (f32[32,3072]{1,0:T(8,128)S(1)}, f32[32,3072]{1,0:T(8,128)}, u32[]{:S(2)}) copy-start(f32[32,3072]{1,0:T(8,128)} %get-tuple-element.100) | copy-start | bytes 1179652

commit v2 on v1

--- a/solution.py
+++ b/solution.py
@@ -22,10 +22,10 @@
 
 
 class Place:
-    def __init__(self, seq_size, fsdp_size):
+    def __init__(self, seq_size, fsdp_size, swap=True):
         self.seq_size, self.fsdp_size = seq_size, fsdp_size
         self.rest = seq_size // (2 * LINE)
-        self.swap = self.rest == fsdp_size
+        self.swap = swap and self.rest == fsdp_size
         self.nf, self.ng = self.rest, fsdp_size
         self.blocks = LINE * self.nf * self.ng
         self.seq = lax.axis_index("seq")
@@ -120,7 +120,7 @@
             for dg in range(at.ng):
                 out.append((abs(dz) + (df > 0) + (dg > 0), dz, df, dg))
     out.sort(key=lambda item: item[0])
-    return [item[1:] for item in out]
+    return out
 
 
 def present(at, dz):
@@ -132,6 +132,8 @@
 class Gather:
     def __init__(self, at, sections, sems, phase):
         self.at, self.sections, self.phase = at, sections, phase
+        plain = Place(at.seq_size, at.fsdp_size, swap=False)
+        self.places = [plain if section[3][-1] == "-" else at for section in sections]
         self.send_sems, self.plane_sems, self.pair_sems = sems
 
     @staticmethod
@@ -147,11 +149,11 @@
     def block(self, number, z, f, g):
         source, whole, columns, _ = self.sections[number]
         rows = source.shape[0]
-        start = pl.multiple_of(self.at.row_block(z, f, g) * rows, rows)
+        start = pl.multiple_of(self.places[number].row_block(z, f, g) * rows, rows)
         return whole.at[pl.ds(start, rows), columns]
 
     def forward(self, number, condition, source, dz, df, dg):
-        at, order = self.at, self.sections[number][3]
+        at, order = self.places[number], self.sections[number][3].strip("-")
         z, f, g = at.z + dz, (at.f + df) % at.nf, (at.g + dg) % at.ng
         place, target = at.index(z, f, g), self.block(number, z, f, g)
         moved = {"z": dz, "f": df, "g": dg}
@@ -185,8 +187,8 @@
         send(True, at.nf + at.ng, at.partner(), pair=True)
 
     def begin(self):
-        at = self.at
         for number in range(len(self.sections)):
+            at = self.places[number]
             self.forward(number, True, self.own(number), 0, 0, 0)
             own = pltpu.make_async_copy(
                 self.own(number),
@@ -199,7 +201,7 @@
                 own.start()
 
     def arrival(self, number, dz, df, dg):
-        at = self.at
+        at = self.places[number]
         z, f, g = at.z + dz, (at.f + df) % at.nf, (at.g + dg) % at.ng
         condition = present(at, dz)
         block = self.block(number, z, f, g)
@@ -209,16 +211,47 @@
         self.forward(number, condition, block, dz, df, dg)
 
     def events(self):
-        return [
-            functools.partial(self.arrival, number, *item)
-            for item in steps_of(self.at)[1:]
+        marked = [
+            (hops, number, place, item)
+            for place, (hops, *item) in enumerate(steps_of(self.at)[1:])
             for number in range(len(self.sections))
         ]
-
-    def finish(self):
-        for number in range(len(self.sections)):
-            for place in range(self.at.blocks):
-                await_block(self.block(number, 0, 0, 0), self.pair_sems.at[number, place])
+        marked.sort(key=lambda entry: entry[:3])
+        return [functools.partial(self.arrival, number, *item) for _, number, _, item in marked]
+
+    def from_partner(self, number, dz, df, dg):
+        at = self.places[number]
+        f, g = at.split(*at.split(at.f, at.g, at.core), 1 - at.core)
+        z, f, g = at.z + dz, (f + df) % at.nf, (g + dg) % at.ng
+        sem = self.pair_sems.at[number, at.index(z, f, g)]
+        when(
+            present(at, dz), functools.partial(await_block, self.block(number, 0, 0, 0), sem)
+        )
+
+    def steps(self, lag):
+        events = self.events()
+
+        def close(event):
+            self.phase.ending = True
+            event()
+            self.from_partner(*event.args)
+            self.phase.ending = False
+
+        def step(number):
+            events[number]()
+            if number >= lag:
+                close(events[number - lag])
+
+        def rest():
+            for event in events[-lag:]:
+                close(event)
+            self.phase.ending = True
+            self.begin()
+            for number in range(len(self.sections)):
+                self.from_partner(number, 0, 0, 0)
+            self.phase.ending = False
+
+        return [functools.partial(step, number) for number in range(len(events))], rest
 
 
 def trade_in(at, source_ref, target_ref, send_sems, recv_sems, phase):
@@ -271,25 +304,34 @@
             await_block(target_ref.at[step], recv_sems.at[step])
 
 
-def first_kernel(sizes, *refs):
+def first_kernel(sizes, spans, weight_ref, gains_ref, hidden_ref, whole_ref, rows_ref, *refs):
     at = Place(*sizes)
-    weight_ref, gains_ref, hidden_ref, whole_ref, all_gains_ref, rows_ref = refs[:6]
-    sems, (trade_send, trade_recv) = refs[6:9], refs[9:]
+    sems, (trade_send, trade_recv, pack_ref, pack_sems) = refs[:3], refs[3:]
+    width, extra_width = weight_ref.shape[1], gains_ref.shape[1]
+    loads = [
+        pltpu.make_async_copy(weight_ref, pack_ref.at[:, pl.ds(0, width)], pack_sems.at[0]),
+        pltpu.make_async_copy(gains_ref, pack_ref.at[:, pl.ds(width, extra_width)], pack_sems.at[1]),
+    ]
+    for load in loads:
+        load.start()
     peers, count = plane_peers(at)
     more, extra = slot_peers(at, hidden_ref.shape[0])
     meet(peers + more, count + extra)
+    for load in loads:
+        load.wait()
     phase = Phase()
-    sections = [
-        (weight_ref, whole_ref, pl.ds(0, weight_ref.shape[1]), "zfg"),
-        (gains_ref, all_gains_ref, pl.ds(0, gains_ref.shape[1]), "zfg"),
-    ]
+    sections, start = [], 0
+    for size, order in spans:
+        sections.append((pack_ref, whole_ref, pl.ds(start, size), order))
+        start += size
     gather = Gather(at, sections, sems, phase)
-    events = gather.events()
-    for phase.ending in (False, True):
-        gather.begin()
-        trade_in(at, hidden_ref, rows_ref, trade_send, trade_recv, phase)
-        run_all(events)
-    gather.finish()
+    steps, rest = gather.steps(12)
+    gather.begin()
+    trade_in(at, hidden_ref, rows_ref, trade_send, trade_recv, phase)
+    run_all(steps)
+    rest()
+    phase.ending = True
+    trade_in(at, hidden_ref, rows_ref, trade_send, trade_recv, phase)
 
 
 def gather_first(weight, gains, hidden, seq_size, fsdp_size):
@@ -297,16 +339,19 @@
     nf, ng = seq_size // (2 * LINE), fsdp_size
     devices = seq_size * fsdp_size
     dma = pltpu.SemaphoreType.DMA
+    shard, width = weight.shape[0], weight.shape[1] + gains.shape[1]
+    half = weight.shape[1] // 2
+    spans = ((half, "zfg"), (width - half, "zfg"))
     return pl.pallas_call(
-        functools.partial(first_kernel, (seq_size, fsdp_size)),
+        functools.partial(first_kernel, (seq_size, fsdp_size), spans),
         out_shape=(
-            jax.ShapeDtypeStruct((weight.shape[0] * devices, weight.shape[1]), BF16),
-            jax.ShapeDtypeStruct((gains.shape[0] * devices, gains.shape[1]), BF16),
+            jax.ShapeDtypeStruct((shard * devices, width), BF16),
             jax.ShapeDtypeStruct((slots * positions, model), BF16),
         ),
         in_specs=[pl.BlockSpec(memory_space=pltpu.VMEM)] * 3,
-        out_specs=[pl.BlockSpec(memory_space=pl.ANY)] * 3,
-        scratch_shapes=Gather.scratch(2, nf, ng) + [dma((slots,)), dma((slots,))],
+        out_specs=[pl.BlockSpec(memory_space=pl.ANY)] * 2,
+        scratch_shapes=Gather.scratch(len(spans), nf, ng)
+        + [dma((slots,)), dma((slots,)), pltpu.VMEM((shard, width), BF16), dma((2,))],
         compiler_params=pltpu.CompilerParams(collective_id=0, has_side_effects=True),
         name="gather_first",
     )(weight, gains, hidden)
@@ -314,7 +359,7 @@
 
 def add_blocks(target, others):
     width = target.shape[1]
-    piece = next(size for size in (512, 384, 256, LANES) if width % size == 0)
+    piece = max(size for size in range(LANES, 1025, LANES) if width % size == 0)
 
     def body(number, carry):
         columns = pl.ds(pl.multiple_of(number * piece, LANES), piece)
@@ -555,22 +600,48 @@
 
 
 def mixed(first, second):
-    marked = [((i + 0.5) / len(steps), kind, step) for kind, steps in enumerate((first, second)) for i, step in enumerate(steps)]
+    marked = []
+    for kind, steps in enumerate((first, second)):
+        marked += [((i + 0.5) / len(steps), kind, step) for i, step in enumerate(steps)]
     return [step for _, _, step in sorted(marked, key=lambda item: item[:2])]
 
 
 def pipelined(scatters):
-    stages = [scatter.stages() for scatter in scatters]
-    begins = [step for stage in stages for step in stage[0]]
-    events = []
-    for slot in range(len(scatters) + 2):
-        turn_steps = []
-        for kind in (3, 2, 1):
-            number = slot - (kind - 1)
-            if 0 <= number < len(scatters):
-                turn_steps = mixed(turn_steps, stages[number][kind]) if turn_steps else stages[number][kind]
-        events += turn_steps
-    return begins, events
+    begins, first, mids, lasts = [], [], [], []
+    for scatter in scatters:
+        starts, pairs, seconds, thirds = scatter.stages()
+        begins += starts
+        first += [step for step in pairs if step.args[2]]
+        mid = []
+        for second in seconds:
+            mid += [step for step in pairs if step.args == (*second.args, 0)] + [second]
+        mids.append(mid)
+        lasts.append(thirds)
+    events = list(first)
+    for slot in range(len(scatters) + 1):
+        some = lasts[slot - 1] if slot else []
+        if slot < len(scatters):
+            some = mixed(some, mids[slot]) if some else mids[slot]
+        events += some
+    return begins, events, len(first)
+
+
+def lagged(events, lag, phase):
+    def close(event):
+        phase.ending = True
+        event()
+        phase.ending = False
+
+    def step(number):
+        events[number]()
+        if number >= lag:
+            close(events[number - lag])
+
+    def rest():
+        for event in events[-lag:]:
+            close(event)
+
+    return [functools.partial(step, number) for number in range(len(events))], rest
 
 
 def split_scratch(refs, count):
@@ -605,7 +676,8 @@
     phase = Phase()
     send = functools.partial(start_copy, phase)
     scatters, places = scatter_sections(at, sources, spans, scratches, phase)
-    begins, events = pipelined(scatters)
+    begins, events, _ = pipelined(scatters)
+    steps, rest = lagged(events, 24, phase)
     other = 1 - at.core
 
     def vectors_g():
@@ -677,14 +749,15 @@
     run_all(begins)
     vectors_g()
     trade_out(at, input_ref, grad_ref, trade_send, trade_recv, phase)
-    run_all(mixed(events, sums()))
+    run_all(mixed(steps, sums()))
     for scatter, (number, start) in zip(scatters, places):
         scatter.store(owned[number], start)
     await_block(sq_c.at[other], sq_recv.at[3, other])
     total_ref[...] = sq_c[0] + sq_c[1]
 
+    rest()
     phase.ending = True
-    run_all(begins + events)
+    run_all(begins)
     trade_out(at, input_ref, grad_ref, trade_send, trade_recv, phase)
     vectors_g()
     vectors_f()
@@ -912,7 +985,7 @@
         for head in range(2):
             log_ref[0, head : head + 1, :] = logs[head]
 
-    events = gather.events()
+    events, rest = gather.steps(24)
     pace = FRONT_PACE
     for number in range(steps - 1):
         group_events = events[number * pace : (number + 1) * pace]
@@ -922,21 +995,19 @@
     @pl.when(step == steps - 1)
     def _():
         run_all(events[(steps - 1) * pace :])
+        rest()
         phase.ending = True
-        gather.begin()
         trade_in(at, dy_ref, dy_rows_ref, trade_send, trade_recv, phase)
-        run_all(events)
         for number in range(kept):
             share(number)
-        gather.finish()
         pltpu.make_async_copy(shared_ref, shared_out, out_sem).wait()
         phase.ending = False
 
 
-FRONT_PACE = 2
-
-
-def front(length, x_rows, gains, cosine, sine, weight, dy, sources, spans, group, tile, seq_size, fsdp_size):
+FRONT_PACE = 4
+
+
+def front(length, x_rows, cosine, sine, weight, dy, sources, spans, group, tile, seq_size, fsdp_size):
     rows, model = x_rows.shape
     slots, positions, _ = dy.shape
     pairs, tiles = model // LANES, rows // tile
@@ -971,7 +1042,8 @@
                 for source in sources
             ]
         ),
-        in_specs=[pl.BlockSpec(memory_space=pltpu.SMEM), vmem, vmem, vmem, vmem]
+        in_specs=[pl.BlockSpec(memory_space=pltpu.SMEM), vmem]
+        + [pl.BlockSpec((model, LANES), lambda i: (0, 3 * model // LANES)), vmem, vmem]
         + [
             pl.BlockSpec(
                 (model, FRONT_TILE),
@@ -995,7 +1067,7 @@
             collective_id=1, has_side_effects=True, vmem_limit_bytes=63_000_000
         ),
         name="front",
-    )(length, x_rows, gains, cosine, sine, weight, dy, *sources)
+    )(length, x_rows, weight, cosine, sine, weight, dy, *sources)
 
 
 def attend_back(length, queries, keys, values, grads, heads_out, logs):
@@ -1045,7 +1117,8 @@
     slots = out_ref.shape[0]
     phase = Phase()
     scatters, places = scatter_sections(at, sources, spans, scratches, phase)
-    begins, events = pipelined(scatters)
+    begins, events, ahead = pipelined(scatters)
+    events, rest = lagged(events, 40, phase)
     base, part = (at.seq // group) * group, at.seq % group
     members = [base + (part + other) % group for other in range(1, group)]
 
@@ -1074,6 +1147,12 @@
         meet(peers + more + others, number + extra + group - 1)
         run_all(begins)
         trade_out(at, result_ref, out_ref, trade_send, trade_recv, phase)
+        run_all(events[:ahead])
+
+    for number in range(1, steps):
+        some = events[ahead + (number - 1) * BACK_PACE : ahead + number * BACK_PACE]
+        if some:
+            pl.when(step == number)(functools.partial(run_all, some))
 
     pl.when(both(step > 0, step % tiles == 0))(lambda: share(step // tiles - 1))
 
@@ -1123,19 +1202,15 @@
 
         lax.fori_loop(0, pairs, body, 0)
 
-    for number in range(steps - 1):
-        some = events[number * BACK_PACE : (number + 1) * BACK_PACE]
-        if some:
-            pl.when(step == number)(functools.partial(run_all, some))
-
     @pl.when(step == steps - 1)
     def _():
         add_parts()
-        run_all(events[(steps - 1) * BACK_PACE :])
+        run_all(events[ahead + (steps - 1) * BACK_PACE :])
         for scatter, (number, start) in zip(scatters, places):
             scatter.store(owned[number], start)
+        rest()
         phase.ending = True
-        run_all(begins + events)
+        run_all(begins)
         trade_out(at, result_ref, out_ref, trade_send, trade_recv, phase)
 
         def body(pair, carry):
@@ -1146,7 +1221,7 @@
         phase.ending = False
 
 
-BACK_PACE = 5
+BACK_PACE = 3
 
 
 def back(length, queries, shared, grads, heads_out, logs, cosine, sine, result, sources, spans, tile, slots, seq_size, fsdp_size):
@@ -1266,7 +1341,7 @@
     )
     in_pack = jnp.concatenate([in_weight[:, :ff], lead, in_weight[:, ff:], lead], axis=1)
     down_pack = jnp.concatenate([down_weight.T, lead], axis=1)
-    w_qkv, all_gains, x_rows = gather_first(qkv_weight, gains, hidden_in, seq_size, fsdp_size)
+    w_qkv, x_rows = gather_first(qkv_weight, gains, hidden_in, seq_size, fsdp_size)
 
     slot = fsdp_place * slots + seq_place // group
     order = jnp.sum(jnp.where(jnp.arange(slot_order.shape[0]) == slot, slot_order, 0))
@@ -1280,13 +1355,12 @@
     act_one, gain_rows, queries, shared, heads_out, logs, dy_rows, w_attn, w_input, w_down = front(
         lengths,
         x_rows,
-        all_gains,
         cosine,
         sine,
         w_qkv,
         out_grad,
         (attn_out_weight, in_pack, down_pack),
-        (((model, "fzg"),), ((wide, "zfg"), (wide, "zfg")), ((wide, "fzg"),)),
+        (((model, "fzg-"),), ((wide, "zfg"), (wide, "zfg")), ((wide, "fzg"),)),
         group,
         tile,
         seq_size,
@@ -1329,7 +1403,7 @@
     early = [(attn_part, ((model, second),)), (down_part, ((wide, second),))]
     wide_part = (input_part, ((wide, "fz"), (wide, "fz")))
     if rows * group <= 1024:
-        early, late = [early[0], wide_part, early[1]], []
+        early, late = [early[1], wide_part, early[0]], []
     else:
         late = [wide_part]
     grad_mixed, out_rows, *owned = back(
@@ -1350,7 +1424,7 @@
         fsdp_size,
     )
     qkv_part = mm_left_t(act_one, grad_mixed).astype(BF16)
-    grad_act_one = mm_right_t(grad_mixed, w_qkv)
+    grad_act_one = mm_right_t(grad_mixed, w_qkv[:, : 3 * model])
     normed_one, inverse_one = normalize(x_wide)
     attn_gain_part = jnp.sum(grad_act_one * normed_one, axis=0)
     grad_x = grad_middle + norm_back(grad_act_one, normed_one, inverse_one, gain_attn)
@@ -1367,8 +1441,11 @@
         seq_size,
         fsdp_size,
     )
-    own_attn, own_down, own_qkv = owned[0], owned[-1], more[-1]
-    own_in = more[0] if len(more) == 2 else owned[1]
+    own_qkv = more[-1]
+    if late[0] is wide_part:
+        (own_attn, own_down), own_in = owned, more[0]
+    else:
+        own_down, own_in, own_attn = owned
     tokens_valid = jnp.sum(seq_lengths).astype(F32)
     root_squares = jnp.sqrt(jnp.sum(totals[:5], axis=1) / (tokens_valid * model))
     own_gains = lax.dynamic_slice_in_dim(totals, (seq_place * fsdp_size + fsdp_place) * shard, shard, 1)

time: 458 us -> 453 us (0.989)
  Pallas kernels: 338 us -> 323 us
  matrix products: 75.8 us -> 80.7 us
    pallas_call x1, Pallas kernels: 124 us -> 117 us  [back(): pl.pallas_call(functools.partial(back_kernel, (seq_size, fsdp_size), grou...]
    dot_general x4, matrix products: 24.4 us -> 30.4 us  [mm_right_t(): lax.dot_general(left, right, (((1,), (1,)), ((), ())), preferred_element_...]
    pallas_call x1, Pallas kernels: 98 us -> 92.5 us  [front(): pl.pallas_call(functools.partial(front_kernel, (seq_size, fsdp_size), gro...]
where the time goes in v2:
time: 453 us; the launch traced here: 448 us
  Pallas kernels  323 us (71%)
  matrix products  80.7 us (18%)
  other arithmetic  25.9 us (6%)
  local copies, waits for them, and re-layouts  15.8 us (3%)
    pallas_call x1, Pallas kernels, back(): pl.pallas_call(functools.partial(back_kernel, (seq_size, fsdp_size), grou...  117 us
    pallas_call x1, Pallas kernels, front(): pl.pallas_call(functools.partial(front_kernel, (seq_size, fsdp_size), gro...  92.5 us
    pallas_call x1, Pallas kernels, scatter_last(): pl.pallas_call(functools.partial(scatter_kernel, (seq_size, fsdp_size), s...  58.3 us
    pallas_call x1, Pallas kernels, gather_first(): pl.pallas_call(functools.partial(first_kernel, (seq_size, fsdp_size), spa...  55.2 us
    dot_general x4, matrix products, mm_right_t(): lax.dot_general(left, right, (((1,), (1,)), ((), ())), preferred_element_...  30.4 us
    dot_general x4, matrix products, mm_left_t(): lax.dot_general(left, right, (((0,), (0,)), ((), ())), preferred_element_...  26.7 us
    dot_general x3, matrix products, mm(): return jnp.dot(left, right, preferred_element_type=F32)  23.6 us
    convert_element_type x1, other arithmetic, shards(): product = (active * gate_half).astype(BF16)  12 us

profile of v2, /device:TPU:27, one launch (start us, length us, event | category | flops | bytes accessed | tf_op | source)
XLA Modules:
  0.0 447.5 jit_solution(4860628727299370812)
XLA Ops:
  0.7 0.1 broadcast_multiply_fusion
  0.8 1.9 fusion.34
  2.7 1.3 fusion.39
  4.0 2.0 fusion.44
  6.0 0.7 copy.19
  6.7 0.8 copy.20
  7.5 0.1 pad.11.clone
  7.6 0.7 maximum_maximum_fusion.gains_ref
  8.2 55.2 %gather_first.1 = (bf16[1024,3200]{1,0:T(8,128)(2,1)}, bf16[512,1024]{1,0:T(8,128)(2,1)}) custom-call(bf16[32,3072]{1,0:T(8,128)(2,1)} %weight_ref.1, bf16[32,128]{1,0:T(8,128)(2,1)} %maximum_maximum_fusion.gains_ref, bf16[8,64,1024]{2,1,0:T(8,128)(2,1)} %hidden_ref.1), custom_call_target="tpu_custom_call" | custom-call | tf_op jit(solution)/shard_map/gather_first/pallas_call | solution.py:345
  63.4 1.1 fusion.48
  64.5 0.8 concatenate.21.refs_8_
  65.4 1.6 concatenate.22.refs_9_
  67.0 92.5 %front.1 = (bf16[512,1024]{1,0:T(8,128)(2,1)}, f32[8,1024]{1,0:T(8,128)}, bf16[512,1024]{1,0:T(8,128)(2,1)}, bf16[1024,2048]{1,0:T(8,128)(2,1)}, bf16[512,1024]{...) custom-call(s32[1]{0:T(128)} %bitcast.refs_0_, ...), custom_call_target="tpu_custom_call" | custom-call | tf_op jit(solution)/shard_map/front/pallas_call | solution.py:1027
  159.5 0.2 convert_reduce_fusion
  159.7 4.8 %fusion.46 = (f32[512]{0:T(512)S(1)}, f32[512,1024]{1,0:T(8,128)S(1)}, f32[512]{0:T(512)S(1)}, f32[512,1024]{1,0:T(8,128)}) fusion(bf16[512,1024]{1,0:T(8,128)(2,1)S(1)} %copy-done, f32[512]{0:T(512)S(1)} %broadcast_multiply_fusion.3, bf16[512,1024]{1,0:T(8,128)(2,1)} %get-tuple-element.34.refs_5_, bf16[1024,1024]{1,0:T(8,128)(2,1)} %get-tuple-element.35), kind=kOutput, calls=%fused_computation.103 | convolution fusion | flops 1076886528 | bytes 8394752 | tf_op jit(solution)/shard_map/dot_general | solution.py:1304
  164.5 0.3 multiply_reduce_fusion.2
  164.9 0.8 fusion.49
  165.7 9.0 %fusion.43 = f32[512,5376]{1,0:T(8,128)S(1)} fusion(bf16[1024,5376]{1,0:T(8,128)(2,1)} %get-tuple-element.37, f32[512,1024]{1,0:T(8,128)S(1)} %get-tuple-element.68, f32[1024]{0:T(1024)S(1)} %bitcast.33, f32[512]{0:T(512)S(1)} %add_rsqrt_fusion.1, f32[512]{0:T(512)S(1)} %get-tuple-element.86), kind=kOutput, calls=%fused_computation.101 | convolution fusion | flops 5639241728 | bytes 24125440 | tf_op jit(solution)/shard_map/dot_general | solution.py:1304
  174.7 12.0 %multiply_convert_fusion = (bf16[512,2688]{1,0:T(8,128)(2,1)S(1)}, f32[512,2688]{1,0:T(8,128)S(1)}) fusion(f32[512,5376]{1,0:T(8,128)S(1)} %fusion.43), kind=kLoop, calls=%fused_computation.8 | loop fusion | flops 90832896 | bytes 19267584 | tf_op jit(solution)/shard_map/convert_element_type | solution.py:1380
  186.7 0.7 fusion.38
  187.4 9.8 %add_convert_fusion = (bf16[512,2688]{1,0:T(8,128)(2,1)}, bf16[512,2688]{1,0:T(8,128)(2,1)}) fusion(f32[512,2688]{1,0:T(8,128)S(1)} %get-tuple-element.66, f32[512,5376]{1,0:T(8,128)S(1)} %fusion.43, bf16[1024,2688]{1,0:T(8,128)(2,1)} %get-tuple-element.38, bf16[512,1024]{1,0:T(8,128)(2,1)} %get-tuple-element.33, f32[512]{0:T(512)S(1)} %fusion.38), kind=kOutput, calls=%fused_computation.10 | convolution fusion | flops 2844917760 | bytes 28575744 | tf_op jit(solution)/shard_map/dot_general | solution.py:1304
  197.2 10.3 %fusion.9 = f32[512,1024]{1,0:T(8,128)S(1)} fusion(bf16[1024,5376]{1,0:T(8,128)(2,1)} %get-tuple-element.37, bf16[512,2688]{1,0:T(8,128)(2,1)} %get-tuple-element.70, bf16[512,2688]{1,0:T(8,128)(2,1)} %get-tuple-element.69), kind=kOutput, calls=%fused_computation.31 | convolution fusion | flops 5648154624 | bytes 18612224 | tf_op jit(solution)/shard_map/dot_general | solution.py:1308
  207.6 7.8 %fusion.25 = (f32[1024]{0:T(1024)S(1)}, f32[1024]{0:T(1024)S(1)}, f32[1024]{0:T(1024)S(1)}, f32[512]{0:T(512)S(1)}, f32[512]{0:T(512)S(1)}, /*index=5*/f32[1024]{0:T(1024)S(1)}, bf16[512,1024]{1,0:T(8,128)(2,1)}) fusion(f32[512]{0:T(512)S(1)} %fusion.38, f32[512,1024]{1,0:T(8,128)S(1)} %get-tuple-element.68, f32[512,1024]{1,0:T(8,128)S(1)} %fusion.9, ...), kind=kOutput, calls=%fused_computation.51 | convolution fusion | flops 2829052928 | bytes 13531136 | tf_op jit(solution)/shard_map/dot_general | solution.py:1308
  215.4 0.9 multiply_add_fusion
  216.2 0.3 copy-done.5
  216.6 2.6 convolution_convert_fusion.3.refs_12_
  219.2 11.7 %convolution_convert_fusion.refs_11_ = bf16[1024,5376]{1,0:T(8,128)(2,1)} fusion(bf16[512,2688]{1,0:T(8,128)(2,1)} %get-tuple-element.70, bf16[512,2688]{1,0:T(8,128)(2,1)} %get-tuple-element.69, f32[512,1024]{1,0:T(8,128)S(1)} %get-tuple-element.68, f32[1024]{0:T(1024)S(1)} %bitcast.36, f32[512]{0:T(512)S(1)} %add_rsqrt_fusion.1, f32[512]{0:T(512)S(1)} %get-tuple-element.86), kind=kOutput, calls=%fused_computation | convolution fusion | flops 5655756800 | bytes 18620416 | tf_op jit(solution)/shard_map/dot_general | solution.py:1312
  230.9 7.1 %convolution_convert_fusion.2.refs_10_ = bf16[1024,2688]{1,0:T(8,128)(2,1)} fusion(bf16[512,2688]{1,0:T(8,128)(2,1)} %copy-done.4, bf16[512,1024]{1,0:T(8,128)(2,1)S(1)} %copy-done.8, f32[512]{0:T(512)S(1)} %fusion.38), kind=kOutput, calls=%fused_computation.5 | convolution fusion | flops 2822897664 | bytes 9308160 | tf_op jit(solution)/shard_map/dot_general | solution.py:1312
  238.0 0.0 copy-done.12
  238.0 2.3 convolution_convert_fusion.4.refs_4_
  240.2 117.3 %back.1 = (bf16[512,3072]{1,0:T(8,128)(2,1)}, bf16[8,64,1024]{2,1,0:T(8,128)(2,1)}, f32[32,2688]{1,0:T(8,128)}, f32[32,5376]{1,0:T(8,128)}, f32[32,1024]{1,0:T(8,128)}) custom-call(s32[1]{0:T(128)} %bitcast.refs_0_, bf16[512,1024]{1,0:T(8,128)(2,1)} %get-tuple-element.31.refs_1_, bf16[1024,2048]{1,0:T(8,128)(2,1)} %get-tuple-element.32.refs_2_.refs_3_, ...), custom_call_target="tpu_custom_call" | custom-call | tf_op jit(solution)/shard_map/back/pallas_call | solution.py:1248
  357.5 1.1 fusion.47
  358.7 1.0 pad_maximum_fusion.3
  359.7 10.0 %fusion.20 = (f32[1024]{0:T(1024)S(1)}, f32[512]{0:T(512)S(1)}, f32[512]{0:T(512)S(1)}, f32[1024]{0:T(1024)S(1)}, f32[1024]{0:T(1024)S(1)}, /*index=5*/f32[512,1024]{1,0:T(8,128)}) fusion(bf16[512,1024]{1,0:T(8,128)(2,1)} %get-tuple-element.29.refs_1_, f32[512]{0:T(512)S(1)} %get-tuple-element.85, f32[512]{0:T(512)S(1)} %broadcast_multiply_fusion.3, ...), kind=kOutput, calls=%fused_computation.46 | convolution fusion | flops 3229085696 | bytes 14706688 | tf_op jit(solution)/shard_map/dot_general | solution.py:1308
  369.7 0.7 stack.31.refs_2_
  370.4 3.4 fusion.19.refs_1_
  373.8 0.0 copy-done.13
  373.8 5.4 %convolution_convert_fusion.1.refs_0_ = bf16[1024,3072]{1,0:T(8,128)(2,1)} fusion(bf16[512,1024]{1,0:T(8,128)(2,1)S(1)} %copy-done.13, bf16[512,3072]{1,0:T(8,128)(2,1)S(1)} %copy-done.11), kind=kOutput, calls=%fused_computation.4 | convolution fusion | flops 3224371200 | bytes 10485760 | tf_op jit(solution)/shard_map/dot_general | solution.py:1312
  379.2 58.3 %scatter_last.1 = (bf16[8,64,1024]{2,1,0:T(8,128)(2,1)}, f32[8,1024]{1,0:T(8,128)}, f32[32,3072]{1,0:T(8,128)}) custom-call(bf16[1024,3072]{1,0:T(8,128)(2,1)} %convolution_convert_fusion.1.refs_0_, bf16[512,1024]{1,0:T(8,128)(2,1)} %fusion.19.refs_1_, f32[8,1024]{1,0:T(8,128)} %stack.31.refs_2_), custom_call_target="tpu_custom_call" | custom-call | tf_op jit(solution)/shard_map/scatter_last/pallas_call | solution.py:781
  437.5 0.8 constant_dynamic-slice_fusion
  438.2 0.5 slice_bitcast_fusion.1
  438.8 0.9 slice_reduce_fusion
  440.3 0.5 divide_sqrt_fusion
  440.9 0.8 slice_bitcast_fusion
  441.6 1.0 copy.25
  442.6 2.3 copy.26
  444.9 1.8 copy.27
  446.6 0.7 copy.28
  (37 shorter events, 0.1 us)
Async XLA Ops:
  67.0 92.5 %copy-start = (bf16[512,1024]{1,0:T(8,128)(2,1)S(1)}, bf16[512,1024]{1,0:T(8,128)(2,1)}, u32[]{:S(2)}) copy-start(bf16[512,1024]{1,0:T(8,128)(2,1)} %get-tuple-element.29.refs_1_) | copy-start | bytes 3145732
  186.7 20.8 %copy-start.4 = (bf16[512,2688]{1,0:T(8,128)(2,1)}, bf16[512,2688]{1,0:T(8,128)(2,1)S(1)}, u32[]{:S(2)}) copy-start(bf16[512,2688]{1,0:T(8,128)(2,1)S(1)} %get-tuple-element.65) | copy-start | bytes 8257540
  207.6 7.8 %copy-start.7 = (bf16[512,1024]{1,0:T(8,128)(2,1)S(1)}, bf16[512,1024]{1,0:T(8,128)(2,1)}, u32[]{:S(2)}) copy-start(bf16[512,1024]{1,0:T(8,128)(2,1)} %get-tuple-element.33) | copy-start | bytes 3145732
  215.4 1.2 copy-start.5
  216.6 21.4 %copy-start.2 = (f32[512,1024]{1,0:T(8,128)}, f32[512,1024]{1,0:T(8,128)S(1)}, u32[]{:S(2)}) copy-start(f32[512,1024]{1,0:T(8,128)S(1)} %multiply_add_fusion) | copy-start | bytes 6291460
  219.2 11.7 %copy-start.8 = (bf16[512,1024]{1,0:T(8,128)(2,1)S(1)}, bf16[512,1024]{1,0:T(8,128)(2,1)}, u32[]{:S(2)}) copy-start(bf16[512,1024]{1,0:T(8,128)(2,1)} %get-tuple-element.33) | copy-start | bytes 3145732
  230.9 7.1 %copy-start.12 = (bf16[1024,1024]{1,0:T(8,128)(2,1)S(1)}, bf16[1024,1024]{1,0:T(8,128)(2,1)}, u32[]{:S(2)}) copy-start(bf16[1024,1024]{1,0:T(8,128)(2,1)} %get-tuple-element.35) | copy-start | bytes 6291460
  359.7 10.7 %copy-start.1 = (bf16[512,1024]{1,0:T(8,128)(2,1)S(1)}, bf16[512,1024]{1,0:T(8,128)(2,1)}, u32[]{:S(2)}) copy-start(bf16[512,1024]{1,0:T(8,128)(2,1)} %get-tuple-element.29.refs_1_) | copy-start | bytes 3145732
  359.7 10.7 %copy-start.3 = (f32[512,1024]{1,0:T(8,128)S(1)}, f32[512,1024]{1,0:T(8,128)}, u32[]{:S(2)}) copy-start(f32[512,1024]{1,0:T(8,128)} %copy-done.2) | copy-start | bytes 6291460
  370.3 3.5 copy-start.11
  370.3 3.5 copy-start.13
  379.2 61.7 %copy-start.9 = (f32[32,2688]{1,0:T(8,128)S(1)}, f32[32,2688]{1,0:T(8,128)}, u32[]{:S(2)}) copy-start(f32[32,2688]{1,0:T(8,128)} %get-tuple-element.47) | copy-start | bytes 1032196
  379.2 62.4 %copy-start.6 = (bf16[8,64,1024]{2,1,0:T(8,128)(2,1)S(1)}, bf16[8,64,1024]{2,1,0:T(8,128)(2,1)}, u32[]{:S(2)}) copy-start(bf16[8,64,1024]{2,1,0:T(8,128)(2,1)} %get-tuple-element.96) | copy-start | bytes 3145732
  379.2 67.4 %copy-start.10 = (f32[32,1024]{1,0:T(8,128)S(1)}, f32[32,1024]{1,0:T(8,128)}, u32[]{:S(2)}) copy-start(f32[32,1024]{1,0:T(8,128)} %get-tuple-element.99) | copy-start | bytes 393220

commit v3 on v2

--- a/solution.py
+++ b/solution.py
@@ -1296,10 +1296,6 @@
     return jnp.cos(angles), jnp.sin(angles)
 
 
-def gelu_exact(values):
-    return jax.nn.gelu(values, approximate=False)
-
-
 def mm(left, right):
     return jnp.dot(left, right, preferred_element_type=F32)
 
@@ -1310,6 +1306,141 @@
 
 def mm_left_t(left, right):
     return lax.dot_general(left, right, (((0,), (0,)), ((), ())), preferred_element_type=F32)
+
+
+SQRT_HALF = 0.7071067811865476
+INV_SQRT_TAU = 0.3989422804014327
+
+
+def gelu_and_slope(values):
+    share = 0.5 + 0.5 * lax.erf(values * SQRT_HALF)
+    density = INV_SQRT_TAU * jnp.exp(-0.5 * values * values)
+    return values * share, share + values * density
+
+
+def mlp_kernel(
+    bounds_ref,
+    x_ref,
+    heads_ref,
+    dy_ref,
+    w_attn_ref,
+    gain_ref,
+    w_in_ref,
+    w_gate_ref,
+    w_down_ref,
+    result_ref,
+    vectors_ref,
+    grad_middle_ref,
+    grad_heads_ref,
+    attn_part_ref,
+    in_part_ref,
+    gate_part_ref,
+    down_part_ref,
+    act,
+    act_turned,
+    grad_branch,
+    grad_turned,
+    middle,
+    branch,
+    grad_act,
+):
+    step = pl.program_id(0)
+    rows = x_ref.shape[0]
+    gain = gain_ref[...]
+    position = bounds_ref[1] + lax.broadcasted_iota(jnp.int32, (rows, 1), 0)
+    valid = jnp.where(position < bounds_ref[0], 1.0, 0.0).astype(F32)
+
+    def squares(row, values):
+        vectors_ref[row : row + 1, :] = jnp.sum(valid * values * values, axis=0, keepdims=True)
+
+    @pl.when(step == 0)
+    def _():
+        x_wide = x_ref[...].astype(F32)
+        attn = mm(heads_ref[...], w_attn_ref[...])
+        total = x_wide + attn
+        middle[...] = total
+        vectors_ref[...] = jnp.zeros_like(vectors_ref)
+        squares(0, x_wide)
+        squares(1, total)
+        squares(3, attn)
+        scaled = normalize(total)[0] * gain
+        act[...] = scaled.astype(BF16)
+        act_turned[...] = scaled.T.astype(BF16)
+        grad_y = dy_ref[...].astype(F32) * valid
+        grad_branch[...] = grad_y.astype(BF16)
+        grad_turned[...] = grad_y.T.astype(BF16)
+        branch[...] = jnp.zeros_like(branch)
+        grad_act[...] = jnp.zeros_like(grad_act)
+
+    input_half = mm(act[...], w_in_ref[...])
+    gate_half = mm(act[...], w_gate_ref[...])
+    grad_product = mm(grad_branch[...], w_down_ref[...])
+    active, slope = gelu_and_slope(input_half)
+    product = (active * gate_half).astype(BF16)
+    grad_input = (grad_product * gate_half * slope).astype(BF16)
+    grad_gate = (grad_product * active).astype(BF16)
+    branch[...] += mm_right_t(product, w_down_ref[...])
+    grad_act[...] += mm_right_t(grad_input, w_in_ref[...]) + mm_right_t(grad_gate, w_gate_ref[...])
+    in_part_ref[...] = mm(act_turned[...], grad_input).astype(BF16)
+    gate_part_ref[...] = mm(act_turned[...], grad_gate).astype(BF16)
+    down_part_ref[...] = mm(grad_turned[...], product).astype(BF16)
+
+    @pl.when(step == pl.num_programs(0) - 1)
+    def _():
+        result = (middle[...] + branch[...]) * valid
+        squares(2, result)
+        squares(4, branch[...])
+        result_ref[...] = result.astype(BF16)
+        normed, inverse = normalize(middle[...])
+        vectors_ref[6:7, :] = jnp.sum(grad_act[...] * normed, axis=0, keepdims=True)
+        grad_y = dy_ref[...].astype(F32) * valid
+        grad_middle = grad_y + norm_back(grad_act[...], normed, inverse, gain)
+        grad_middle_ref[...] = grad_middle
+        grad_attn = grad_middle.astype(BF16)
+        grad_heads_ref[...] = mm_right_t(grad_attn, w_attn_ref[...]).astype(BF16)
+        attn_part_ref[...] = mm_left_t(heads_ref[...], grad_attn).astype(BF16)
+
+
+MLP_TILE = 896
+
+
+def mlp(bounds, x_rows, heads_out, dy_rows, w_attn, gain, w_input, w_down):
+    rows, model = x_rows.shape
+    wide = w_down.shape[1]
+    tile = MLP_TILE if wide % MLP_TILE == 0 else LANES
+    steps = wide // tile
+    vmem = pl.BlockSpec(memory_space=pltpu.VMEM)
+    by_column = pl.BlockSpec((model, tile), lambda i: (0, i))
+    part = jax.ShapeDtypeStruct((model, wide), BF16)
+    return pl.pallas_call(
+        mlp_kernel,
+        grid=(steps,),
+        out_shape=(
+            jax.ShapeDtypeStruct((rows, model), BF16),
+            jax.ShapeDtypeStruct((8, model), F32),
+            jax.ShapeDtypeStruct((rows, model), F32),
+            jax.ShapeDtypeStruct((rows, model), BF16),
+            jax.ShapeDtypeStruct((model, model), BF16),
+            part,
+            part,
+            part,
+        ),
+        in_specs=[pl.BlockSpec(memory_space=pltpu.SMEM)]
+        + [vmem] * 5
+        + [by_column, pl.BlockSpec((model, tile), lambda i: (0, steps + i)), by_column],
+        out_specs=[vmem] * 5 + [by_column] * 3,
+        scratch_shapes=[
+            pltpu.VMEM((rows, model), BF16),
+            pltpu.VMEM((model, rows), BF16),
+            pltpu.VMEM((rows, model), BF16),
+            pltpu.VMEM((model, rows), BF16),
+            pltpu.VMEM((rows, model), F32),
+            pltpu.VMEM((rows, model), F32),
+            pltpu.VMEM((rows, model), F32),
+        ],
+        compiler_params=pltpu.CompilerParams(vmem_limit_bytes=63_000_000),
+        name="mlp",
+    )(bounds, x_rows, heads_out, dy_rows, w_attn, gain, w_input, w_input, w_down)
 
 
 def shards(
@@ -1348,7 +1479,6 @@
     length = jnp.sum(jnp.where(jnp.arange(seq_lengths.shape[0]) == order, seq_lengths, 0))
     lengths = length.astype(jnp.int32)[None]
     places = (seq_place % group) * rows + jnp.arange(rows, dtype=jnp.int32)
-    valid = (places < length).astype(F32)[:, None]
     cosine, sine = rotary_tables(places, head_size)
 
     tile = 512 if rows % 512 == 0 and rows * group <= 1024 else 128
@@ -1368,44 +1498,19 @@
     )
     gain_attn, gain_mlp = gain_rows[0:1], gain_rows[1:2]
 
-    x_wide = x_rows.astype(F32)
-    attn = mm(heads_out, w_attn)
-    middle = x_wide + attn
-    normed_two, inverse_two = normalize(middle)
-    act_two = (normed_two * gain_mlp).astype(BF16)
-    joined = mm(act_two, w_input)
-    input_half = joined[:, :wide]
-    gate_half = joined[:, wide:]
-    active, active_pull = jax.vjp(gelu_exact, input_half)
-    product = (active * gate_half).astype(BF16)
-    branch = mm_right_t(product, w_down)
-    result = (middle + branch) * valid
-    squares = [
-        jnp.sum(valid * tensor * tensor, axis=0) for tensor in (x_wide, middle, result, attn, branch)
-    ]
-
-    grad_y = dy_rows.astype(F32) * valid
-    grad_branch = grad_y.astype(BF16)
-    down_part = mm_left_t(grad_branch, product).astype(BF16)
-    grad_product = mm(grad_branch, w_down)
-    grad_joined = jnp.concatenate(
-        [active_pull(grad_product * gate_half)[0], grad_product * active], axis=1
-    ).astype(BF16)
-    input_part = mm_left_t(act_two, grad_joined).astype(BF16)
-    grad_act_two = mm_right_t(grad_joined, w_input)
-    mlp_gain_part = jnp.sum(grad_act_two * normed_two, axis=0)
-    grad_middle = grad_y + norm_back(grad_act_two, normed_two, inverse_two, gain_mlp)
-    grad_attn = grad_middle.astype(BF16)
-    attn_part = mm_left_t(heads_out, grad_attn).astype(BF16)
-    grad_heads = mm_right_t(grad_attn, w_attn).astype(BF16)
+    bounds = jnp.stack([lengths[0], places[0]])
+    result, vectors, grad_middle, grad_heads, attn_part, in_part, gate_part, down_part = mlp(
+        bounds, x_rows, heads_out, dy_rows, w_attn, gain_mlp, w_input, w_down
+    )
 
     second = "zf" if seq_size == 4 * LINE else "fz"
     early = [(attn_part, ((model, second),)), (down_part, ((wide, second),))]
-    wide_part = (input_part, ((wide, "fz"), (wide, "fz")))
-    if rows * group <= 1024:
-        early, late = [early[1], wide_part, early[0]], []
+    wide_parts = [(in_part, ((wide, "fz"),)), (gate_part, ((wide, "fz"),))]
+    fits = rows * group <= 1024
+    if fits:
+        early, late = [early[1], *wide_parts, early[0]], []
     else:
-        late = [wide_part]
+        late = wide_parts
     grad_mixed, out_rows, *owned = back(
         lengths,
         queries,
@@ -1415,7 +1520,7 @@
         logs,
         cosine,
         sine,
-        result.astype(BF16),
+        result,
         [part for part, _ in early],
         tuple(parts for _, parts in early),
         tile,
@@ -1425,11 +1530,11 @@
     )
     qkv_part = mm_left_t(act_one, grad_mixed).astype(BF16)
     grad_act_one = mm_right_t(grad_mixed, w_qkv[:, : 3 * model])
-    normed_one, inverse_one = normalize(x_wide)
+    normed_one, inverse_one = normalize(x_rows.astype(F32))
     attn_gain_part = jnp.sum(grad_act_one * normed_one, axis=0)
     grad_x = grad_middle + norm_back(grad_act_one, normed_one, inverse_one, gain_attn)
 
-    vectors = jnp.stack(squares + [attn_gain_part, mlp_gain_part, jnp.zeros((model,), F32)])
+    vectors = vectors.at[5].set(attn_gain_part)
     half = 3 * model // 2
     late.append((qkv_part, ((half, "fz"), (half, second))))
     grad_rows, totals, *more = scatter_last(
@@ -1442,10 +1547,11 @@
         fsdp_size,
     )
     own_qkv = more[-1]
-    if late[0] is wide_part:
-        (own_attn, own_down), own_in = owned, more[0]
+    if fits:
+        own_down, own_in, own_gate, own_attn = owned
     else:
-        own_down, own_in, own_attn = owned
+        own_attn, own_down = owned
+        own_in, own_gate = more[:2]
     tokens_valid = jnp.sum(seq_lengths).astype(F32)
     root_squares = jnp.sqrt(jnp.sum(totals[:5], axis=1) / (tokens_valid * model))
     own_gains = lax.dynamic_slice_in_dim(totals, (seq_place * fsdp_size + fsdp_place) * shard, shard, 1)
@@ -1454,7 +1560,7 @@
         grad_rows,
         own_qkv,
         own_attn,
-        jnp.concatenate([own_in[:, :ff], own_in[:, wide : wide + ff]], axis=1),
+        jnp.concatenate([own_in[:, :ff], own_gate[:, :ff]], axis=1),
         own_down[:, :ff].T,
         own_gains[5],
         own_gains[6],

time: 453 us -> 421 us (0.929)
  matrix products: 80.7 us -> 14.3 us
  Pallas kernels: 323 us -> 370 us
  other arithmetic: 25.9 us -> 16.7 us
    pallas_call x0 -> x1, Pallas kernels: none -> 47.5 us  [mlp(): pl.pallas_call(mlp_kernel, grid=(steps,), out_shape=(jax.ShapeDtypeStruct...]
    dot_general x3 -> x0, matrix products: 23.6 us -> none  [mm(): return jnp.dot(left, right, preferred_element_type=F32)]
    dot_general x4 -> x1, matrix products: 30.4 us -> 8.93 us  [mm_right_t(): lax.dot_general(left, right, (((1,), (1,)), ((), ())), preferred_element_...]
    dot_general x4 -> x1, matrix products: 26.7 us -> 5.41 us  [mm_left_t(): lax.dot_general(left, right, (((0,), (0,)), ((), ())), preferred_element_...]
    convert_element_type x3 -> x0, other arithmetic: 12.7 us -> none  [the longest x1 12 us: shards(): product = (active * gate_half).astype(BF16)]
where the time goes in v3:
time: 421 us; the launch traced here: 415 us
  Pallas kernels  370 us (88%)
  other arithmetic  16.7 us (4%)
  matrix products  14.3 us (3%)
  local copies, waits for them, and re-layouts  12 us (3%)
    pallas_call x1, Pallas kernels, back(): pl.pallas_call(functools.partial(back_kernel, (seq_size, fsdp_size), grou...  117 us
    pallas_call x1, Pallas kernels, front(): pl.pallas_call(functools.partial(front_kernel, (seq_size, fsdp_size), gro...  92.4 us
    pallas_call x1, Pallas kernels, scatter_last(): pl.pallas_call(functools.partial(scatter_kernel, (seq_size, fsdp_size), s...  58.3 us
    pallas_call x1, Pallas kernels, gather_first(): pl.pallas_call(functools.partial(first_kernel, (seq_size, fsdp_size), spa...  55.2 us
    pallas_call x1, Pallas kernels, mlp(): pl.pallas_call(mlp_kernel, grid=(steps,), out_shape=(jax.ShapeDtypeStruct...  47.5 us
    dot_general x1, matrix products, mm_right_t(): lax.dot_general(left, right, (((1,), (1,)), ((), ())), preferred_element_...  8.93 us

profile of v3, /device:TPU:27, one launch (start us, length us, event | category | flops | bytes accessed | tf_op | source)
XLA Modules:
  0.0 415.0 jit_solution(69493399227186588)
XLA Ops:
  0.6 0.0 copy-start.5
  0.7 0.0 copy-start.7
  0.7 0.1 broadcast_multiply_fusion
  0.8 1.9 fusion.14
  2.7 1.3 fusion.17
  4.0 1.9 fusion.19
  5.9 0.7 copy.19
  6.7 0.8 copy.20
  7.4 0.1 pad.13.clone
  7.5 0.7 maximum_maximum_fusion.gains_ref
  8.2 55.2 %gather_first.1 = (bf16[1024,3200]{1,0:T(8,128)(2,1)}, bf16[512,1024]{1,0:T(8,128)(2,1)}) custom-call(bf16[32,3072]{1,0:T(8,128)(2,1)} %weight_ref.1, bf16[32,128]{1,0:T(8,128)(2,1)} %maximum_maximum_fusion.gains_ref, bf16[8,64,1024]{2,1,0:T(8,128)(2,1)} %hidden_ref.1), custom_call_target="tpu_custom_call" | custom-call | tf_op jit(solution)/shard_map/gather_first/pallas_call | solution.py:345
  63.4 0.0 copy-done.5
  63.4 0.1 fusion.20
  63.5 0.8 concatenate.19.refs_8_
  64.3 0.0 copy-done.7
  64.3 0.7 concatenate.20.refs_9_
  65.0 92.4 %front.1 = (bf16[512,1024]{1,0:T(8,128)(2,1)}, f32[8,1024]{1,0:T(8,128)}, bf16[512,1024]{1,0:T(8,128)(2,1)}, bf16[1024,2048]{1,0:T(8,128)(2,1)}, bf16[512,1024]{...) custom-call(s32[1]{0:T(128)} %bitcast.refs_0_, ...), custom_call_target="tpu_custom_call" | custom-call | tf_op jit(solution)/shard_map/front/pallas_call | solution.py:1027
  157.4 1.4 fusion.21
  158.9 0.5 slice.53
  159.4 1.9 pad_add_fusion.bounds_ref
  161.2 47.5 %mlp.1 = (bf16[512,1024]{1,0:T(8,128)(2,1)}, f32[8,1024]{1,0:T(8,128)}, f32[512,1024]{1,0:T(8,128)}, bf16[512,1024]{1,0:T(8,128)(2,1)}, bf16[1024,1024]{1,0:T(8,...) custom-call(s32[2]{0:T(128)} %pad_add_fusion.bounds_ref, ...), custom_call_target="tpu_custom_call" | custom-call | tf_op jit(solution)/shard_map/mlp/pallas_call | solution.py:1415
  208.8 117.0 %back.1 = (bf16[512,3072]{1,0:T(8,128)(2,1)}, bf16[8,64,1024]{2,1,0:T(8,128)(2,1)}, f32[32,2688]{1,0:T(8,128)}, f32[32,2688]{1,0:T(8,128)}, f32[32,2688]{1,0:T(8,128)}, /*index=5*/f32[32,1024]{1,0:T(8,128)}) custom-call(s32[1]{0:T(128)} %bitcast.refs_0_, bf16[512,1024]{1,0:T(8,128)(2,1)} %get-tuple-element.52.refs_1_, ...), custom_call_target="tpu_custom_call" | custom-call | tf_op jit(solution)/shard_map/back/pallas_call | solution.py:1248
  325.8 0.0 copy-start
  325.8 2.2 pad_maximum_fusion
  327.9 1.4 convert_reduce_fusion
  329.4 0.0 copy-done
  329.4 0.4 fusion.13
  329.8 8.9 %fusion.12 = (f32[1024]{0:T(1024)S(1)}, f32[512]{0:T(512)S(1)}, f32[512]{0:T(512)S(1)}, f32[512,1024]{1,0:T(8,128)}) fusion(bf16[512,1024]{1,0:T(8,128)(2,1)S(1)} %copy-done, f32[512]{0:T(512)S(1)} %add_rsqrt_fusion, f32[512]{0:T(512)S(1)} %broadcast_multiply_fusion.3, f32[1024]{0:T(1024)S(1)} %bitcast.20, bf16[512,3072]{1,0:T(8,128)(2,1)} %get-tuple-element.69, ...), kind=kOutput, calls=%fused_computation.15 | convolution fusion | flops 3225942016 | bytes 12599296 | tf_op jit(solution)/shard_map/dot_general | solution.py:1304
  338.7 1.4 scatter.4.refs_2_
  340.1 0.0 copy-done.1
  340.1 0.0 copy-start.9
  340.2 0.0 copy-start.10
  340.2 3.4 fusion.11.refs_1_
  343.6 0.0 copy-done.9
  343.6 0.0 copy-done.10
  343.6 5.4 %convolution_convert_fusion.refs_0_ = bf16[1024,3072]{1,0:T(8,128)(2,1)} fusion(bf16[512,1024]{1,0:T(8,128)(2,1)S(1)} %copy-done.10, bf16[512,3072]{1,0:T(8,128)(2,1)S(1)} %copy-done.9), kind=kOutput, calls=%fused_computation.2 | convolution fusion | flops 3224371200 | bytes 10485760 | tf_op jit(solution)/shard_map/dot_general | solution.py:1308
  349.0 58.3 %scatter_last.1 = (bf16[8,64,1024]{2,1,0:T(8,128)(2,1)}, f32[8,1024]{1,0:T(8,128)}, f32[32,3072]{1,0:T(8,128)}) custom-call(bf16[1024,3072]{1,0:T(8,128)(2,1)} %convolution_convert_fusion.refs_0_, bf16[512,1024]{1,0:T(8,128)(2,1)} %fusion.11.refs_1_, f32[8,1024]{1,0:T(8,128)} %scatter.4.refs_2_), custom_call_target="tpu_custom_call" | custom-call | tf_op jit(solution)/shard_map/scatter_last/pallas_call | solution.py:781
  407.3 0.0 copy-start.3
  407.3 0.8 constant_dynamic-slice_fusion
  408.2 0.5 slice_bitcast_fusion.1
  408.7 0.9 slice_reduce_fusion
  410.1 0.5 divide_sqrt_fusion
  410.7 0.8 slice_bitcast_fusion
  411.4 0.0 copy-done.2
  411.4 1.0 copy.26
  412.4 1.0 copy.27
  413.4 0.7 copy.28
  414.1 0.7 copy.29
  (17 shorter events, 0.1 us)
Async XLA Ops:
  0.6 62.7 %copy-start.5 = (bf16[32,5248]{1,0:T(8,128)(2,1)S(1)}, bf16[32,5248]{1,0:T(8,128)(2,1)}, u32[]{:S(2)}) copy-start(bf16[32,5248]{1,0:T(8,128)(2,1)} %param.16) | copy-start | bytes 1007620
  0.7 63.7 %copy-start.7 = (bf16[2624,32]{0,1:T(8,128)(2,1)S(1)}, bf16[2624,32]{0,1:T(8,128)(2,1)}, u32[]{:S(2)}) copy-start(bf16[2624,32]{0,1:T(8,128)(2,1)} %param.17) | copy-start | bytes 503812
  325.8 3.6 copy-start
  329.8 10.3 %copy-start.1 = (f32[512,1024]{1,0:T(8,128)S(1)}, f32[512,1024]{1,0:T(8,128)}, u32[]{:S(2)}) copy-start(f32[512,1024]{1,0:T(8,128)} %get-tuple-element.70) | copy-start | bytes 6291460
  340.1 3.5 copy-start.9
  340.2 3.5 copy-start.10
  349.0 61.6 %copy-start.6 = (f32[32,2688]{1,0:T(8,128)S(1)}, f32[32,2688]{1,0:T(8,128)}, u32[]{:S(2)}) copy-start(f32[32,2688]{1,0:T(8,128)} %get-tuple-element.77) | copy-start | bytes 1032196
  349.0 62.4 %copy-start.2 = (bf16[8,64,1024]{2,1,0:T(8,128)(2,1)S(1)}, bf16[8,64,1024]{2,1,0:T(8,128)(2,1)}, u32[]{:S(2)}) copy-start(bf16[8,64,1024]{2,1,0:T(8,128)(2,1)} %get-tuple-element.104) | copy-start | bytes 3145732
  407.3 5.1 %copy-start.3 = (bf16[8,64,1024]{2,1,0:T(8,128)(2,1)S(1)}, bf16[8,64,1024]{2,1,0:T(8,128)(2,1)}, u32[]{:S(2)}) copy-start(bf16[8,64,1024]{2,1,0:T(8,128)(2,1)} %get-tuple-element.105) | copy-start | bytes 3145732
  411.4 1.9 copy-start.4
  411.4 2.7 copy-start.8

commit v4 on v3

--- a/solution.py
+++ b/solution.py
@@ -444,7 +444,8 @@
         at = self.at
         z, f, g = self.where_is(dz, df, dg)
         place, other = at.index(z, f, g), 1 - at.core
-        pf, pg = at.split(*at.split(f, g, at.core), other)
+        pf, pg = at.split(*at.split(at.f, at.g, at.core), other)
+        pf, pg = (pf + df) % at.nf, (pg + dg) % at.ng
         there = at.index(z, pf, pg)
 
         def body():
@@ -607,10 +608,10 @@
 
 
 def pipelined(scatters):
-    begins, first, mids, lasts = [], [], [], []
+    first, mids, lasts, starts = [], [], [], {}
     for scatter in scatters:
-        starts, pairs, seconds, thirds = scatter.stages()
-        begins += starts
+        begins, pairs, seconds, thirds = scatter.stages()
+        starts.update(zip(pairs, begins))
         first += [step for step in pairs if step.args[2]]
         mid = []
         for second in seconds:
@@ -623,7 +624,17 @@
         if slot < len(scatters):
             some = mixed(some, mids[slot]) if some else mids[slot]
         events += some
-    return begins, events, len(first)
+    begins = [starts[event] for event in events if event in starts]
+    later = iter(begins[AHEAD:])
+
+    def with_begin(event):
+        begin = next(later, None) if event in starts else None
+        return event if begin is None else functools.partial(run_all, [event, begin])
+
+    return begins[:AHEAD], [with_begin(event) for event in events], len(first)
+
+
+AHEAD = 64
 
 
 def lagged(events, lag, phase):
@@ -1104,16 +1115,19 @@
     sections = sum(len(parts) for parts in spans)
     count = len(spans)
     length_ref, q_ref, k_ref, v_ref, g_ref, o_ref, log_ref, cos_ref, sin_ref, result_ref = refs[:10]
-    sources, refs = refs[10 : 10 + count], refs[10 + count :]
-    mixed_ref, out_ref = refs[:2]
-    owned, refs = refs[2 : 2 + count], refs[2 + count :]
+    act_ref, x_ref, middle_ref, gain_ref, vectors_ref, w_ref = refs[10:16]
+    sources, refs = refs[16 : 16 + count], refs[16 + count :]
+    out_ref, part_ref, grad_x_ref, sums_ref = refs[:4]
+    owned, refs = refs[4 : 4 + count], refs[4 + count :]
     scratches, refs = split_scratch(refs, sections)
-    dk_acc, dv_acc, parts_ref, arrived, sum_send, sum_recv, trade_send, trade_recv = refs
+    dk_acc, dv_acc, parts_ref, arrived, sum_send, sum_recv, trade_send, trade_recv = refs[:8]
+    mixed_ref, act_turned, grad_act = refs[8:]
     step = pl.program_id(0)
     tile = q_ref.shape[0]
     rows, model = result_ref.shape
     tiles, pairs = rows // tile, model // LANES
-    steps = pairs * tiles + 1
+    attending = pairs * tiles
+    steps = attending + 1 + 3 * model // FRONT_TILE
     slots = out_ref.shape[0]
     phase = Phase()
     scatters, places = scatter_sections(at, sources, spans, scratches, phase)
@@ -1154,9 +1168,10 @@
         if some:
             pl.when(step == number)(functools.partial(run_all, some))
 
-    pl.when(both(step > 0, step % tiles == 0))(lambda: share(step // tiles - 1))
-
-    @pl.when(step < steps - 1)
+    shared_now = jnp.logical_and(both(step > 0, step <= attending), step % tiles == 0)
+    pl.when(shared_now)(lambda: share(step // tiles - 1))
+
+    @pl.when(step < attending)
     def _():
         pair, piece = step // tiles, step % tiles
         own = pl.ds(pl.multiple_of(piece * tile, tile), tile)
@@ -1202,9 +1217,26 @@
 
         lax.fori_loop(0, pairs, body, 0)
 
+    @pl.when(step == attending)
+    def _():
+        add_parts()
+        act_turned[...] = act_ref[...].astype(F32).T.astype(BF16)
+        grad_act[...] = jnp.zeros_like(grad_act)
+
+    @pl.when(step > attending)
+    def _():
+        start = pl.multiple_of((step - attending - 1) * FRONT_TILE, FRONT_TILE)
+        grad_mixed = mixed_ref[:, pl.ds(start, FRONT_TILE)]
+        grad_act[...] += mm_right_t(grad_mixed, w_ref[...])
+        part_ref[...] = mm(act_turned[...], grad_mixed).astype(BF16)
+
     @pl.when(step == steps - 1)
     def _():
-        add_parts()
+        normed, inverse = normalize(x_ref[...].astype(F32))
+        sums_ref[...] = vectors_ref[...]
+        sums_ref[5:6, :] = jnp.sum(grad_act[...] * normed, axis=0, keepdims=True)
+        grad_x = middle_ref[...] + norm_back(grad_act[...], normed, inverse, gain_ref[0:1, :])
+        grad_x_ref[...] = grad_x.astype(BF16)
         run_all(events[ahead + (steps - 1) * BACK_PACE :])
         for scatter, (number, start) in zip(scatters, places):
             scatter.store(owned[number], start)
@@ -1224,13 +1256,35 @@
 BACK_PACE = 3
 
 
-def back(length, queries, shared, grads, heads_out, logs, cosine, sine, result, sources, spans, tile, slots, seq_size, fsdp_size):
+def back(
+    length,
+    queries,
+    shared,
+    grads,
+    heads_out,
+    logs,
+    cosine,
+    sine,
+    result,
+    act,
+    x_rows,
+    grad_middle,
+    gain,
+    vectors,
+    weight,
+    sources,
+    spans,
+    tile,
+    slots,
+    seq_size,
+    fsdp_size,
+):
     rows, keys, model = queries.shape[0], shared.shape[0], queries.shape[1]
     group, positions = keys // rows, rows // slots
     pairs, tiles = model // LANES, rows // tile
     nf, ng = seq_size // (2 * LINE), fsdp_size
     devices = seq_size * fsdp_size
-    shard = sources[0].shape[0] // devices
+    shard = model // devices
     vmem, anywhere = pl.BlockSpec(memory_space=pltpu.VMEM), pl.BlockSpec(memory_space=pl.ANY)
     dma = pltpu.SemaphoreType.DMA
 
@@ -1241,17 +1295,23 @@
         return jnp.minimum(i, pairs * tiles - 1) % tiles
 
     by_row = pl.BlockSpec((tile, LANES), lambda i: (tile_of(i), pair_of(i)))
+    last = 3 * model // FRONT_TILE - 1
+    by_column = pl.BlockSpec(
+        (model, FRONT_TILE), lambda i: (0, jnp.clip(i - pairs * tiles - 1, 0, last))
+    )
     scratch = []
     for parts in spans:
         for size, order in parts:
             scratch += Scatter.scratch(order, shard, size, nf, ng)
     return pl.pallas_call(
         functools.partial(back_kernel, (seq_size, fsdp_size), group, spans),
-        grid=(pairs * tiles + 1,),
+        grid=(pairs * tiles + 2 + last,),
         out_shape=tuple(
             [
-                jax.ShapeDtypeStruct((rows, 3 * model), BF16),
                 jax.ShapeDtypeStruct((slots, positions, model), BF16),
+                jax.ShapeDtypeStruct((model, 3 * model), BF16),
+                jax.ShapeDtypeStruct((rows, model), BF16),
+                jax.ShapeDtypeStruct(vectors.shape, F32),
             ]
             + [jax.ShapeDtypeStruct((shard, source.shape[1]), F32) for source in sources]
         ),
@@ -1267,8 +1327,10 @@
             vmem,
             vmem,
         ]
+        + [vmem] * 5
+        + [by_column]
         + [anywhere] * len(sources),
-        out_specs=[vmem, anywhere] + [vmem] * len(sources),
+        out_specs=[anywhere, by_column, vmem, vmem] + [vmem] * len(sources),
         scratch_shapes=scratch
         + [
             pltpu.VMEM((keys, LANES), F32),
@@ -1279,12 +1341,33 @@
             dma((2, group - 1, pairs)),
             dma((slots,)),
             dma((slots,)),
+            pltpu.VMEM((rows, 3 * model), BF16),
+            pltpu.VMEM((model, rows), BF16),
+            pltpu.VMEM((rows, model), F32),
         ],
         compiler_params=pltpu.CompilerParams(
             collective_id=2, has_side_effects=True, vmem_limit_bytes=67_000_000
         ),
         name="back",
-    )(length, queries, shared, shared, grads, heads_out, logs, cosine, sine, result, *sources)
+    )(
+        length,
+        queries,
+        shared,
+        shared,
+        grads,
+        heads_out,
+        logs,
+        cosine,
+        sine,
+        result,
+        act,
+        x_rows,
+        grad_middle,
+        gain,
+        vectors,
+        weight,
+        *sources,
+    )
 
 
 def rotary_tables(places, head_size):
@@ -1346,7 +1429,7 @@
 ):
     step = pl.program_id(0)
     rows = x_ref.shape[0]
-    gain = gain_ref[...]
+    gain = gain_ref[1:2, :]
     position = bounds_ref[1] + lax.broadcasted_iota(jnp.int32, (rows, 1), 0)
     valid = jnp.where(position < bounds_ref[0], 1.0, 0.0).astype(F32)
 
@@ -1477,13 +1560,14 @@
     slot = fsdp_place * slots + seq_place // group
     order = jnp.sum(jnp.where(jnp.arange(slot_order.shape[0]) == slot, slot_order, 0))
     length = jnp.sum(jnp.where(jnp.arange(seq_lengths.shape[0]) == order, seq_lengths, 0))
-    lengths = length.astype(jnp.int32)[None]
-    places = (seq_place % group) * rows + jnp.arange(rows, dtype=jnp.int32)
+    base = (seq_place % group) * rows
+    bounds = jnp.stack([length.astype(jnp.int32), base.astype(jnp.int32)])
+    places = base + jnp.arange(rows, dtype=jnp.int32)
     cosine, sine = rotary_tables(places, head_size)
 
     tile = 512 if rows % 512 == 0 and rows * group <= 1024 else 128
     act_one, gain_rows, queries, shared, heads_out, logs, dy_rows, w_attn, w_input, w_down = front(
-        lengths,
+        bounds,
         x_rows,
         cosine,
         sine,
@@ -1496,23 +1580,23 @@
         seq_size,
         fsdp_size,
     )
-    gain_attn, gain_mlp = gain_rows[0:1], gain_rows[1:2]
-
-    bounds = jnp.stack([lengths[0], places[0]])
+
     result, vectors, grad_middle, grad_heads, attn_part, in_part, gate_part, down_part = mlp(
-        bounds, x_rows, heads_out, dy_rows, w_attn, gain_mlp, w_input, w_down
+        bounds, x_rows, heads_out, dy_rows, w_attn, gain_rows, w_input, w_down
     )
 
     second = "zf" if seq_size == 4 * LINE else "fz"
-    early = [(attn_part, ((model, second),)), (down_part, ((wide, second),))]
-    wide_parts = [(in_part, ((wide, "fz"),)), (gate_part, ((wide, "fz"),))]
-    fits = rows * group <= 1024
-    if fits:
-        early, late = [early[1], *wide_parts, early[0]], []
-    else:
-        late = wide_parts
-    grad_mixed, out_rows, *owned = back(
-        lengths,
+    early = [
+        (down_part, ((wide, second),)),
+        (in_part, ((wide, "fz"),)),
+        (gate_part, ((wide, "fz"),)),
+        (attn_part, ((model, second),)),
+    ]
+    late = []
+    if rows * group > 1024:
+        early, late = late, early
+    out_rows, qkv_part, grad_x, vectors, *owned = back(
+        bounds,
         queries,
         shared,
         grad_heads,
@@ -1521,6 +1605,12 @@
         cosine,
         sine,
         result,
+        act_one,
+        x_rows,
+        grad_middle,
+        gain_rows,
+        vectors,
+        w_qkv,
         [part for part, _ in early],
         tuple(parts for _, parts in early),
         tile,
@@ -1528,30 +1618,18 @@
         seq_size,
         fsdp_size,
     )
-    qkv_part = mm_left_t(act_one, grad_mixed).astype(BF16)
-    grad_act_one = mm_right_t(grad_mixed, w_qkv[:, : 3 * model])
-    normed_one, inverse_one = normalize(x_rows.astype(F32))
-    attn_gain_part = jnp.sum(grad_act_one * normed_one, axis=0)
-    grad_x = grad_middle + norm_back(grad_act_one, normed_one, inverse_one, gain_attn)
-
-    vectors = vectors.at[5].set(attn_gain_part)
     half = 3 * model // 2
     late.append((qkv_part, ((half, "fz"), (half, second))))
     grad_rows, totals, *more = scatter_last(
         [part for part, _ in late],
         tuple(parts for _, parts in late),
-        grad_x.astype(BF16),
+        grad_x,
         vectors,
         slots,
         seq_size,
         fsdp_size,
     )
-    own_qkv = more[-1]
-    if fits:
-        own_down, own_in, own_gate, own_attn = owned
-    else:
-        own_attn, own_down = owned
-        own_in, own_gate = more[:2]
+    own_down, own_in, own_gate, own_attn, own_qkv = owned + more
     tokens_valid = jnp.sum(seq_lengths).astype(F32)
     root_squares = jnp.sqrt(jnp.sum(totals[:5], axis=1) / (tokens_valid * model))
     own_gains = lax.dynamic_slice_in_dim(totals, (seq_place * fsdp_size + fsdp_place) * shard, shard, 1)

time: 421 us -> 417 us (level)
  matrix products: 14.3 us -> 0 us
  Pallas kernels: 370 us -> 384 us
  other arithmetic: 16.7 us -> 10.6 us
    pallas_call x1, Pallas kernels: 117 us -> 132 us  [back(): pl.pallas_call(functools.partial(back_kernel, (seq_size, fsdp_size), grou...]
    dot_general x2 -> x0, matrix products: 14.3 us -> none  [the longest x1 8.93 us: mm_right_t(): lax.dot_general(left, right, (((1,), (1,)), ((), ())), preferred_element_...]
where the time goes in v4:
time: 417 us; the launch traced here: 410 us
  Pallas kernels  384 us (92%)
  local copies, waits for them, and re-layouts  13.9 us (3%)
  other arithmetic  10.6 us (3%)
    pallas_call x1, Pallas kernels, back(): pl.pallas_call(functools.partial(back_kernel, (seq_size, fsdp_size), grou...  132 us
    pallas_call x1, Pallas kernels, front(): pl.pallas_call(functools.partial(front_kernel, (seq_size, fsdp_size), gro...  91.8 us
    pallas_call x1, Pallas kernels, scatter_last(): pl.pallas_call(functools.partial(scatter_kernel, (seq_size, fsdp_size), s...  58 us
    pallas_call x1, Pallas kernels, gather_first(): pl.pallas_call(functools.partial(first_kernel, (seq_size, fsdp_size), spa...  55.2 us
    pallas_call x1, Pallas kernels, mlp(): pl.pallas_call(mlp_kernel, grid=(steps,), out_shape=(jax.ShapeDtypeStruct...  47.3 us

profile of v4, /device:TPU:27, one launch (start us, length us, event | category | flops | bytes accessed | tf_op | source)
XLA Modules:
  0.0 410.2 jit_solution(6058409355632492245)
XLA Ops:
  0.7 1.3 fusion.2
  2.0 0.1 pad.9.clone
  2.1 1.9 fusion.4
  4.7 1.2 pad_add_fusion.refs_0_.bounds_ref
  5.9 0.7 copy.19
  6.6 0.8 copy.20
  7.4 0.7 maximum_maximum_fusion.gains_ref
  8.1 1.6 concatenate.18.refs_9_
  9.7 0.1 broadcast_multiply_fusion
  9.8 1.9 fusion
  11.7 1.1 fusion.5
  12.8 0.8 concatenate.17.refs_8_
  13.6 55.2 %gather_first.1 = (bf16[1024,3200]{1,0:T(8,128)(2,1)}, bf16[512,1024]{1,0:T(8,128)(2,1)}) custom-call(bf16[32,3072]{1,0:T(8,128)(2,1)} %weight_ref.1, bf16[32,128]{1,0:T(8,128)(2,1)} %maximum_maximum_fusion.gains_ref, bf16[8,64,1024]{2,1,0:T(8,128)(2,1)} %hidden_ref.1), custom_call_target="tpu_custom_call" | custom-call | tf_op jit(solution)/shard_map/gather_first/pallas_call | solution.py:345
  68.8 91.8 %front.1 = (bf16[512,1024]{1,0:T(8,128)(2,1)}, f32[8,1024]{1,0:T(8,128)}, bf16[512,1024]{1,0:T(8,128)(2,1)}, bf16[1024,2048]{1,0:T(8,128)(2,1)}, bf16[512,1024]{...) custom-call(s32[2]{0:T(128)} %pad_add_fusion.refs_0_.bounds_ref, ...), custom_call_target="tpu_custom_call" | custom-call | tf_op jit(solution)/shard_map/front/pallas_call | solution.py:1038
  160.5 47.3 %mlp.1 = (bf16[512,1024]{1,0:T(8,128)(2,1)}, f32[8,1024]{1,0:T(8,128)}, f32[512,1024]{1,0:T(8,128)}, bf16[512,1024]{1,0:T(8,128)(2,1)}, bf16[1024,1024]{1,0:T(8,...) custom-call(s32[2]{0:T(128)} %pad_add_fusion.refs_0_.bounds_ref, ...), custom_call_target="tpu_custom_call" | custom-call | tf_op jit(solution)/shard_map/mlp/pallas_call | solution.py:1498
  207.8 131.9 %back.1 = (bf16[8,64,1024]{2,1,0:T(8,128)(2,1)}, bf16[1024,3072]{1,0:T(8,128)(2,1)}, bf16[512,1024]{1,0:T(8,128)(2,1)}, f32[8,1024]{1,0:T(8,128)}, f32[32,2688]{...) custom-call(s32[2]{0:T(128)} %pad_add_fusion.refs_0_.bounds_ref, ...), custom_call_target="tpu_custom_call" | custom-call | tf_op jit(solution)/shard_map/back/pallas_call | solution.py:1306
  339.7 0.0 copy-start
  339.7 1.8 slice_bitcast_fusion
  341.6 2.1 pad_maximum_fusion
  343.6 0.0 copy-start.1
  343.7 58.0 %scatter_last.1 = (bf16[8,64,1024]{2,1,0:T(8,128)(2,1)}, f32[8,1024]{1,0:T(8,128)}, f32[32,3072]{1,0:T(8,128)}) custom-call(bf16[1024,3072]{1,0:T(8,128)(2,1)} %get-tuple-element.61.refs_0_, bf16[512,1024]{1,0:T(8,128)(2,1)} %get-tuple-element.62.refs_1_, f32[8,1024]{1,0:T(8,128)} %get-tuple-element.63.refs_2_), custom_call_target="tpu_custom_call" | custom-call | tf_op jit(solution)/shard_map/scatter_last/pallas_call | solution.py:792
  401.7 0.9 slice_reduce_fusion
  402.6 0.7 constant_dynamic-slice_fusion
  403.3 0.5 slice_bitcast_fusion.1
  403.8 0.5 divide_sqrt_fusion
  404.4 0.0 copy-done
  404.4 1.0 copy.25
  405.3 2.3 copy.26
  407.6 1.8 copy.27
  409.4 0.0 copy-done.1
  409.4 0.7 copy.28
  (4 shorter events, 0.0 us)
Async XLA Ops:
  339.7 64.6 %copy-start = (bf16[8,64,1024]{2,1,0:T(8,128)(2,1)S(1)}, bf16[8,64,1024]{2,1,0:T(8,128)(2,1)}, u32[]{:S(2)}) copy-start(bf16[8,64,1024]{2,1,0:T(8,128)(2,1)} %get-tuple-element.88) | copy-start | bytes 3145732
  343.6 65.7 %copy-start.1 = (f32[32,1024]{1,0:T(8,128)S(1)}, f32[32,1024]{1,0:T(8,128)}, u32[]{:S(2)}) copy-start(f32[32,1024]{1,0:T(8,128)} %get-tuple-element.91) | copy-start | bytes 393220

commit v5 on v4

--- a/solution.py
+++ b/solution.py
@@ -688,7 +688,7 @@
     send = functools.partial(start_copy, phase)
     scatters, places = scatter_sections(at, sources, spans, scratches, phase)
     begins, events, _ = pipelined(scatters)
-    steps, rest = lagged(events, 24, phase)
+    steps, rest = lagged(events, 64, phase)
     other = 1 - at.core
 
     def vectors_g():
@@ -1132,7 +1132,7 @@
     phase = Phase()
     scatters, places = scatter_sections(at, sources, spans, scratches, phase)
     begins, events, ahead = pipelined(scatters)
-    events, rest = lagged(events, 40, phase)
+    events, rest = lagged(events, 120, phase)
     base, part = (at.seq // group) * group, at.seq % group
     members = [base + (part + other) % group for other in range(1, group)]
 

time: 417 us -> 403 us (0.966)
  Pallas kernels: 384 us -> 371 us
    pallas_call x1, Pallas kernels: 132 us -> 119 us  [back(): pl.pallas_call(functools.partial(back_kernel, (seq_size, fsdp_size), grou...]
where the time goes in v5:
time: 403 us; the launch traced here: 397 us
  Pallas kernels  371 us (92%)
  local copies, waits for them, and re-layouts  13.9 us (3%)
  other arithmetic  10.6 us (3%)
    pallas_call x1, Pallas kernels, back(): pl.pallas_call(functools.partial(back_kernel, (seq_size, fsdp_size), grou...  119 us
    pallas_call x1, Pallas kernels, front(): pl.pallas_call(functools.partial(front_kernel, (seq_size, fsdp_size), gro...  91.8 us
    pallas_call x1, Pallas kernels, scatter_last(): pl.pallas_call(functools.partial(scatter_kernel, (seq_size, fsdp_size), s...  57.6 us
    pallas_call x1, Pallas kernels, gather_first(): pl.pallas_call(functools.partial(first_kernel, (seq_size, fsdp_size), spa...  55.2 us
    pallas_call x1, Pallas kernels, mlp(): pl.pallas_call(mlp_kernel, grid=(steps,), out_shape=(jax.ShapeDtypeStruct...  47.3 us

profile of v5, /device:TPU:27, one launch (start us, length us, event | category | flops | bytes accessed | tf_op | source)
XLA Modules:
  0.0 396.9 jit_solution(9915975489703074421)
XLA Ops:
  0.7 1.3 fusion.2
  2.0 0.1 pad.9.clone
  2.1 1.9 fusion.4
  4.7 1.2 pad_add_fusion.refs_0_.bounds_ref
  5.9 0.7 copy.19
  6.6 0.8 copy.20
  7.4 0.7 maximum_maximum_fusion.gains_ref
  8.1 1.6 concatenate.18.refs_9_
  9.7 0.1 broadcast_multiply_fusion
  9.8 1.9 fusion
  11.7 1.1 fusion.5
  12.8 0.8 concatenate.17.refs_8_
  13.6 55.2 %gather_first.1 = (bf16[1024,3200]{1,0:T(8,128)(2,1)}, bf16[512,1024]{1,0:T(8,128)(2,1)}) custom-call(bf16[32,3072]{1,0:T(8,128)(2,1)} %weight_ref.1, bf16[32,128]{1,0:T(8,128)(2,1)} %maximum_maximum_fusion.gains_ref, bf16[8,64,1024]{2,1,0:T(8,128)(2,1)} %hidden_ref.1), custom_call_target="tpu_custom_call" | custom-call | tf_op jit(solution)/shard_map/gather_first/pallas_call | solution.py:345
  68.8 91.8 %front.1 = (bf16[512,1024]{1,0:T(8,128)(2,1)}, f32[8,1024]{1,0:T(8,128)}, bf16[512,1024]{1,0:T(8,128)(2,1)}, bf16[1024,2048]{1,0:T(8,128)(2,1)}, bf16[512,1024]{...) custom-call(s32[2]{0:T(128)} %pad_add_fusion.refs_0_.bounds_ref, ...), custom_call_target="tpu_custom_call" | custom-call | tf_op jit(solution)/shard_map/front/pallas_call | solution.py:1038
  160.5 47.3 %mlp.1 = (bf16[512,1024]{1,0:T(8,128)(2,1)}, f32[8,1024]{1,0:T(8,128)}, f32[512,1024]{1,0:T(8,128)}, bf16[512,1024]{1,0:T(8,128)(2,1)}, bf16[1024,1024]{1,0:T(8,...) custom-call(s32[2]{0:T(128)} %pad_add_fusion.refs_0_.bounds_ref, ...), custom_call_target="tpu_custom_call" | custom-call | tf_op jit(solution)/shard_map/mlp/pallas_call | solution.py:1498
  207.8 119.0 %back.1 = (bf16[8,64,1024]{2,1,0:T(8,128)(2,1)}, bf16[1024,3072]{1,0:T(8,128)(2,1)}, bf16[512,1024]{1,0:T(8,128)(2,1)}, f32[8,1024]{1,0:T(8,128)}, f32[32,2688]{...) custom-call(s32[2]{0:T(128)} %pad_add_fusion.refs_0_.bounds_ref, ...), custom_call_target="tpu_custom_call" | custom-call | tf_op jit(solution)/shard_map/back/pallas_call | solution.py:1306
  326.8 0.0 copy-start
  326.8 1.8 slice_bitcast_fusion
  328.6 2.1 pad_maximum_fusion
  330.7 0.0 copy-start.1
  330.7 57.6 %scatter_last.1 = (bf16[8,64,1024]{2,1,0:T(8,128)(2,1)}, f32[8,1024]{1,0:T(8,128)}, f32[32,3072]{1,0:T(8,128)}) custom-call(bf16[1024,3072]{1,0:T(8,128)(2,1)} %get-tuple-element.61.refs_0_, bf16[512,1024]{1,0:T(8,128)(2,1)} %get-tuple-element.62.refs_1_, f32[8,1024]{1,0:T(8,128)} %get-tuple-element.63.refs_2_), custom_call_target="tpu_custom_call" | custom-call | tf_op jit(solution)/shard_map/scatter_last/pallas_call | solution.py:792
  388.3 0.9 slice_reduce_fusion
  389.2 0.7 constant_dynamic-slice_fusion
  390.0 0.5 slice_bitcast_fusion.1
  390.5 0.5 divide_sqrt_fusion
  391.0 0.0 copy-done
  391.0 1.0 copy.25
  392.0 2.3 copy.26
  394.2 1.8 copy.27
  396.0 0.0 copy-done.1
  396.0 0.7 copy.28
  (4 shorter events, 0.0 us)
Async XLA Ops:
  326.8 64.2 %copy-start = (bf16[8,64,1024]{2,1,0:T(8,128)(2,1)S(1)}, bf16[8,64,1024]{2,1,0:T(8,128)(2,1)}, u32[]{:S(2)}) copy-start(bf16[8,64,1024]{2,1,0:T(8,128)(2,1)} %get-tuple-element.88) | copy-start | bytes 3145732
  330.7 65.3 %copy-start.1 = (f32[32,1024]{1,0:T(8,128)S(1)}, f32[32,1024]{1,0:T(8,128)}, u32[]{:S(2)}) copy-start(f32[32,1024]{1,0:T(8,128)} %get-tuple-element.91) | copy-start | bytes 393220
